TPU v7x, 512 devices: a whole 4x4x16 slice. The times are simulated.
512 devices in a mesh: ingest: 64 (over z, y), codes: 8 (over x, core).
Axes of the slice: x: 4, y: 4, z: 16, core: 2. Of those that a mesh axis runs over, the one named last changes fastest.
Arguments:
- vectors: bfloat16 [16384, 1024], P('ingest'), may hold values from -6 to 6
- codes: int32 [8, 16384], P(None, 'ingest'), may hold values from 0 to 4095, as said below
- codebook: bfloat16 [8, 4096, 1024], P('codes', 'ingest'), may hold values from -5 to 5
- pairs: int32 [256, 64], replicated, may hold values from 0 to 255, as said below
Outputs:
- new_codebook: float32 [8, 4096, 1024], P('codes', 'ingest')
- gram: float32 [8, 4096, 8192], P('codes', 'ingest')
Inputs may be any that keep to these rules, and one draw needn't show every extreme that they name: In each codebook and each aligned block of 256 vectors (the vectors of one index of ingest), at most 8 codes fall in any one range j * 64 to (j + 1) * 64 - 1; in each codebook one such range holds exactly 8 codes of every block. `pairs`: block s is codes (s % 32) * 128 to (s % 32) * 128 + 127 of codebook s // 32; every entry of row r names a block of a codebook other than that of block r; entries may repeat.
All inputs are finite; a program needn't handle non-finite values.
Results may differ from a plain program's by a relative error of at most 0.015.
Values may be sent and summed in bfloat16 or wider, within the bound.
No kernel may reach another device: no remote copies, remote signals or barrier semaphores. Data moves between devices by JAX's collectives and lax.ppermute only.
A program may use at most 64 MiB of HBM per device.

v0:
```python
import jax
import jax.numpy as jnp
from jax import lax
from jax.sharding import PartitionSpec as P

K = 4096
BLK = 128
P_SIZE = 64
KB = 32


def shards(vectors, codes, codebook, pairs):
    owners = lax.axis_size("ingest")
    my_owner = lax.axis_index("ingest")
    my_group = lax.axis_index("codes")
    rows_count = vectors.shape[0]
    books_dev = codebook.shape[0]
    own_rows = codebook.shape[1]
    feature_dim = codebook.shape[2]
    codebooks = codes.shape[0]
    capacity = 2 * rows_count // owners
    slot_total = owners * books_dev * capacity
    local_codes = lax.dynamic_slice_in_dim(codes, my_group * books_dev, books_dev, 0)
    target = local_codes // own_rows
    within = local_codes - target * own_rows
    owner_hits = (target[:, :, None] == jnp.arange(owners, dtype=jnp.int32)).astype(jnp.int32)
    before = jnp.cumsum(owner_hits, axis=1) - owner_hits
    slot_rank = jnp.sum(before * owner_hits, axis=2)
    book_offset = jnp.arange(books_dev, dtype=jnp.int32)[:, None]
    slot_index = (target * books_dev + book_offset) * capacity + slot_rank
    slot_flat = slot_index.reshape(-1)
    vector_ids = jnp.broadcast_to(
        jnp.arange(rows_count, dtype=jnp.int32), (books_dev, rows_count)
    ).reshape(-1)
    slot_vector = jnp.full((slot_total,), rows_count, jnp.int32).at[slot_flat].set(vector_ids)
    asked_rows = (within + book_offset * own_rows).reshape(-1)
    slot_request = jnp.full((slot_total,), -1, jnp.int32).at[slot_flat].set(asked_rows)
    slot_request = slot_request.reshape(owners, books_dev * capacity)
    flat_book = codebook.reshape(books_dev * own_rows, feature_dim)
    picked = jnp.take(
        flat_book,
        jnp.maximum(
            lax.all_to_all(slot_request, "ingest", split_axis=0, concat_axis=0, tiled=True), 0
        ),
        axis=0,
    )
    returned = lax.all_to_all(picked, "ingest", split_axis=0, concat_axis=0, tiled=True)
    fetched = jnp.take(returned.reshape(slot_total, feature_dim), slot_index, axis=0)
    partial_sum = jnp.sum(fetched.astype(jnp.float32), axis=0)
    full_sum = lax.psum(partial_sum.astype(jnp.bfloat16), "codes").astype(jnp.float32)
    residual = (vectors.astype(jnp.float32) - full_sum).astype(jnp.bfloat16)
    residual_ext = jnp.concatenate([residual, jnp.zeros((1, feature_dim), jnp.bfloat16)], axis=0)
    codes_ext = jnp.concatenate([codes.T, jnp.full((1, codebooks), -1, jnp.int32)], axis=0)
    send_rows = jnp.take(residual_ext, slot_vector, axis=0).reshape(
        owners, books_dev * capacity, feature_dim
    )
    send_codes = jnp.take(codes_ext, slot_vector, axis=0).reshape(
        owners, books_dev * capacity, codebooks
    )
    got_rows, got_codes = (
        lax.all_to_all(send_rows, "ingest", split_axis=0, concat_axis=0, tiled=True),
        lax.all_to_all(send_codes, "ingest", split_axis=0, concat_axis=0, tiled=True),
    )
    got_rows = got_rows.reshape(owners, books_dev, capacity, feature_dim)
    got_codes = got_codes.reshape(owners, books_dev, capacity, codebooks)
    group_size = min(P_SIZE, 8)
    contract = (((0,), (0,)), ((), ()))
    rows_in = got_rows[:, 0].reshape(owners * capacity, feature_dim)
    tuples = got_codes[:, 0].reshape(owners * capacity, codebooks)
    book_global = my_group * books_dev + 0
    own_code = lax.dynamic_index_in_dim(tuples, book_global, 1, keepdims=False)
    local_row = own_code - my_owner * own_rows
    member = (local_row[:, None] == jnp.arange(own_rows, dtype=jnp.int32)).astype(jnp.bfloat16)
    right_side = lax.dot_general(member, rows_in, contract, preferred_element_type=jnp.float32)
    code_count = jnp.sum(member, axis=0, dtype=jnp.float32)
    current = codebook[0].astype(jnp.float32)
    updated_list = [current + (right_side - 2.0 * current) / (code_count[:, None] + 2.0)]
    first_row = book_global * K + my_owner * own_rows + 0
    partner = lax.dynamic_index_in_dim(pairs, first_row // BLK, 0, keepdims=False)
    partner_book = partner // KB
    partner_start = partner % KB * BLK
    partner_code = jnp.take(tuples, partner_book, axis=1) - partner_start[None, :]
    columns = []
    for group_index in range(P_SIZE // group_size):
        chosen = partner_code[:, group_index * group_size : (group_index + 1) * group_size]
        onehot_table = (chosen[:, :, None] == jnp.arange(BLK, dtype=jnp.int32)).astype(jnp.bfloat16)
        onehot_table = onehot_table.reshape(chosen.shape[0], group_size * BLK)
        columns.append(
            lax.dot_general(member, onehot_table, contract, preferred_element_type=jnp.float32)
        )
    gram_pieces = jnp.concatenate(columns, axis=1)
    gram_list = [gram_pieces]
    return (jnp.stack(updated_list), jnp.stack(gram_list))


def solution(mesh):
    in_specs = (P("ingest", None), P(None, "ingest"), P("codes", "ingest", None), P())
    out_specs = (P("codes", "ingest", None), P("codes", "ingest", None))
    return jax.shard_map(shards, mesh=mesh, in_specs=in_specs, out_specs=out_specs, check_vma=False)
```

profile of v0, /device:TPU:6, one launch (start us, length us, event | category | flops | bytes accessed | tf_op | source)
XLA Modules:
  0.0 258.5 jit_solution(1867541813753504236)
XLA Ops:
  7.2 0.7 multiply_subtract_fusion
  8.0 0.6 reduce-window.6
  8.6 0.2 slice_reduce_fusion
  9.1 0.1 fusion.38
  9.3 1.4 scatter_custom_fusion.1
  10.8 33.1 %all_to_all.24 = s32[64,1,8]{2,1,0:T(1,128)S(1)} all-to-all(s32[64,1,8]{2,1,0:T(1,128)S(1)} %bitcast.133), channel_id=1, replica_groups=mesh['ingest'=64,'codes'=8] {'ingest'}, dimensions={0} | all-to-all | bytes 4096 | tf_op jit(solution)/shard_map/all_to_all | solution.py:43
  44.3 2.1 gather_fusion.1
  46.4 1.1 bitcast_select_fusion.1
  47.5 4.7 %all-to-all-start.2 = ((bf16[64,8,1024]{2,1,0:T(8,128)(2,1)}), bf16[64,8,1024]{2,1,0:T(8,128)(2,1)S(1)}, u32[]{:S(2)}, u32[]{:S(2)}) async-start(bf16[64,8,1024]{2,1,0:T(8,128)(2,1)} %bitcast_select_fusion.1), calls=%async_computation.2 | async-start | bytes 2097152 | tf_op jit(solution)/shard_map/all_to_all | solution.py:47
  52.2 1.4 scatter_custom_fusion
  53.7 52.6 %all-to-all-done.2 = bf16[64,8,1024]{2,1,0:T(8,128)(2,1)S(1)} async-done(((bf16[64,8,1024]{2,1,0:T(8,128)(2,1)}), bf16[64,8,1024]{2,1,0:T(8,128)(2,1)S(1)}, u32[]{:S(2)}, u32[]{:S(2)}) %all-to-all-start.2) | async-done | bytes 1048608 | tf_op jit(solution)/shard_map/all_to_all | solution.py:47
  106.3 1.2 gather_fusion.2
  107.5 0.9 broadcast_select_fusion
  108.6 1.0 gather_fusion
  109.9 0.7 broadcast_select_fusion.1
  110.6 5.8 %all-to-all-start = ((s32[64,8,8]{1,2,0:T(8,128)}), s32[64,8,8]{1,2,0:T(8,128)S(1)}, u32[]{:S(2)}, u32[]{:S(2)}) async-start(s32[64,8,8]{1,2,0:T(8,128)} %broadcast_select_fusion.1), calls=%async_computation | async-start | bytes 524288 | tf_op jit(solution)/shard_map/all_to_all | solution.py:62
  116.5 57.7 %all-reduce.4.cloned.1.call-done = bf16[256,1024]{1,0:T(8,128)(2,1)} async-done(((bf16[256,1024]{1,0:T(8,128)(2,1)}), bf16[256,1024]{1,0:T(8,128)(2,1)}) %all-reduce.4.cloned.1.call-update) | async-done | bytes 524304 | tf_op jit(solution)/shard_map/psum | solution.py:50
  174.2 1.2 subtract_convert_fusion
  175.4 2.1 gather_fusion.3
  177.5 1.2 bitcast_select_fusion
  178.7 15.8 %all-to-all-start.3 = ((bf16[64,8,1024]{2,1,0:T(8,128)(2,1)}), bf16[64,8,1024]{2,1,0:T(8,128)(2,1)S(1)}, u32[]{:S(2)}, u32[]{:S(2)}) async-start(bf16[64,8,1024]{2,1,0:T(8,128)(2,1)} %bitcast_select_fusion), calls=%async_computation.3 | async-start | bytes 2097152 | tf_op jit(solution)/shard_map/all_to_all | solution.py:61
  194.6 0.2 fusion.41
  194.9 0.2 reshape_squeeze_reshape.6
  195.0 0.7 gather_fusion.4
  195.9 0.1 copy.73
  196.1 0.1 copy.74
  196.2 0.1 copy.75
  196.3 0.1 copy.76
  196.5 0.1 copy.77
  196.6 0.1 copy.78
  197.0 0.6 eq.209
  197.6 1.4 fusion.15
  199.0 0.6 eq.215
  199.6 1.4 fusion.14
  200.9 0.6 eq.218
  201.5 1.4 fusion.13
  202.9 0.6 eq.221
  203.5 1.4 fusion.12
  204.9 0.6 eq.224
  205.5 1.4 fusion.11
  206.8 0.6 eq.227
  207.4 1.4 fusion.10
  208.8 0.6 eq.230
  209.4 1.4 fusion.9
  210.8 0.6 eq.233
  211.4 1.4 fusion.8
  212.7 37.9 %all-to-all-done.3 = bf16[64,8,1024]{2,1,0:T(8,128)(2,1)S(1)} async-done(((bf16[64,8,1024]{2,1,0:T(8,128)(2,1)}), bf16[64,8,1024]{2,1,0:T(8,128)(2,1)S(1)}, u32[]{:S(2)}, u32[]{:S(2)}) %all-to-all-start.3) | async-done | bytes 1048608 | tf_op jit(solution)/shard_map/all_to_all | solution.py:61
  250.6 1.0 fusion.18
  (50 shorter events, 1.9 us)
Async XLA Ops:
  7.2 37.1 %copy-start = (bf16[1,64,1024]{2,1,0:T(8,128)(2,1)S(1)}, bf16[1,64,1024]{2,1,0:T(8,128)(2,1)}, u32[]{:S(2)}) copy-start(bf16[1,64,1024]{2,1,0:T(8,128)(2,1)} %param.6) | copy-start | bytes 393220
  47.5 58.8 %all-to-all-start.2 = ((bf16[64,8,1024]{2,1,0:T(8,128)(2,1)}), bf16[64,8,1024]{2,1,0:T(8,128)(2,1)S(1)}, u32[]{:S(2)}, u32[]{:S(2)}) async-start(bf16[64,8,1024]{2,1,0:T(8,128)(2,1)} %bitcast_select_fusion.1), calls=%async_computation.2 | async-start | bytes 2097152 | tf_op jit(solution)/shard_map/all_to_all | solution.py:47
  52.2 122.0 %all-reduce.4.cloned.1.call-start = ((), (), s32[]{:S(2)}) async-start(), calls=%async_computation.4 | async-start | bytes 1048576 | tf_op jit(solution)/shard_map/psum | solution.py:50
  106.3 2.1 copy-start.3
  108.6 65.6 %copy-start.1 = (bf16[256,1024]{1,0:T(8,128)(2,1)S(1)}, bf16[256,1024]{1,0:T(8,128)(2,1)}, u32[]{:S(2)}) copy-start(bf16[256,1024]{1,0:T(8,128)(2,1)} %param.4) | copy-start | bytes 1572868
  110.6 68.1 %all-to-all-start = ((s32[64,8,8]{1,2,0:T(8,128)}), s32[64,8,8]{1,2,0:T(8,128)S(1)}, u32[]{:S(2)}, u32[]{:S(2)}) async-start(s32[64,8,8]{1,2,0:T(8,128)} %broadcast_select_fusion.1), calls=%async_computation | async-start | bytes 524288 | tf_op jit(solution)/shard_map/all_to_all | solution.py:62
  177.5 17.0 %copy-start.2 = (s32[256,64]{0,1:T(8,128)S(1)}, s32[256,64]{0,1:T(8,128)}, u32[]{:S(2)}) copy-start(s32[256,64]{0,1:T(8,128)} %param.7) | copy-start | bytes 196612
  178.7 72.0 %all-to-all-start.3 = ((bf16[64,8,1024]{2,1,0:T(8,128)(2,1)}), bf16[64,8,1024]{2,1,0:T(8,128)(2,1)S(1)}, u32[]{:S(2)}, u32[]{:S(2)}) async-start(bf16[64,8,1024]{2,1,0:T(8,128)(2,1)} %bitcast_select_fusion), calls=%async_computation.3 | async-start | bytes 2097152 | tf_op jit(solution)/shard_map/all_to_all | solution.py:61
Sparse Core Ops, SparseCore 0:
  108.5 65.5 all-reduce.3
where the time goes:
time: 259 us; the launch traced here: 258 us
  waiting for transfers between devices  148 us (57%)
  blocking collectives  33.1 us (13%)
  starting transfers between devices  26.4 us (10%)
  local copies, waits for them, and re-layouts  17.1 us (7%)
  between operations  14.4 us (6%)
  matrix products  11.9 us (5%)
  other arithmetic  7.29 us (3%)
    psum x1, waiting for transfers between devices, shards(): lax.psum(partial_sum.astype(jnp.bfloat16), 'codes').astype(jnp.float32)  57.7 us
    all_to_all x1, waiting for transfers between devices, shards(): lax.all_to_all(picked, 'ingest', split_axis=0, concat_axis=0, tiled=True)  52.6 us
    all_to_all x1, waiting for transfers between devices, shards(): lax.all_to_all(send_rows, 'ingest', split_axis=0, concat_axis=0, tiled=True)  37.9 us
    all_to_all x1, blocking collectives, shards(): lax.all_to_all(slot_request, 'ingest', split_axis=0, concat_axis=0, tiled...  33.1 us
    all_to_all x1, starting transfers between devices, shards(): lax.all_to_all(send_rows, 'ingest', split_axis=0, concat_axis=0, tiled=True)  15.8 us
    dot_general x8, matrix products, shards(): lax.dot_general(member, onehot_table, contract, preferred_element_type=jn...  10.9 us
    all_to_all x1, starting transfers between devices, shards(): lax.all_to_all(send_codes, 'ingest', split_axis=0, concat_axis=0, tiled=T...  5.85 us
  transfers between devices with their start and end apart: 4, of which 3 were waited for; matrix products, arithmetic and copies ran while one was open for 10% of the time, Pallas kernels for 0%

commit v1 on v0

v1 whole, which is shorter than its diff:
```python
import jax
import jax.numpy as jnp
from jax import lax
from jax.sharding import Mesh, PartitionSpec as P

K = 4096
BLK = 128
P_SIZE = 64
KB = 32
Z, Y, X, C = 16, 4, 4, 2
SIZES = {"z": Z, "y": Y, "x": X, "core": C}
CAP = 8
HALF = 32
CONTRACT_FIRST = (((0,), (0,)), ((), ()))
CONTRACT_INNER = (((1,), (0,)), ((), ()))


def pull(value, axis, step):
    size = SIZES[axis]
    return lax.ppermute(value, axis, [((i + step) % size, i) for i in range(size)])


def gather_codes(codes):
    far = jnp.stack([codes] + [pull(codes, "z", 4 * j) for j in (1, 2, 3)])
    return jnp.stack([far, pull(far, "z", 1), pull(far, "z", 2), pull(far, "z", -1)])


def gather_book(part, first, second):
    line = jnp.stack([part] + [pull(part, first, s) for s in (1, 2, 3)])
    plane = [line] + [pull(line, second, s) for s in (1, 2, 3)]
    stacked = jnp.stack(plane, axis=1 if first == "x" else 0)
    return stacked.reshape(X * Y * part.shape[0], part.shape[1])


def half_round(value):
    return value.astype(jnp.bfloat16)


def wide(value):
    return value.astype(jnp.float32)


def reconstruct(onehot, book, chain):
    partial = lax.dot_general(onehot, book, CONTRACT_FIRST, preferred_element_type=jnp.float32)
    rows = partial.shape[0] // 2
    features = partial.shape[1]
    merged = partial[:rows] + wide(pull(half_round(partial[rows:]), "core", 1))
    merged = merged.reshape(4, 4, HALF, features)
    two = half_round(merged[2])
    if chain:
        two = pull(jnp.concatenate([two[3:], two[:3]]), "z", 2)
    else:
        two = pull(two, "z", -2)
    near = merged[0] + wide(pull(half_round(merged[1]), "z", -1))
    near = near + wide(pull(half_round(merged[3]), "z", 1)) + wide(two)
    recon = near[0]
    for j in (1, 2, 3):
        recon = recon + wide(pull(half_round(near[j]), "z", -4 * j))
    return recon


def spread(residual, chain):
    far = jnp.stack([residual] + [pull(residual, "z", 4 * j) for j in (1, 2, 3)])
    if chain:
        two = pull(far, "z", -2)
        two = jnp.concatenate([two[1:], two[:1]])
    else:
        two = pull(far, "z", 2)
    own = jnp.stack([far, pull(far, "z", 1), two, pull(far, "z", -1)])
    own = own.reshape(16 * HALF, residual.shape[1])
    return jnp.concatenate([own, pull(own, "core", 1)])


def collect(onehot, residuals, first, second):
    partial = lax.dot_general(
        onehot, residuals, CONTRACT_INNER, preferred_element_type=jnp.float32
    )
    partial = partial.reshape(X, Y, -1, partial.shape[1])
    if first == "y":
        partial = jnp.swapaxes(partial, 0, 1)
    line = partial[0]
    for s in (1, 2, 3):
        line = line + wide(pull(half_round(partial[s]), first, -s))
    total = line[0]
    for s in (1, 2, 3):
        total = total + wide(pull(half_round(line[s]), second, -s))
    return total


def gram_block(all_codes, pairs, book, owner, own_rows):
    blocks, codebooks, length = all_codes.shape
    mine = lax.dynamic_index_in_dim(all_codes, book, 1, keepdims=False)
    hit = mine // own_rows == owner
    upper = (jnp.arange(length)[:, None] < jnp.arange(length)[None, :]).astype(jnp.bfloat16)
    rank = lax.dot_general(
        hit.astype(jnp.bfloat16), upper, CONTRACT_INNER, preferred_element_type=jnp.float32
    ).astype(jnp.int32)
    rank = jnp.where(hit, rank, -1)
    slots = jnp.arange(CAP, dtype=jnp.int32)
    chosen = (rank[:, None, :] == slots[None, :, None]).astype(jnp.bfloat16)
    digits = jnp.concatenate([all_codes // BLK, all_codes % BLK], axis=1).astype(jnp.bfloat16)
    packed = lax.dot_general(
        chosen, digits, (((2,), (2,)), ((0,), (0,))), preferred_element_type=jnp.float32
    ).astype(jnp.int32)
    filled = slots[None, :] < jnp.sum(hit.astype(jnp.int32), axis=1)[:, None]
    tuples = packed[:, :, :codebooks] * BLK + packed[:, :, codebooks:]
    tuples = jnp.where(filled[:, :, None], tuples, -1).reshape(blocks * CAP, codebooks)
    own_code = lax.dynamic_index_in_dim(tuples, book, 1, keepdims=False)
    local_row = own_code - owner * own_rows
    member = (local_row[:, None] == jnp.arange(own_rows, dtype=jnp.int32)).astype(jnp.bfloat16)
    code_count = jnp.sum(member, axis=0, dtype=jnp.float32)
    first_row = book * K + owner * own_rows
    partner = lax.dynamic_index_in_dim(pairs, first_row // BLK, 0, keepdims=False)
    partner_book = partner // KB
    partner_start = partner % KB * BLK
    partner_code = jnp.take(tuples, partner_book, axis=1) - partner_start[None, :]
    group = 8
    columns = []
    for g in range(P_SIZE // group):
        part = partner_code[:, g * group : (g + 1) * group]
        table = (part[:, :, None] == jnp.arange(BLK, dtype=jnp.int32)).astype(jnp.bfloat16)
        table = table.reshape(part.shape[0], group * BLK)
        columns.append(
            lax.dot_general(member, table, CONTRACT_FIRST, preferred_element_type=jnp.float32)
        )
    return jnp.concatenate(columns, axis=1), code_count


def shards(vectors, codes, codebook, pairs):
    z, y = lax.axis_index("z"), lax.axis_index("y")
    x, core = lax.axis_index("x"), lax.axis_index("core")
    codebooks, length = codes.shape
    own_rows, features = codebook.shape[1:]
    owner = z * Y + y
    book = x * C + core
    width = features // 2
    zcodes = gather_codes(codes)
    all_codes = jnp.stack([zcodes] + [pull(zcodes, "y", s) for s in (1, 2, 3)])
    portion = 2 * HALF * x
    starts = (portion + HALF * core, portion + HALF * (1 - core))
    picked = jnp.stack([lax.dynamic_slice_in_dim(zcodes, s, HALF, 3) for s in starts])
    held = [
        lax.dynamic_index_in_dim(picked, (x + s) % X * C + core, 3, keepdims=False)
        for s in range(X)
    ]
    held = jnp.stack(held).reshape(X, 2 * 16 * HALF)
    relative = jnp.where(
        held // (Y * own_rows) == z, (held - owner * own_rows) % (Y * own_rows), -1
    )
    local = jnp.arange(Y * own_rows, dtype=jnp.int32)
    onehot = (relative[:, None, :] == local[None, :, None]).astype(jnp.bfloat16)
    onehot = onehot.reshape(X * Y * own_rows, 2 * 16 * HALF)
    mine = lax.dynamic_slice_in_dim(vectors, starts[0], HALF, 0)
    orders = (("x", "y"), ("y", "x"))
    totals = []
    for chain, (first, second) in enumerate(orders):
        part = codebook[0, :, chain * width : (chain + 1) * width]
        rows = gather_book(part, first, second)
        recon = reconstruct(onehot, rows, chain)
        wanted = mine[:, chain * width : (chain + 1) * width]
        residual = half_round(wide(wanted) - recon)
        totals.append(collect(onehot, spread(residual, chain), first, second))
    right_side = jnp.concatenate(totals, axis=1)
    flat_codes = all_codes.reshape(-1, codebooks, length)
    gram, code_count = gram_block(flat_codes, pairs, book, owner, own_rows)
    current = wide(codebook[0])
    updated = current + (right_side - 2.0 * current) / (code_count[:, None] + 2.0)
    return updated[None], gram[None]


def solution(mesh):
    grid = Mesh(mesh.devices.reshape(Z, Y, X, C), ("z", "y", "x", "core"))
    rows, books = ("z", "y"), ("x", "core")
    in_specs = (P(rows, None), P(None, rows), P(books, rows, None), P())
    out_specs = (P(books, rows, None), P(books, rows, None))
    return jax.shard_map(shards, mesh=grid, in_specs=in_specs, out_specs=out_specs, check_vma=False)
```

time: 259 us -> 301 us (1.16)
  starting transfers between devices: 26.4 us -> 244 us
  waiting for transfers between devices: 148 us -> 16.4 us
  blocking collectives: 33.1 us -> 0 us
  between operations: 14.4 us -> 2.17 us
  local copies, waits for them, and re-layouts: 17.1 us -> 10.6 us
  other arithmetic: 7.29 us -> 12.7 us
    ppermute x0 -> x61, starting transfers between devices: none -> 244 us  [pull(): lax.ppermute(value, axis, [((i + step) % size, i) for i in range(size)])]
    all_to_all x3 -> x0, waiting for transfers between devices: 90.5 us -> none  [the longest x1 52.6 us: shards(): lax.all_to_all(picked, 'ingest', split_axis=0, concat_axis=0, tiled=True)]
    psum x1 -> x0, waiting for transfers between devices: 57.7 us -> none  [shards(): lax.psum(partial_sum.astype(jnp.bfloat16), 'codes').astype(jnp.float32)]
    all_to_all x1 -> x0, blocking collectives: 33.1 us -> none  [shards(): lax.all_to_all(slot_request, 'ingest', split_axis=0, concat_axis=0, tiled...]
    all_to_all x3 -> x0, starting transfers between devices: 26.3 us -> none  [the longest x1 15.8 us: shards(): lax.all_to_all(send_rows, 'ingest', split_axis=0, concat_axis=0, tiled=True)]
    ppermute x0 -> x61, waiting for transfers between devices: none -> 16.4 us  [pull(): lax.ppermute(value, axis, [((i + step) % size, i) for i in range(size)])]
    another operation x2 -> x20, other arithmetic: 0.65 us -> 7.08 us  [the longest x4 3.53 us: gather_book(): stacked = jnp.stack(plane, axis=1 if first == 'x' else 0)]
    gather x6 -> x1, local copies, waits for them, and re-layouts: 7.09 us -> 0.67 us  [gram_block(): jnp.take(tuples, partner_book, axis=1) - partner_start[None, :]]
  transfers between devices with their start and end apart: 4 -> 61, of which waited for: 3 -> 9; matrix products, arithmetic and copies ran while one was open for 10% -> 11% of each run, Pallas kernels for 0% -> 0%
where the time goes in v1:
time: 301 us; the launch traced here: 298 us
  starting transfers between devices  244 us (81%)
  waiting for transfers between devices  16.4 us (5%)
  matrix products  12.9 us (4%)
  other arithmetic  12.7 us (4%)
  local copies, waits for them, and re-layouts  10.6 us (4%)
    ppermute x61, starting transfers between devices, pull(): lax.ppermute(value, axis, [((i + step) % size, i) for i in range(size)])  244 us
    ppermute x61, waiting for transfers between devices, pull(): lax.ppermute(value, axis, [((i + step) % size, i) for i in range(size)])  16.4 us
    dot_general x8, matrix products, gram_block(): lax.dot_general(member, table, CONTRACT_FIRST, preferred_element_type=jnp...  7.38 us
  transfers between devices with their start and end apart: 61, of which 9 were waited for; matrix products, arithmetic and copies ran while one was open for 11% of the time, Pallas kernels for 0%

profile of v1, /device:TPU:6, one launch (start us, length us, event | category | flops | bytes accessed | tf_op | source)
XLA Modules:
  0.0 298.4 jit_solution(10161843482560428862)
XLA Ops:
  0.6 9.1 %collective-permute-start.2 = (s32[8,256]{1,0:T(8,128)}, s32[8,256]{1,0:T(8,128)S(1)}, u32[]{:S(2)}, u32[]{:S(2)}) collective-permute-start(s32[8,256]{1,0:T(8,128)} %param.5), channel_id=1, source_target_pairs={{384,0},{416,32},{448,64},{480,96},{0,128},{32,160},{64,192},{96,2... | collective-permute-start | bytes 24584 | tf_op jit(solution)/shard_map/ppermute | solution.py:20
  9.7 10.9 %collective-permute-start.1 = (s32[8,256]{1,0:T(8,128)}, s32[8,256]{1,0:T(8,128)S(1)}, u32[]{:S(2)}, u32[]{:S(2)}) collective-permute-start(s32[8,256]{1,0:T(8,128)} %param.5), channel_id=1, source_target_pairs={{256,0},{288,32},{320,64},{352,96},{384,128},{416,160},{448,192},{... | collective-permute-start | bytes 24584 | tf_op jit(solution)/shard_map/ppermute | solution.py:20
  20.7 5.5 %collective-permute-start = (s32[8,256]{1,0:T(8,128)}, s32[8,256]{1,0:T(8,128)S(1)}, u32[]{:S(2)}, u32[]{:S(2)}) collective-permute-start(s32[8,256]{1,0:T(8,128)} %param.5), channel_id=1, source_target_pairs={{128,0},{160,32},{192,64},{224,96},{256,128},{288,160},{320,192},{... | collective-permute-start | bytes 24584 | tf_op jit(solution)/shard_map/ppermute | solution.py:20
  29.4 4.3 %collective-permute-start.7 = (bf16[64,512]{1,0:T(8,128)(2,1)S(1)}, bf16[64,512]{1,0:T(8,128)(2,1)S(1)}, u32[]{:S(2)}, u32[]{:S(2)}) collective-permute-start(bf16[64,512]{1,0:T(8,128)(2,1)S(1)} %get-tuple-element.63), channel_id=1, source_target_pairs={{4,0},{6,2},{0,4},{2,6},{5,1},{7,3},{1,5},{3,7},{12,8},{14,10},{8,... | collective-permute-start | bytes 196616 | tf_op jit(solution)/shard_map/ppermute | solution.py:20
  35.6 2.9 collective-permute-start.5
  41.0 3.6 %collective-permute-start.3 = (s32[4,8,256]{2,1,0:T(8,128)S(1)}, s32[4,8,256]{2,1,0:T(8,128)S(1)}, u32[]{:S(2)}, u32[]{:S(2)}) collective-permute-start(s32[4,8,256]{2,1,0:T(8,128)S(1)} %get-tuple-element.74), channel_id=1, source_target_pairs={{32,0},{64,32},{96,64},{128,96},{160,128},{192,160},{224,192},{256... | collective-permute-start | bytes 98312 | tf_op jit(solution)/shard_map/ppermute | solution.py:20
  46.6 3.5 %collective-permute-start.34 = (bf16[64,512]{1,0:T(8,128)(2,1)S(1)}, bf16[64,512]{1,0:T(8,128)(2,1)S(1)}, u32[]{:S(2)}, u32[]{:S(2)}) collective-permute-start(bf16[64,512]{1,0:T(8,128)(2,1)S(1)} %get-tuple-element.64), channel_id=1, source_target_pairs={{24,0},{0,8},{8,16},{16,24},{25,1},{1,9},{9,17},{17,25},{26,2},{2,... | collective-permute-start | bytes 196616 | tf_op jit(solution)/shard_map/ppermute | solution.py:20
  50.1 4.8 %collective-permute-start.33 = (bf16[64,512]{1,0:T(8,128)(2,1)S(1)}, bf16[64,512]{1,0:T(8,128)(2,1)S(1)}, u32[]{:S(2)}, u32[]{:S(2)}) collective-permute-start(bf16[64,512]{1,0:T(8,128)(2,1)S(1)} %get-tuple-element.64), channel_id=1, source_target_pairs={{16,0},{24,8},{0,16},{8,24},{17,1},{25,9},{1,17},{9,25},{18,2},{26... | collective-permute-start | bytes 196616 | tf_op jit(solution)/shard_map/ppermute | solution.py:20
  58.0 3.3 %collective-permute-start.32 = (bf16[64,512]{1,0:T(8,128)(2,1)S(1)}, bf16[64,512]{1,0:T(8,128)(2,1)S(1)}, u32[]{:S(2)}, u32[]{:S(2)}) collective-permute-start(bf16[64,512]{1,0:T(8,128)(2,1)S(1)} %get-tuple-element.64), channel_id=1, source_target_pairs={{8,0},{16,8},{24,16},{0,24},{9,1},{17,9},{25,17},{1,25},{10,2},{18... | collective-permute-start | bytes 196616 | tf_op jit(solution)/shard_map/ppermute | solution.py:20
  63.8 2.7 collective-permute-start.59
  66.6 3.8 %collective-permute-start.58 = (s32[4,4,8,256]{3,2,1,0:T(8,128)S(1)}, s32[4,4,8,256]{3,2,1,0:T(8,128)S(1)}, u32[]{:S(2)}, u32[]{:S(2)}) collective-permute-start(s32[4,4,8,256]{3,2,1,0:T(8,128)S(1)} %get-tuple-element.56), channel_id=1, source_target_pairs={{8,0},{16,8},{24,16},{0,24},{9,1},{17,9},{25,17},{1,25},{10,2},{18... | collective-permute-start | bytes 393224 | tf_op jit(solution)/shard_map/ppermute | solution.py:20
  73.9 4.0 %collective-permute-start.10 = (bf16[4,64,512]{2,1,0:T(8,128)(2,1)}, bf16[4,64,512]{2,1,0:T(8,128)(2,1)}, u32[]{:S(2)}, u32[]{:S(2)}) collective-permute-start(bf16[4,64,512]{2,1,0:T(8,128)(2,1)} %get-tuple-element.41), channel_id=1, source_target_pairs={{16,0},{24,8},{0,16},{8,24},{17,1},{25,9},{1,17},{9,25},{18,2},{26... | collective-permute-start | bytes 786440 | tf_op jit(solution)/shard_map/ppermute | solution.py:20
  78.0 5.1 %collective-permute-start.37 = (bf16[4,64,512]{2,1,0:T(8,128)(2,1)S(1)}, bf16[4,64,512]{2,1,0:T(8,128)(2,1)}, u32[]{:S(2)}, u32[]{:S(2)}) collective-permute-start(bf16[4,64,512]{2,1,0:T(8,128)(2,1)S(1)} %get-tuple-element.46), channel_id=1, source_target_pairs={{6,0},{0,2},{2,4},{4,6},{7,1},{1,3},{3,5},{5,7},{14,8},{8,10},{10,... | collective-permute-start | bytes 786440 | tf_op jit(solution)/shard_map/ppermute | solution.py:20
  85.1 3.3 %collective-permute-start.35 = (bf16[4,64,512]{2,1,0:T(8,128)(2,1)S(1)}, bf16[4,64,512]{2,1,0:T(8,128)(2,1)}, u32[]{:S(2)}, u32[]{:S(2)}) collective-permute-start(bf16[4,64,512]{2,1,0:T(8,128)(2,1)S(1)} %get-tuple-element.46), channel_id=1, source_target_pairs={{2,0},{4,2},{6,4},{0,6},{3,1},{5,3},{7,5},{1,7},{10,8},{12,10},{14... | collective-permute-start | bytes 786440 | tf_op jit(solution)/shard_map/ppermute | solution.py:20
  96.5 4.5 %collective-permute-start.9 = (bf16[4,64,512]{2,1,0:T(8,128)(2,1)}, bf16[4,64,512]{2,1,0:T(8,128)(2,1)}, u32[]{:S(2)}, u32[]{:S(2)}) collective-permute-start(bf16[4,64,512]{2,1,0:T(8,128)(2,1)} %get-tuple-element.41), channel_id=1, source_target_pairs={{8,0},{16,8},{24,16},{0,24},{9,1},{17,9},{25,17},{1,25},{10,2},{18... | collective-permute-start | bytes 786440 | tf_op jit(solution)/shard_map/ppermute | solution.py:20
  116.4 4.8 %collective-permute-start.15 = (bf16[4,32,512]{2,1,0:T(8,128)(2,1)S(1)}, bf16[4,32,512]{2,1,0:T(8,128)(2,1)S(1)}, u32[]{:S(2)}, u32[]{:S(2)}) collective-permute-start(bf16[4,32,512]{2,1,0:T(8,128)(2,1)S(1)} %bitcast.322), channel_id=1, source_target_pairs={{448,0},{480,32},{0,64},{32,96},{64,128},{96,160},{128,192},{160,2... | collective-permute-start | bytes 393224 | tf_op jit(solution)/shard_map/ppermute | solution.py:20
  121.2 3.1 %collective-permute-start.14 = (bf16[4,32,512]{2,1,0:T(8,128)(2,1)S(1)}, bf16[4,32,512]{2,1,0:T(8,128)(2,1)S(1)}, u32[]{:S(2)}, u32[]{:S(2)}) collective-permute-start(bf16[4,32,512]{2,1,0:T(8,128)(2,1)S(1)} %bitcast.321), channel_id=1, source_target_pairs={{32,0},{64,32},{96,64},{128,96},{160,128},{192,160},{224,192},{256... | collective-permute-start | bytes 393224 | tf_op jit(solution)/shard_map/ppermute | solution.py:20
  124.4 2.7 collective-permute-start.13
  127.1 3.1 %collective-permute-start.41 = (bf16[4,32,512]{2,1,0:T(8,128)(2,1)S(1)}, bf16[4,32,512]{2,1,0:T(8,128)(2,1)S(1)}, u32[]{:S(2)}, u32[]{:S(2)}) collective-permute-start(bf16[4,32,512]{2,1,0:T(8,128)(2,1)S(1)} %pad_maximum_fusion.7), channel_id=1, source_target_pairs={{64,0},{96,32},{128,64},{160,96},{192,128},{224,160},{256,192},{28... | collective-permute-start | bytes 393224 | tf_op jit(solution)/shard_map/ppermute | solution.py:20
  130.3 3.1 %collective-permute-start.40 = (bf16[4,32,512]{2,1,0:T(8,128)(2,1)S(1)}, bf16[4,32,512]{2,1,0:T(8,128)(2,1)S(1)}, u32[]{:S(2)}, u32[]{:S(2)}) collective-permute-start(bf16[4,32,512]{2,1,0:T(8,128)(2,1)S(1)} %bitcast.319), channel_id=1, source_target_pairs={{32,0},{64,32},{96,64},{128,96},{160,128},{192,160},{224,192},{256... | collective-permute-start | bytes 393224 | tf_op jit(solution)/shard_map/ppermute | solution.py:20
  133.4 3.4 %collective-permute-start.39 = (bf16[4,32,512]{2,1,0:T(8,128)(2,1)S(1)}, bf16[4,32,512]{2,1,0:T(8,128)(2,1)S(1)}, u32[]{:S(2)}, u32[]{:S(2)}) collective-permute-start(bf16[4,32,512]{2,1,0:T(8,128)(2,1)S(1)} %bitcast.318), channel_id=1, source_target_pairs={{480,0},{0,32},{32,64},{64,96},{96,128},{128,160},{160,192},{192,2... | collective-permute-start | bytes 393224 | tf_op jit(solution)/shard_map/ppermute | solution.py:20
  138.9 10.6 %collective-permute-start.17 = (bf16[32,512]{1,0:T(8,128)(2,1)S(1)}, bf16[32,512]{1,0:T(8,128)(2,1)S(1)}, u32[]{:S(2)}, u32[]{:S(2)}) collective-permute-start(bf16[32,512]{1,0:T(8,128)(2,1)S(1)} %get-tuple-element.61), channel_id=1, source_target_pairs={{256,0},{288,32},{320,64},{352,96},{384,128},{416,160},{448,192},{... | collective-permute-start | bytes 98312 | tf_op jit(solution)/shard_map/ppermute | solution.py:20
  149.5 4.3 %collective-permute-start.16 = (bf16[32,512]{1,0:T(8,128)(2,1)S(1)}, bf16[32,512]{1,0:T(8,128)(2,1)S(1)}, u32[]{:S(2)}, u32[]{:S(2)}) collective-permute-start(bf16[32,512]{1,0:T(8,128)(2,1)S(1)} %get-tuple-element.59), channel_id=1, source_target_pairs={{384,0},{416,32},{448,64},{480,96},{0,128},{32,160},{64,192},{96,2... | collective-permute-start | bytes 98312 | tf_op jit(solution)/shard_map/ppermute | solution.py:20
  153.9 5.5 %collective-permute-start.44 = (bf16[32,512]{1,0:T(8,128)(2,1)S(1)}, bf16[32,512]{1,0:T(8,128)(2,1)S(1)}, u32[]{:S(2)}, u32[]{:S(2)}) collective-permute-start(bf16[32,512]{1,0:T(8,128)(2,1)S(1)} %get-tuple-element.69), channel_id=1, source_target_pairs={{128,0},{160,32},{192,64},{224,96},{256,128},{288,160},{320,192},{... | collective-permute-start | bytes 98312 | tf_op jit(solution)/shard_map/ppermute | solution.py:20
  159.4 3.9 %collective-permute-start.43 = (bf16[32,512]{1,0:T(8,128)(2,1)S(1)}, bf16[32,512]{1,0:T(8,128)(2,1)S(1)}, u32[]{:S(2)}, u32[]{:S(2)}) collective-permute-start(bf16[32,512]{1,0:T(8,128)(2,1)S(1)} %get-tuple-element.70), channel_id=1, source_target_pairs={{256,0},{288,32},{320,64},{352,96},{384,128},{416,160},{448,192},{... | collective-permute-start | bytes 98312 | tf_op jit(solution)/shard_map/ppermute | solution.py:20
  163.3 7.8 %collective-permute-start.42 = (bf16[32,512]{1,0:T(8,128)(2,1)S(1)}, bf16[32,512]{1,0:T(8,128)(2,1)S(1)}, u32[]{:S(2)}, u32[]{:S(2)}) collective-permute-start(bf16[32,512]{1,0:T(8,128)(2,1)S(1)} %get-tuple-element.68), channel_id=1, source_target_pairs={{384,0},{416,32},{448,64},{480,96},{0,128},{32,160},{64,192},{96,2... | collective-permute-start | bytes 98312 | tf_op jit(solution)/shard_map/ppermute | solution.py:20
  174.8 7.1 %collective-permute-start.47 = (bf16[32,512]{1,0:T(8,128)(2,1)S(1)}, bf16[32,512]{1,0:T(8,128)(2,1)S(1)}, u32[]{:S(2)}, u32[]{:S(2)}) collective-permute-start(bf16[32,512]{1,0:T(8,128)(2,1)S(1)} %get-tuple-element.31), channel_id=1, source_target_pairs={{384,0},{416,32},{448,64},{480,96},{0,128},{32,160},{64,192},{96,2... | collective-permute-start | bytes 98312 | tf_op jit(solution)/shard_map/ppermute | solution.py:20
  182.0 7.1 %collective-permute-start.46 = (bf16[32,512]{1,0:T(8,128)(2,1)S(1)}, bf16[32,512]{1,0:T(8,128)(2,1)S(1)}, u32[]{:S(2)}, u32[]{:S(2)}) collective-permute-start(bf16[32,512]{1,0:T(8,128)(2,1)S(1)} %get-tuple-element.31), channel_id=1, source_target_pairs={{256,0},{288,32},{320,64},{352,96},{384,128},{416,160},{448,192},{... | collective-permute-start | bytes 98312 | tf_op jit(solution)/shard_map/ppermute | solution.py:20
  189.1 5.2 %collective-permute-start.45 = (bf16[32,512]{1,0:T(8,128)(2,1)S(1)}, bf16[32,512]{1,0:T(8,128)(2,1)S(1)}, u32[]{:S(2)}, u32[]{:S(2)}) collective-permute-start(bf16[32,512]{1,0:T(8,128)(2,1)S(1)} %get-tuple-element.31), channel_id=1, source_target_pairs={{128,0},{160,32},{192,64},{224,96},{256,128},{288,160},{320,192},{... | collective-permute-start | bytes 98312 | tf_op jit(solution)/shard_map/ppermute | solution.py:20
  196.6 2.9 collective-permute-done.45
  199.5 3.1 %collective-permute-start.50 = (bf16[4,32,512]{2,1,0:T(8,128)(2,1)S(1)}, bf16[4,32,512]{2,1,0:T(8,128)(2,1)S(1)}, u32[]{:S(2)}, u32[]{:S(2)}) collective-permute-start(bf16[4,32,512]{2,1,0:T(8,128)(2,1)S(1)} %get-tuple-element.67), channel_id=1, source_target_pairs={{480,0},{0,32},{32,64},{64,96},{96,128},{128,160},{160,192},{192,2... | collective-permute-start | bytes 393224 | tf_op jit(solution)/shard_map/ppermute | solution.py:20
  204.6 4.8 %collective-permute-start.48 = (bf16[4,32,512]{2,1,0:T(8,128)(2,1)S(1)}, bf16[4,32,512]{2,1,0:T(8,128)(2,1)S(1)}, u32[]{:S(2)}, u32[]{:S(2)}) collective-permute-start(bf16[4,32,512]{2,1,0:T(8,128)(2,1)S(1)} %get-tuple-element.67), channel_id=1, source_target_pairs={{32,0},{64,32},{96,64},{128,96},{160,128},{192,160},{224,192},{256... | collective-permute-start | bytes 393224 | tf_op jit(solution)/shard_map/ppermute | solution.py:20
  211.4 4.3 %collective-permute-start.21 = (bf16[32,512]{1,0:T(8,128)(2,1)S(1)}, bf16[32,512]{1,0:T(8,128)(2,1)S(1)}, u32[]{:S(2)}, u32[]{:S(2)}) collective-permute-start(bf16[32,512]{1,0:T(8,128)(2,1)S(1)} %get-tuple-element.30), channel_id=1, source_target_pairs={{384,0},{416,32},{448,64},{480,96},{0,128},{32,160},{64,192},{96,2... | collective-permute-start | bytes 98312 | tf_op jit(solution)/shard_map/ppermute | solution.py:20
  215.7 8.4 %collective-permute-start.20 = (bf16[32,512]{1,0:T(8,128)(2,1)S(1)}, bf16[32,512]{1,0:T(8,128)(2,1)S(1)}, u32[]{:S(2)}, u32[]{:S(2)}) collective-permute-start(bf16[32,512]{1,0:T(8,128)(2,1)S(1)} %get-tuple-element.30), channel_id=1, source_target_pairs={{256,0},{288,32},{320,64},{352,96},{384,128},{416,160},{448,192},{... | collective-permute-start | bytes 98312 | tf_op jit(solution)/shard_map/ppermute | solution.py:20
  224.1 5.1 %collective-permute-start.19 = (bf16[32,512]{1,0:T(8,128)(2,1)S(1)}, bf16[32,512]{1,0:T(8,128)(2,1)S(1)}, u32[]{:S(2)}, u32[]{:S(2)}) collective-permute-start(bf16[32,512]{1,0:T(8,128)(2,1)S(1)} %get-tuple-element.30), channel_id=1, source_target_pairs={{128,0},{160,32},{192,64},{224,96},{256,128},{288,160},{320,192},{... | collective-permute-start | bytes 98312 | tf_op jit(solution)/shard_map/ppermute | solution.py:20
  235.8 5.2 %collective-permute-start.23 = (bf16[4,32,512]{2,1,0:T(8,128)(2,1)S(1)}, bf16[4,32,512]{2,1,0:T(8,128)(2,1)S(1)}, u32[]{:S(2)}, u32[]{:S(2)}) collective-permute-start(bf16[4,32,512]{2,1,0:T(8,128)(2,1)S(1)} %get-tuple-element.58), channel_id=1, source_target_pairs={{64,0},{96,32},{128,64},{160,96},{192,128},{224,160},{256,192},{28... | collective-permute-start | bytes 393224 | tf_op jit(solution)/shard_map/ppermute | solution.py:20
  243.0 3.3 %collective-permute-done.23 = bf16[4,32,512]{2,1,0:T(8,128)(2,1)S(1)} collective-permute-done((bf16[4,32,512]{2,1,0:T(8,128)(2,1)S(1)}, bf16[4,32,512]{2,1,0:T(8,128)(2,1)S(1)}, u32[]{:S(2)}, u32[]{:S(2)}) %collective-permute-start.23) | collective-permute-done | bytes 131104 | tf_op jit(solution)/shard_map/ppermute | solution.py:20
  254.1 3.4 %collective-permute-start.53 = (bf16[4,64,512]{2,1,0:T(8,128)(2,1)S(1)}, bf16[4,64,512]{2,1,0:T(8,128)(2,1)S(1)}, u32[]{:S(2)}, u32[]{:S(2)}) collective-permute-start(bf16[4,64,512]{2,1,0:T(8,128)(2,1)S(1)} %get-tuple-element.27), channel_id=1, source_target_pairs={{16,0},{24,8},{0,16},{8,24},{17,1},{25,9},{1,17},{9,25},{18,2},{26... | collective-permute-start | bytes 786440 | tf_op jit(solution)/shard_map/ppermute | solution.py:20
  261.4 3.9 %collective-permute-start.28 = (bf16[4,64,512]{2,1,0:T(8,128)(2,1)S(1)}, bf16[4,64,512]{2,1,0:T(8,128)(2,1)S(1)}, u32[]{:S(2)}, u32[]{:S(2)}) collective-permute-start(bf16[4,64,512]{2,1,0:T(8,128)(2,1)S(1)} %bitcast.306), channel_id=1, source_target_pairs={{2,0},{4,2},{6,4},{0,6},{3,1},{5,3},{7,5},{1,7},{10,8},{12,10},{14... | collective-permute-start | bytes 786440 | tf_op jit(solution)/shard_map/ppermute | solution.py:20
  265.4 3.2 %collective-permute-start.27 = (bf16[4,64,512]{2,1,0:T(8,128)(2,1)S(1)}, bf16[4,64,512]{2,1,0:T(8,128)(2,1)S(1)}, u32[]{:S(2)}, u32[]{:S(2)}) collective-permute-start(bf16[4,64,512]{2,1,0:T(8,128)(2,1)S(1)} %bitcast.305), channel_id=1, source_target_pairs={{4,0},{6,2},{0,4},{2,6},{5,1},{7,3},{1,5},{3,7},{12,8},{14,10},{8,... | collective-permute-start | bytes 786440 | tf_op jit(solution)/shard_map/ppermute | solution.py:20
  268.6 3.3 %collective-permute-start.26 = (bf16[4,64,512]{2,1,0:T(8,128)(2,1)S(1)}, bf16[4,64,512]{2,1,0:T(8,128)(2,1)S(1)}, u32[]{:S(2)}, u32[]{:S(2)}) collective-permute-start(bf16[4,64,512]{2,1,0:T(8,128)(2,1)S(1)} %bitcast.304), channel_id=1, source_target_pairs={{6,0},{0,2},{2,4},{4,6},{7,1},{1,3},{3,5},{5,7},{14,8},{8,10},{10,... | collective-permute-start | bytes 786440 | tf_op jit(solution)/shard_map/ppermute | solution.py:20
  272.2 3.9 %collective-permute-start.57 = (bf16[64,512]{1,0:T(8,128)(2,1)S(1)}, bf16[64,512]{1,0:T(8,128)(2,1)S(1)}, u32[]{:S(2)}, u32[]{:S(2)}) collective-permute-start(bf16[64,512]{1,0:T(8,128)(2,1)S(1)} %get-tuple-element.43), channel_id=1, source_target_pairs={{2,0},{4,2},{6,4},{0,6},{3,1},{5,3},{7,5},{1,7},{10,8},{12,10},{14... | collective-permute-start | bytes 196616 | tf_op jit(solution)/shard_map/ppermute | solution.py:20
  276.1 3.2 %collective-permute-start.56 = (bf16[64,512]{1,0:T(8,128)(2,1)S(1)}, bf16[64,512]{1,0:T(8,128)(2,1)S(1)}, u32[]{:S(2)}, u32[]{:S(2)}) collective-permute-start(bf16[64,512]{1,0:T(8,128)(2,1)S(1)} %get-tuple-element.44), channel_id=1, source_target_pairs={{4,0},{6,2},{0,4},{2,6},{5,1},{7,3},{1,5},{3,7},{12,8},{14,10},{8,... | collective-permute-start | bytes 196616 | tf_op jit(solution)/shard_map/ppermute | solution.py:20
  279.3 3.3 %collective-permute-start.55 = (bf16[64,512]{1,0:T(8,128)(2,1)S(1)}, bf16[64,512]{1,0:T(8,128)(2,1)S(1)}, u32[]{:S(2)}, u32[]{:S(2)}) collective-permute-start(bf16[64,512]{1,0:T(8,128)(2,1)S(1)} %get-tuple-element.42), channel_id=1, source_target_pairs={{6,0},{0,2},{2,4},{4,6},{7,1},{1,3},{3,5},{5,7},{14,8},{8,10},{10,... | collective-permute-start | bytes 196616 | tf_op jit(solution)/shard_map/ppermute | solution.py:20
  282.8 4.0 %collective-permute-start.31 = (bf16[64,512]{1,0:T(8,128)(2,1)S(1)}, bf16[64,512]{1,0:T(8,128)(2,1)S(1)}, u32[]{:S(2)}, u32[]{:S(2)}) collective-permute-start(bf16[64,512]{1,0:T(8,128)(2,1)S(1)} %get-tuple-element.38), channel_id=1, source_target_pairs={{8,0},{16,8},{24,16},{0,24},{9,1},{17,9},{25,17},{1,25},{10,2},{18... | collective-permute-start | bytes 196616 | tf_op jit(solution)/shard_map/ppermute | solution.py:20
  286.9 3.3 %collective-permute-start.30 = (bf16[64,512]{1,0:T(8,128)(2,1)S(1)}, bf16[64,512]{1,0:T(8,128)(2,1)S(1)}, u32[]{:S(2)}, u32[]{:S(2)}) collective-permute-start(bf16[64,512]{1,0:T(8,128)(2,1)S(1)} %get-tuple-element.39), channel_id=1, source_target_pairs={{16,0},{24,8},{0,16},{8,24},{17,1},{25,9},{1,17},{9,25},{18,2},{26... | collective-permute-start | bytes 196616 | tf_op jit(solution)/shard_map/ppermute | solution.py:20
  290.2 3.3 %collective-permute-start.29 = (bf16[64,512]{1,0:T(8,128)(2,1)S(1)}, bf16[64,512]{1,0:T(8,128)(2,1)S(1)}, u32[]{:S(2)}, u32[]{:S(2)}) collective-permute-start(bf16[64,512]{1,0:T(8,128)(2,1)S(1)} %get-tuple-element.37), channel_id=1, source_target_pairs={{24,0},{0,8},{8,16},{16,24},{25,1},{1,9},{9,17},{17,25},{26,2},{2,... | collective-permute-start | bytes 196616 | tf_op jit(solution)/shard_map/ppermute | solution.py:20
  294.9 2.6 collective-permute-done.29
  (182 shorter events, 78.3 us)
Async XLA Ops:
  0.6 34.2 %collective-permute-start.2 = (s32[8,256]{1,0:T(8,128)}, s32[8,256]{1,0:T(8,128)S(1)}, u32[]{:S(2)}, u32[]{:S(2)}) collective-permute-start(s32[8,256]{1,0:T(8,128)} %param.5), channel_id=1, source_target_pairs={{384,0},{416,32},{448,64},{480,96},{0,128},{32,160},{64,192},{96,2... | collective-permute-start | bytes 24584 | tf_op jit(solution)/shard_map/ppermute | solution.py:20
  9.7 25.1 %collective-permute-start.1 = (s32[8,256]{1,0:T(8,128)}, s32[8,256]{1,0:T(8,128)S(1)}, u32[]{:S(2)}, u32[]{:S(2)}) collective-permute-start(s32[8,256]{1,0:T(8,128)} %param.5), channel_id=1, source_target_pairs={{256,0},{288,32},{320,64},{352,96},{384,128},{416,160},{448,192},{... | collective-permute-start | bytes 24584 | tf_op jit(solution)/shard_map/ppermute | solution.py:20
  20.7 14.2 %collective-permute-start = (s32[8,256]{1,0:T(8,128)}, s32[8,256]{1,0:T(8,128)S(1)}, u32[]{:S(2)}, u32[]{:S(2)}) collective-permute-start(s32[8,256]{1,0:T(8,128)} %param.5), channel_id=1, source_target_pairs={{128,0},{160,32},{192,64},{224,96},{256,128},{288,160},{320,192},{... | collective-permute-start | bytes 24584 | tf_op jit(solution)/shard_map/ppermute | solution.py:20
  27.0 30.9 %collective-permute-start.8 = (bf16[64,512]{1,0:T(8,128)(2,1)S(1)}, bf16[64,512]{1,0:T(8,128)(2,1)S(1)}, u32[]{:S(2)}, u32[]{:S(2)}) collective-permute-start(bf16[64,512]{1,0:T(8,128)(2,1)S(1)} %get-tuple-element.63), channel_id=1, source_target_pairs={{6,0},{0,2},{2,4},{4,6},{7,1},{1,3},{3,5},{5,7},{14,8},{8,10},{10,... | collective-permute-start | bytes 196616 | tf_op jit(solution)/shard_map/ppermute | solution.py:20
  29.4 31.8 %collective-permute-start.7 = (bf16[64,512]{1,0:T(8,128)(2,1)S(1)}, bf16[64,512]{1,0:T(8,128)(2,1)S(1)}, u32[]{:S(2)}, u32[]{:S(2)}) collective-permute-start(bf16[64,512]{1,0:T(8,128)(2,1)S(1)} %get-tuple-element.63), channel_id=1, source_target_pairs={{4,0},{6,2},{0,4},{2,6},{5,1},{7,3},{1,5},{3,7},{12,8},{14,10},{8,... | collective-permute-start | bytes 196616 | tf_op jit(solution)/shard_map/ppermute | solution.py:20
  44.7 19.2 %collective-permute-start.6 = (bf16[64,512]{1,0:T(8,128)(2,1)S(1)}, bf16[64,512]{1,0:T(8,128)(2,1)S(1)}, u32[]{:S(2)}, u32[]{:S(2)}) collective-permute-start(bf16[64,512]{1,0:T(8,128)(2,1)S(1)} %get-tuple-element.63), channel_id=1, source_target_pairs={{2,0},{4,2},{6,4},{0,6},{3,1},{5,3},{7,5},{1,7},{10,8},{12,10},{14... | collective-permute-start | bytes 196616 | tf_op jit(solution)/shard_map/ppermute | solution.py:20
  46.6 20.0 %collective-permute-start.34 = (bf16[64,512]{1,0:T(8,128)(2,1)S(1)}, bf16[64,512]{1,0:T(8,128)(2,1)S(1)}, u32[]{:S(2)}, u32[]{:S(2)}) collective-permute-start(bf16[64,512]{1,0:T(8,128)(2,1)S(1)} %get-tuple-element.64), channel_id=1, source_target_pairs={{24,0},{0,8},{8,16},{16,24},{25,1},{1,9},{9,17},{17,25},{26,2},{2,... | collective-permute-start | bytes 196616 | tf_op jit(solution)/shard_map/ppermute | solution.py:20
  50.1 21.1 %collective-permute-start.33 = (bf16[64,512]{1,0:T(8,128)(2,1)S(1)}, bf16[64,512]{1,0:T(8,128)(2,1)S(1)}, u32[]{:S(2)}, u32[]{:S(2)}) collective-permute-start(bf16[64,512]{1,0:T(8,128)(2,1)S(1)} %get-tuple-element.64), channel_id=1, source_target_pairs={{16,0},{24,8},{0,16},{8,24},{17,1},{25,9},{1,17},{9,25},{18,2},{26... | collective-permute-start | bytes 196616 | tf_op jit(solution)/shard_map/ppermute | solution.py:20
  58.0 15.9 %collective-permute-start.32 = (bf16[64,512]{1,0:T(8,128)(2,1)S(1)}, bf16[64,512]{1,0:T(8,128)(2,1)S(1)}, u32[]{:S(2)}, u32[]{:S(2)}) collective-permute-start(bf16[64,512]{1,0:T(8,128)(2,1)S(1)} %get-tuple-element.64), channel_id=1, source_target_pairs={{8,0},{16,8},{24,16},{0,24},{9,1},{17,9},{25,17},{1,25},{10,2},{18... | collective-permute-start | bytes 196616 | tf_op jit(solution)/shard_map/ppermute | solution.py:20
  61.2 16.7 %collective-permute-start.60 = (s32[4,4,8,256]{3,2,1,0:T(8,128)S(1)}, s32[4,4,8,256]{3,2,1,0:T(8,128)S(1)}, u32[]{:S(2)}, u32[]{:S(2)}) collective-permute-start(s32[4,4,8,256]{3,2,1,0:T(8,128)S(1)} %get-tuple-element.56), channel_id=1, source_target_pairs={{24,0},{0,8},{8,16},{16,24},{25,1},{1,9},{9,17},{17,25},{26,2},{2,... | collective-permute-start | bytes 393224 | tf_op jit(solution)/shard_map/ppermute | solution.py:20
  63.8 19.3 %collective-permute-start.59 = (s32[4,4,8,256]{3,2,1,0:T(8,128)S(1)}, s32[4,4,8,256]{3,2,1,0:T(8,128)S(1)}, u32[]{:S(2)}, u32[]{:S(2)}) collective-permute-start(s32[4,4,8,256]{3,2,1,0:T(8,128)S(1)} %get-tuple-element.56), channel_id=1, source_target_pairs={{16,0},{24,8},{0,16},{8,24},{17,1},{25,9},{1,17},{9,25},{18,2},{26... | collective-permute-start | bytes 393224 | tf_op jit(solution)/shard_map/ppermute | solution.py:20
  66.6 18.5 %collective-permute-start.58 = (s32[4,4,8,256]{3,2,1,0:T(8,128)S(1)}, s32[4,4,8,256]{3,2,1,0:T(8,128)S(1)}, u32[]{:S(2)}, u32[]{:S(2)}) collective-permute-start(s32[4,4,8,256]{3,2,1,0:T(8,128)S(1)} %get-tuple-element.56), channel_id=1, source_target_pairs={{8,0},{16,8},{24,16},{0,24},{9,1},{17,9},{25,17},{1,25},{10,2},{18... | collective-permute-start | bytes 393224 | tf_op jit(solution)/shard_map/ppermute | solution.py:20
  71.2 38.1 %collective-permute-start.11 = (bf16[4,64,512]{2,1,0:T(8,128)(2,1)}, bf16[4,64,512]{2,1,0:T(8,128)(2,1)}, u32[]{:S(2)}, u32[]{:S(2)}) collective-permute-start(bf16[4,64,512]{2,1,0:T(8,128)(2,1)} %get-tuple-element.41), channel_id=1, source_target_pairs={{24,0},{0,8},{8,16},{16,24},{25,1},{1,9},{9,17},{17,25},{26,2},{2,... | collective-permute-start | bytes 786440 | tf_op jit(solution)/shard_map/ppermute | solution.py:20
  73.9 35.4 %collective-permute-start.10 = (bf16[4,64,512]{2,1,0:T(8,128)(2,1)}, bf16[4,64,512]{2,1,0:T(8,128)(2,1)}, u32[]{:S(2)}, u32[]{:S(2)}) collective-permute-start(bf16[4,64,512]{2,1,0:T(8,128)(2,1)} %get-tuple-element.41), channel_id=1, source_target_pairs={{16,0},{24,8},{0,16},{8,24},{17,1},{25,9},{1,17},{9,25},{18,2},{26... | collective-permute-start | bytes 786440 | tf_op jit(solution)/shard_map/ppermute | solution.py:20
  78.0 18.5 %collective-permute-start.37 = (bf16[4,64,512]{2,1,0:T(8,128)(2,1)S(1)}, bf16[4,64,512]{2,1,0:T(8,128)(2,1)}, u32[]{:S(2)}, u32[]{:S(2)}) collective-permute-start(bf16[4,64,512]{2,1,0:T(8,128)(2,1)S(1)} %get-tuple-element.46), channel_id=1, source_target_pairs={{6,0},{0,2},{2,4},{4,6},{7,1},{1,3},{3,5},{5,7},{14,8},{8,10},{10,... | collective-permute-start | bytes 786440 | tf_op jit(solution)/shard_map/ppermute | solution.py:20
  83.1 17.9 %collective-permute-start.36 = (bf16[4,64,512]{2,1,0:T(8,128)(2,1)S(1)}, bf16[4,64,512]{2,1,0:T(8,128)(2,1)}, u32[]{:S(2)}, u32[]{:S(2)}) collective-permute-start(bf16[4,64,512]{2,1,0:T(8,128)(2,1)S(1)} %get-tuple-element.46), channel_id=1, source_target_pairs={{4,0},{6,2},{0,4},{2,6},{5,1},{7,3},{1,5},{3,7},{12,8},{14,10},{8,... | collective-permute-start | bytes 786440 | tf_op jit(solution)/shard_map/ppermute | solution.py:20
  85.1 15.9 %collective-permute-start.35 = (bf16[4,64,512]{2,1,0:T(8,128)(2,1)S(1)}, bf16[4,64,512]{2,1,0:T(8,128)(2,1)}, u32[]{:S(2)}, u32[]{:S(2)}) collective-permute-start(bf16[4,64,512]{2,1,0:T(8,128)(2,1)S(1)} %get-tuple-element.46), channel_id=1, source_target_pairs={{2,0},{4,2},{6,4},{0,6},{3,1},{5,3},{7,5},{1,7},{10,8},{12,10},{14... | collective-permute-start | bytes 786440 | tf_op jit(solution)/shard_map/ppermute | solution.py:20
  96.5 12.8 %collective-permute-start.9 = (bf16[4,64,512]{2,1,0:T(8,128)(2,1)}, bf16[4,64,512]{2,1,0:T(8,128)(2,1)}, u32[]{:S(2)}, u32[]{:S(2)}) collective-permute-start(bf16[4,64,512]{2,1,0:T(8,128)(2,1)} %get-tuple-element.41), channel_id=1, source_target_pairs={{8,0},{16,8},{24,16},{0,24},{9,1},{17,9},{25,17},{1,25},{10,2},{18... | collective-permute-start | bytes 786440 | tf_op jit(solution)/shard_map/ppermute | solution.py:20
  116.4 17.1 %collective-permute-start.15 = (bf16[4,32,512]{2,1,0:T(8,128)(2,1)S(1)}, bf16[4,32,512]{2,1,0:T(8,128)(2,1)S(1)}, u32[]{:S(2)}, u32[]{:S(2)}) collective-permute-start(bf16[4,32,512]{2,1,0:T(8,128)(2,1)S(1)} %bitcast.322), channel_id=1, source_target_pairs={{448,0},{480,32},{0,64},{32,96},{64,128},{96,160},{128,192},{160,2... | collective-permute-start | bytes 393224 | tf_op jit(solution)/shard_map/ppermute | solution.py:20
  121.2 15.6 %collective-permute-start.14 = (bf16[4,32,512]{2,1,0:T(8,128)(2,1)S(1)}, bf16[4,32,512]{2,1,0:T(8,128)(2,1)S(1)}, u32[]{:S(2)}, u32[]{:S(2)}) collective-permute-start(bf16[4,32,512]{2,1,0:T(8,128)(2,1)S(1)} %bitcast.321), channel_id=1, source_target_pairs={{32,0},{64,32},{96,64},{128,96},{160,128},{192,160},{224,192},{256... | collective-permute-start | bytes 393224 | tf_op jit(solution)/shard_map/ppermute | solution.py:20
  124.4 12.5 %collective-permute-start.13 = (bf16[4,32,512]{2,1,0:T(8,128)(2,1)S(1)}, bf16[4,32,512]{2,1,0:T(8,128)(2,1)S(1)}, u32[]{:S(2)}, u32[]{:S(2)}) collective-permute-start(bf16[4,32,512]{2,1,0:T(8,128)(2,1)S(1)} %bitcast.320), channel_id=1, source_target_pairs={{480,0},{0,32},{32,64},{64,96},{96,128},{128,160},{160,192},{192,2... | collective-permute-start | bytes 393224 | tf_op jit(solution)/shard_map/ppermute | solution.py:20
  127.1 22.4 %collective-permute-start.41 = (bf16[4,32,512]{2,1,0:T(8,128)(2,1)S(1)}, bf16[4,32,512]{2,1,0:T(8,128)(2,1)S(1)}, u32[]{:S(2)}, u32[]{:S(2)}) collective-permute-start(bf16[4,32,512]{2,1,0:T(8,128)(2,1)S(1)} %pad_maximum_fusion.7), channel_id=1, source_target_pairs={{64,0},{96,32},{128,64},{160,96},{192,128},{224,160},{256,192},{28... | collective-permute-start | bytes 393224 | tf_op jit(solution)/shard_map/ppermute | solution.py:20
  130.3 23.6 %collective-permute-start.40 = (bf16[4,32,512]{2,1,0:T(8,128)(2,1)S(1)}, bf16[4,32,512]{2,1,0:T(8,128)(2,1)S(1)}, u32[]{:S(2)}, u32[]{:S(2)}) collective-permute-start(bf16[4,32,512]{2,1,0:T(8,128)(2,1)S(1)} %bitcast.319), channel_id=1, source_target_pairs={{32,0},{64,32},{96,64},{128,96},{160,128},{192,160},{224,192},{256... | collective-permute-start | bytes 393224 | tf_op jit(solution)/shard_map/ppermute | solution.py:20
  133.4 20.4 %collective-permute-start.39 = (bf16[4,32,512]{2,1,0:T(8,128)(2,1)S(1)}, bf16[4,32,512]{2,1,0:T(8,128)(2,1)S(1)}, u32[]{:S(2)}, u32[]{:S(2)}) collective-permute-start(bf16[4,32,512]{2,1,0:T(8,128)(2,1)S(1)} %bitcast.318), channel_id=1, source_target_pairs={{480,0},{0,32},{32,64},{64,96},{96,128},{128,160},{160,192},{192,2... | collective-permute-start | bytes 393224 | tf_op jit(solution)/shard_map/ppermute | solution.py:20
  136.9 26.4 %collective-permute-start.18 = (bf16[32,512]{1,0:T(8,128)(2,1)S(1)}, bf16[32,512]{1,0:T(8,128)(2,1)S(1)}, u32[]{:S(2)}, u32[]{:S(2)}) collective-permute-start(bf16[32,512]{1,0:T(8,128)(2,1)S(1)} %get-tuple-element.60), channel_id=1, source_target_pairs={{128,0},{160,32},{192,64},{224,96},{256,128},{288,160},{320,192},{... | collective-permute-start | bytes 98312 | tf_op jit(solution)/shard_map/ppermute | solution.py:20
  138.9 34.4 %collective-permute-start.17 = (bf16[32,512]{1,0:T(8,128)(2,1)S(1)}, bf16[32,512]{1,0:T(8,128)(2,1)S(1)}, u32[]{:S(2)}, u32[]{:S(2)}) collective-permute-start(bf16[32,512]{1,0:T(8,128)(2,1)S(1)} %get-tuple-element.61), channel_id=1, source_target_pairs={{256,0},{288,32},{320,64},{352,96},{384,128},{416,160},{448,192},{... | collective-permute-start | bytes 98312 | tf_op jit(solution)/shard_map/ppermute | solution.py:20
  149.5 23.8 %collective-permute-start.16 = (bf16[32,512]{1,0:T(8,128)(2,1)S(1)}, bf16[32,512]{1,0:T(8,128)(2,1)S(1)}, u32[]{:S(2)}, u32[]{:S(2)}) collective-permute-start(bf16[32,512]{1,0:T(8,128)(2,1)S(1)} %get-tuple-element.59), channel_id=1, source_target_pairs={{384,0},{416,32},{448,64},{480,96},{0,128},{32,160},{64,192},{96,2... | collective-permute-start | bytes 98312 | tf_op jit(solution)/shard_map/ppermute | solution.py:20
  153.9 19.4 %collective-permute-start.44 = (bf16[32,512]{1,0:T(8,128)(2,1)S(1)}, bf16[32,512]{1,0:T(8,128)(2,1)S(1)}, u32[]{:S(2)}, u32[]{:S(2)}) collective-permute-start(bf16[32,512]{1,0:T(8,128)(2,1)S(1)} %get-tuple-element.69), channel_id=1, source_target_pairs={{128,0},{160,32},{192,64},{224,96},{256,128},{288,160},{320,192},{... | collective-permute-start | bytes 98312 | tf_op jit(solution)/shard_map/ppermute | solution.py:20
  159.4 14.6 %collective-permute-start.43 = (bf16[32,512]{1,0:T(8,128)(2,1)S(1)}, bf16[32,512]{1,0:T(8,128)(2,1)S(1)}, u32[]{:S(2)}, u32[]{:S(2)}) collective-permute-start(bf16[32,512]{1,0:T(8,128)(2,1)S(1)} %get-tuple-element.70), channel_id=1, source_target_pairs={{256,0},{288,32},{320,64},{352,96},{384,128},{416,160},{448,192},{... | collective-permute-start | bytes 98312 | tf_op jit(solution)/shard_map/ppermute | solution.py:20
  174.8 21.6 %collective-permute-start.47 = (bf16[32,512]{1,0:T(8,128)(2,1)S(1)}, bf16[32,512]{1,0:T(8,128)(2,1)S(1)}, u32[]{:S(2)}, u32[]{:S(2)}) collective-permute-start(bf16[32,512]{1,0:T(8,128)(2,1)S(1)} %get-tuple-element.31), channel_id=1, source_target_pairs={{384,0},{416,32},{448,64},{480,96},{0,128},{32,160},{64,192},{96,2... | collective-permute-start | bytes 98312 | tf_op jit(solution)/shard_map/ppermute | solution.py:20
  182.0 14.7 %collective-permute-start.46 = (bf16[32,512]{1,0:T(8,128)(2,1)S(1)}, bf16[32,512]{1,0:T(8,128)(2,1)S(1)}, u32[]{:S(2)}, u32[]{:S(2)}) collective-permute-start(bf16[32,512]{1,0:T(8,128)(2,1)S(1)} %get-tuple-element.31), channel_id=1, source_target_pairs={{256,0},{288,32},{320,64},{352,96},{384,128},{416,160},{448,192},{... | collective-permute-start | bytes 98312 | tf_op jit(solution)/shard_map/ppermute | solution.py:20
  199.5 29.8 %collective-permute-start.50 = (bf16[4,32,512]{2,1,0:T(8,128)(2,1)S(1)}, bf16[4,32,512]{2,1,0:T(8,128)(2,1)S(1)}, u32[]{:S(2)}, u32[]{:S(2)}) collective-permute-start(bf16[4,32,512]{2,1,0:T(8,128)(2,1)S(1)} %get-tuple-element.67), channel_id=1, source_target_pairs={{480,0},{0,32},{32,64},{64,96},{96,128},{128,160},{160,192},{192,2... | collective-permute-start | bytes 393224 | tf_op jit(solution)/shard_map/ppermute | solution.py:20
  202.7 21.4 %collective-permute-start.49 = (bf16[4,32,512]{2,1,0:T(8,128)(2,1)S(1)}, bf16[4,32,512]{2,1,0:T(8,128)(2,1)S(1)}, u32[]{:S(2)}, u32[]{:S(2)}) collective-permute-start(bf16[4,32,512]{2,1,0:T(8,128)(2,1)S(1)} %get-tuple-element.67), channel_id=1, source_target_pairs={{448,0},{480,32},{0,64},{32,96},{64,128},{96,160},{128,192},{160,2... | collective-permute-start | bytes 393224 | tf_op jit(solution)/shard_map/ppermute | solution.py:20
  204.6 24.7 %collective-permute-start.48 = (bf16[4,32,512]{2,1,0:T(8,128)(2,1)S(1)}, bf16[4,32,512]{2,1,0:T(8,128)(2,1)S(1)}, u32[]{:S(2)}, u32[]{:S(2)}) collective-permute-start(bf16[4,32,512]{2,1,0:T(8,128)(2,1)S(1)} %get-tuple-element.67), channel_id=1, source_target_pairs={{32,0},{64,32},{96,64},{128,96},{160,128},{192,160},{224,192},{256... | collective-permute-start | bytes 393224 | tf_op jit(solution)/shard_map/ppermute | solution.py:20
  211.4 20.1 %collective-permute-start.21 = (bf16[32,512]{1,0:T(8,128)(2,1)S(1)}, bf16[32,512]{1,0:T(8,128)(2,1)S(1)}, u32[]{:S(2)}, u32[]{:S(2)}) collective-permute-start(bf16[32,512]{1,0:T(8,128)(2,1)S(1)} %get-tuple-element.30), channel_id=1, source_target_pairs={{384,0},{416,32},{448,64},{480,96},{0,128},{32,160},{64,192},{96,2... | collective-permute-start | bytes 98312 | tf_op jit(solution)/shard_map/ppermute | solution.py:20
  215.7 15.7 %collective-permute-start.20 = (bf16[32,512]{1,0:T(8,128)(2,1)S(1)}, bf16[32,512]{1,0:T(8,128)(2,1)S(1)}, u32[]{:S(2)}, u32[]{:S(2)}) collective-permute-start(bf16[32,512]{1,0:T(8,128)(2,1)S(1)} %get-tuple-element.30), channel_id=1, source_target_pairs={{256,0},{288,32},{320,64},{352,96},{384,128},{416,160},{448,192},{... | collective-permute-start | bytes 98312 | tf_op jit(solution)/shard_map/ppermute | solution.py:20
  229.4 21.4 %collective-permute-start.51 = (bf16[512,512]{1,0:T(8,128)(2,1)S(1)}, bf16[512,512]{1,0:T(8,128)(2,1)S(1)}, u32[]{:S(2)}, u32[]{:S(2)}) collective-permute-start(bf16[512,512]{1,0:T(8,128)(2,1)S(1)} %bitcast.299), channel_id=1, source_target_pairs={{1,0},{0,1},{3,2},{2,3},{5,4},{4,5},{7,6},{6,7},{9,8},{8,9},{11,10... | collective-permute-start | bytes 1572872 | tf_op jit(solution)/shard_map/ppermute | solution.py:20
  248.9 11.2 %collective-permute-start.25 = (bf16[512,512]{1,0:T(8,128)(2,1)S(1)}, bf16[512,512]{1,0:T(8,128)(2,1)S(1)}, u32[]{:S(2)}, u32[]{:S(2)}) collective-permute-start(bf16[512,512]{1,0:T(8,128)(2,1)S(1)} %bitcast.301), channel_id=1, source_target_pairs={{1,0},{0,1},{3,2},{2,3},{5,4},{4,5},{7,6},{6,7},{9,8},{8,9},{11,10... | collective-permute-start | bytes 1572872 | tf_op jit(solution)/shard_map/ppermute | solution.py:20
  252.2 16.4 %collective-permute-start.54 = (bf16[4,64,512]{2,1,0:T(8,128)(2,1)S(1)}, bf16[4,64,512]{2,1,0:T(8,128)(2,1)S(1)}, u32[]{:S(2)}, u32[]{:S(2)}) collective-permute-start(bf16[4,64,512]{2,1,0:T(8,128)(2,1)S(1)} %get-tuple-element.26), channel_id=1, source_target_pairs={{8,0},{16,8},{24,16},{0,24},{9,1},{17,9},{25,17},{1,25},{10,2},{18... | collective-permute-start | bytes 786440 | tf_op jit(solution)/shard_map/ppermute | solution.py:20
  254.1 17.8 %collective-permute-start.53 = (bf16[4,64,512]{2,1,0:T(8,128)(2,1)S(1)}, bf16[4,64,512]{2,1,0:T(8,128)(2,1)S(1)}, u32[]{:S(2)}, u32[]{:S(2)}) collective-permute-start(bf16[4,64,512]{2,1,0:T(8,128)(2,1)S(1)} %get-tuple-element.27), channel_id=1, source_target_pairs={{16,0},{24,8},{0,16},{8,24},{17,1},{25,9},{1,17},{9,25},{18,2},{26... | collective-permute-start | bytes 786440 | tf_op jit(solution)/shard_map/ppermute | solution.py:20
  257.6 14.4 %collective-permute-start.52 = (bf16[4,64,512]{2,1,0:T(8,128)(2,1)S(1)}, bf16[4,64,512]{2,1,0:T(8,128)(2,1)S(1)}, u32[]{:S(2)}, u32[]{:S(2)}) collective-permute-start(bf16[4,64,512]{2,1,0:T(8,128)(2,1)S(1)} %get-tuple-element.25), channel_id=1, source_target_pairs={{24,0},{0,8},{8,16},{16,24},{25,1},{1,9},{9,17},{17,25},{26,2},{2,... | collective-permute-start | bytes 786440 | tf_op jit(solution)/shard_map/ppermute | solution.py:20
  261.4 17.9 %collective-permute-start.28 = (bf16[4,64,512]{2,1,0:T(8,128)(2,1)S(1)}, bf16[4,64,512]{2,1,0:T(8,128)(2,1)S(1)}, u32[]{:S(2)}, u32[]{:S(2)}) collective-permute-start(bf16[4,64,512]{2,1,0:T(8,128)(2,1)S(1)} %bitcast.306), channel_id=1, source_target_pairs={{2,0},{4,2},{6,4},{0,6},{3,1},{5,3},{7,5},{1,7},{10,8},{12,10},{14... | collective-permute-start | bytes 786440 | tf_op jit(solution)/shard_map/ppermute | solution.py:20
  265.4 17.3 %collective-permute-start.27 = (bf16[4,64,512]{2,1,0:T(8,128)(2,1)S(1)}, bf16[4,64,512]{2,1,0:T(8,128)(2,1)S(1)}, u32[]{:S(2)}, u32[]{:S(2)}) collective-permute-start(bf16[4,64,512]{2,1,0:T(8,128)(2,1)S(1)} %bitcast.305), channel_id=1, source_target_pairs={{4,0},{6,2},{0,4},{2,6},{5,1},{7,3},{1,5},{3,7},{12,8},{14,10},{8,... | collective-permute-start | bytes 786440 | tf_op jit(solution)/shard_map/ppermute | solution.py:20
  268.6 14.1 %collective-permute-start.26 = (bf16[4,64,512]{2,1,0:T(8,128)(2,1)S(1)}, bf16[4,64,512]{2,1,0:T(8,128)(2,1)S(1)}, u32[]{:S(2)}, u32[]{:S(2)}) collective-permute-start(bf16[4,64,512]{2,1,0:T(8,128)(2,1)S(1)} %bitcast.304), channel_id=1, source_target_pairs={{6,0},{0,2},{2,4},{4,6},{7,1},{1,3},{3,5},{5,7},{14,8},{8,10},{10,... | collective-permute-start | bytes 786440 | tf_op jit(solution)/shard_map/ppermute | solution.py:20
  272.2 18.0 %collective-permute-start.57 = (bf16[64,512]{1,0:T(8,128)(2,1)S(1)}, bf16[64,512]{1,0:T(8,128)(2,1)S(1)}, u32[]{:S(2)}, u32[]{:S(2)}) collective-permute-start(bf16[64,512]{1,0:T(8,128)(2,1)S(1)} %get-tuple-element.43), channel_id=1, source_target_pairs={{2,0},{4,2},{6,4},{0,6},{3,1},{5,3},{7,5},{1,7},{10,8},{12,10},{14... | collective-permute-start | bytes 196616 | tf_op jit(solution)/shard_map/ppermute | solution.py:20
  276.1 17.4 %collective-permute-start.56 = (bf16[64,512]{1,0:T(8,128)(2,1)S(1)}, bf16[64,512]{1,0:T(8,128)(2,1)S(1)}, u32[]{:S(2)}, u32[]{:S(2)}) collective-permute-start(bf16[64,512]{1,0:T(8,128)(2,1)S(1)} %get-tuple-element.44), channel_id=1, source_target_pairs={{4,0},{6,2},{0,4},{2,6},{5,1},{7,3},{1,5},{3,7},{12,8},{14,10},{8,... | collective-permute-start | bytes 196616 | tf_op jit(solution)/shard_map/ppermute | solution.py:20
  279.3 14.2 %collective-permute-start.55 = (bf16[64,512]{1,0:T(8,128)(2,1)S(1)}, bf16[64,512]{1,0:T(8,128)(2,1)S(1)}, u32[]{:S(2)}, u32[]{:S(2)}) collective-permute-start(bf16[64,512]{1,0:T(8,128)(2,1)S(1)} %get-tuple-element.42), channel_id=1, source_target_pairs={{6,0},{0,2},{2,4},{4,6},{7,1},{1,3},{3,5},{5,7},{14,8},{8,10},{10,... | collective-permute-start | bytes 196616 | tf_op jit(solution)/shard_map/ppermute | solution.py:20
  282.8 10.7 %collective-permute-start.31 = (bf16[64,512]{1,0:T(8,128)(2,1)S(1)}, bf16[64,512]{1,0:T(8,128)(2,1)S(1)}, u32[]{:S(2)}, u32[]{:S(2)}) collective-permute-start(bf16[64,512]{1,0:T(8,128)(2,1)S(1)} %get-tuple-element.38), channel_id=1, source_target_pairs={{8,0},{16,8},{24,16},{0,24},{9,1},{17,9},{25,17},{1,25},{10,2},{18... | collective-permute-start | bytes 196616 | tf_op jit(solution)/shard_map/ppermute | solution.py:20
  (17 other events, 148.8 us)

commit v2 on v0

v2 whole, which is shorter than its diff:
```python
import functools

import jax
import jax.numpy as jnp
from jax import lax
from jax.experimental import pallas as pl
from jax.experimental.pallas import tpu as pltpu
from jax.sharding import Mesh, PartitionSpec as P

K = 4096
BLK = 128
P_SIZE = 64
KB = 32
Z, Y, X, C = 16, 4, 4, 2
SIZES = {"z": Z, "y": Y, "x": X, "core": C}
OWN = 64
CAP = 8
HALF = 32
PLANE = Y * OWN
CHUNK = 512
NT = (((1,), (1,)), ((), ()))
NN = (((1,), (0,)), ((), ()))


def pull(value, axis, step):
    size = SIZES[axis]
    return lax.ppermute(value, axis, [((i + step) % size, i) for i in range(size)])


def ring_pull(value):
    pairs = []
    for z in range(Z):
        pairs.append((((z + 1) % Z) * C, z * C))
        pairs.append((((z - 1) % Z) * C + 1, z * C + 1))
    return lax.ppermute(value, ("z", "core"), pairs)


def gather_codes(codes):
    held = codes[None]
    for step in (8, 4, 2, 1):
        held = jnp.concatenate([held, pull(held, "z", step)])
    by_z = held
    for step in (2, 1):
        held = jnp.concatenate([held, pull(held, "y", step)])
    return by_z, held


def gather_rows(piece):
    start = jnp.stack([piece, pull(piece, "core", 1)])
    chain = [start]
    for _ in range(7):
        chain.append(ring_pull(chain[-1]))
    last = ring_pull(chain[7][0])
    early = pull(jnp.stack(chain[1:5]), "core", 1)
    late = pull(jnp.concatenate(chain[5:8] + [last[None]]), "core", 1)
    other = [None] + [early[i] for i in range(4)] + [late[2 * i : 2 * i + 2] for i in range(3)]
    ends = (last, late[6])
    order = []
    for e in range(2):
        order += [chain[t][e] for t in range(8)] + [ends[e]]
        order += [other[16 - t][1 - e] for t in range(9, 16)]
    book = jnp.concatenate([unit[:OWN] for unit in order])
    vectors = jnp.concatenate([unit[OWN:] for unit in order])
    return book, vectors


def compact(all_codes, local):
    blocks, codebooks, length = all_codes.shape
    ranges = local // OWN
    hit = ranges[:, :, None, :] == jnp.arange(Y, dtype=jnp.int32)[None, None, :, None]
    hit = hit.reshape(blocks, X * Y, length)
    lane = jnp.arange(length)
    upper = (lane[:, None] < lane[None, :]).astype(jnp.bfloat16)
    rank = lax.dot_general(
        hit.astype(jnp.bfloat16).reshape(blocks * X * Y, length),
        upper,
        NN,
        preferred_element_type=jnp.float32,
    )
    rank = jnp.where(hit, rank.reshape(hit.shape).astype(jnp.int32), -1)
    slots = jnp.arange(CAP, dtype=jnp.int32)
    chosen = (rank[:, :, None, :] == slots[None, None, :, None]).astype(jnp.bfloat16)
    chosen = chosen.reshape(blocks, X * Y * CAP, length)
    digits = jnp.concatenate([all_codes // BLK, all_codes % BLK], axis=1).astype(jnp.bfloat16)
    packed = lax.dot_general(
        digits, chosen, (((2,), (2,)), ((0,), (0,))), preferred_element_type=jnp.float32
    ).astype(jnp.int32)
    filled = slots < jnp.sum(hit.astype(jnp.int32), axis=2)[:, :, None]
    filled = filled.reshape(blocks, 1, X * Y * CAP)
    tuples = jnp.where(filled, packed[:, :codebooks] * BLK + packed[:, codebooks:], -1)
    tuples = tuples.reshape(blocks, codebooks, X, Y * CAP)
    return tuples.transpose(2, 1, 0, 3)


def match(index_row, count):
    ids = lax.broadcasted_iota(jnp.int32, (count, index_row.shape[1]), 0)
    return jnp.where(ids == index_row, 1.0, 0.0).astype(jnp.bfloat16)


def pair_kernel(row_ref, column_ref, out_ref, total_ref):
    step = pl.program_id(1)

    @pl.when(step == 0)
    def _():
        total_ref[...] = jnp.zeros_like(total_ref)

    member = match(row_ref[0], PLANE)
    width = Z * OWN
    for e in range(C):
        table = match(column_ref[0, e : e + 1, :], width)
        span = slice(e * width, (e + 1) * width)
        total_ref[:, span] += lax.dot_general(
            member, table, NT, preferred_element_type=jnp.float32
        )

    @pl.when(step == pl.num_programs(1) - 1)
    def _():
        out_ref[0] = total_ref[...].astype(out_ref.dtype)


def pair_counts(row_index, column_index):
    books, _, slots = row_index.shape
    columns = C * Z * OWN
    return pl.pallas_call(
        pair_kernel,
        grid=(books, slots // CHUNK),
        in_specs=[
            pl.BlockSpec((1, 1, CHUNK), lambda i, s: (i, 0, s)),
            pl.BlockSpec((1, C, CHUNK), lambda i, s: (i, 0, s)),
        ],
        out_specs=pl.BlockSpec((1, PLANE, columns), lambda i, s: (i, 0, 0)),
        out_shape=jax.ShapeDtypeStruct((books, PLANE, columns), jnp.bfloat16),
        scratch_shapes=[pltpu.VMEM((PLANE, columns), jnp.float32)],
        name="pair_counts",
    )(row_index, column_index)


def gram_kernel(book_ref, start_ref, row_ref, codes_ref, out_ref):
    group = pl.program_id(0)
    member = match(row_ref[...], OWN)
    per_step = out_ref.shape[1] // BLK
    for j in range(per_step):
        p = group * per_step + j
        offset = codes_ref[pl.ds(book_ref[p], 1), :] - start_ref[p]
        out_ref[:, j * BLK : (j + 1) * BLK] = lax.dot_general(
            member, match(offset, BLK), NT, preferred_element_type=jnp.float32
        )


def gram_counts(partner_book, partner_start, row_index, tuples):
    slots = tuples.shape[1]
    width = 8 * BLK
    return pl.pallas_call(
        gram_kernel,
        grid_spec=pltpu.PrefetchScalarGridSpec(
            num_scalar_prefetch=2,
            grid=(P_SIZE * BLK // width,),
            in_specs=[
                pl.BlockSpec((1, slots), lambda g, b, s: (0, 0)),
                pl.BlockSpec(tuples.shape, lambda g, b, s: (0, 0)),
            ],
            out_specs=pl.BlockSpec((OWN, width), lambda g, b, s: (0, g)),
        ),
        out_shape=jax.ShapeDtypeStruct((OWN, P_SIZE * BLK), jnp.float32),
        name="gram_counts",
    )(partner_book, partner_start, row_index, tuples)


def by_parity(rows, core):
    shape = rows.shape
    grouped = rows.reshape(shape[:-2] + (X, C, shape[-1]))
    return lax.dynamic_index_in_dim(grouped, core, len(shape) - 1, keepdims=False)


def slot_indices(tuples, z, y, x, core):
    sign = 1 - 2 * core
    own = jnp.stack(
        [lax.dynamic_index_in_dim(tuples[i], i * C + core, 0, keepdims=True) for i in range(X)]
    )
    row_index = jnp.where(own >= 0, own - PLANE * z, -1)
    columns = []
    for e in range(C):
        book = x * C + (core + e) % C
        code = lax.dynamic_index_in_dim(tuples, book, 1, keepdims=False)
        place = ((code // PLANE - z) * sign) % Z * OWN + code % OWN
        inside = (code >= 0) & (code // OWN % Y == y)
        columns.append(jnp.where(inside, place, -1))
    return row_index, jnp.stack(columns, axis=1)


def vector_rows(by_z, z, x, core):
    codes = by_z.reshape(2, 2, 2, 2, X * C, -1).transpose(3, 2, 1, 0, 4, 5)
    codes = by_z_order(codes)
    portion = lax.dynamic_slice_in_dim(codes, 2 * HALF * x, 2 * HALF, 2)
    portion = by_parity(portion, core).reshape(Z, X, C, HALF)
    plus = portion.transpose(1, 2, 0, 3)
    minus = jnp.concatenate([portion[:1], portion[:0:-1]]).transpose(1, 2, 0, 3)[:, ::-1]
    chosen = jnp.where(core == 0, plus, minus).reshape(X, 1, C * Z * HALF)
    return chosen - PLANE * z


def by_z_order(codes):
    return codes.reshape(Z, X * C, codes.shape[-1])


def shards(vectors, codes, codebook, pairs):
    z, y = lax.axis_index("z"), lax.axis_index("y")
    x, core = lax.axis_index("x"), lax.axis_index("core")
    features = codebook.shape[2]
    owner = z * Y + y
    book = x * C + core
    mine = lax.dynamic_slice_in_dim(vectors, 2 * HALF * x + HALF * core, HALF, 0)
    by_z, all_codes = gather_codes(codes)
    rows, spread = gather_rows(jnp.concatenate([codebook[0], mine]))
    local = by_parity(all_codes, core) - PLANE * z
    tuples = compact(all_codes, local)
    tuples = tuples.reshape(X, tuples.shape[1], -1)
    row_index, column_index = slot_indices(tuples, z, y, x, core)
    counts = pair_counts(row_index, column_index).reshape(X * PLANE, -1)
    ids = jnp.arange(PLANE, dtype=jnp.int32)[None, :, None]
    assigned = (vector_rows(by_z, z, x, core) == ids).astype(jnp.bfloat16)
    assigned = assigned.reshape(X * PLANE, -1)
    partial = lax.dot_general(assigned, spread, NN, preferred_element_type=jnp.float32)
    partial -= lax.dot_general(counts, rows, NN, preferred_element_type=jnp.float32)
    sent = partial.astype(jnp.bfloat16).reshape(X * Y, OWN, features)
    received = lax.all_to_all(sent, ("x", "y"), split_axis=0, concat_axis=0, tiled=True)
    right_side = jnp.sum(received.astype(jnp.float32), axis=0)
    held = lax.dynamic_index_in_dim(tuples, x, 0, keepdims=False)
    held = held.reshape(X * C, -1, Y, CAP)
    held = lax.dynamic_index_in_dim(held, y, 2, keepdims=False).reshape(X * C, -1)
    own_row = lax.dynamic_index_in_dim(held, book, 0, keepdims=True)
    own_row = jnp.where(own_row >= 0, own_row - owner * OWN, -1)
    partner = lax.dynamic_index_in_dim(pairs, (book * K + owner * OWN) // BLK, 0, keepdims=False)
    gram = gram_counts(partner // KB, partner % KB * BLK, own_row, held)
    matched = own_row == jnp.arange(OWN, dtype=jnp.int32)[:, None]
    code_count = jnp.sum(matched.astype(jnp.float32), axis=1)
    current = codebook[0].astype(jnp.float32)
    updated = current + (right_side - 2.0 * current) / (code_count[:, None] + 2.0)
    return updated[None], gram[None]


def solution(mesh):
    grid = Mesh(mesh.devices.reshape(Z, Y, X, C), ("z", "y", "x", "core"))
    rows, books = ("z", "y"), ("x", "core")
    in_specs = (P(rows, None), P(None, rows), P(books, rows, None), P())
    out_specs = (P(books, rows, None), P(books, rows, None))
    return jax.shard_map(shards, mesh=grid, in_specs=in_specs, out_specs=out_specs, check_vma=False)
```

time: 259 us -> 238 us (0.919)
  waiting for transfers between devices: 148 us -> 50.8 us
  starting transfers between devices: 26.4 us -> 89.2 us
  blocking collectives: 33.1 us -> 0 us
  local copies, waits for them, and re-layouts: 17.1 us -> 41.4 us
  Pallas kernels: 0 us -> 22.1 us
  between operations: 14.4 us -> 1.47 us
  other arithmetic: 7.29 us -> 17.5 us
    ppermute x0 -> x17, starting transfers between devices: none -> 81.8 us  [the longest x9 50.3 us: pull(): lax.ppermute(value, axis, [((i + step) % size, i) for i in range(size)])]
    all_to_all x3 -> x1, waiting for transfers between devices: 90.5 us -> 17.5 us  [shards(): lax.all_to_all(sent, ('x', 'y'), split_axis=0, concat_axis=0, tiled=True)]
    psum x1 -> x0, waiting for transfers between devices: 57.7 us -> none  [shards(): lax.psum(partial_sum.astype(jnp.bfloat16), 'codes').astype(jnp.float32)]
    ppermute x0 -> x17, waiting for transfers between devices: none -> 33.3 us  [the longest x8 27.2 us: ring_pull(): return lax.ppermute(value, ('z', 'core'), pairs)]
    unnamed x9 -> x93, local copies, waits for them, and re-layouts: 0.14 us -> 33.4 us
    all_to_all x1 -> x0, blocking collectives: 33.1 us -> none  [shards(): lax.all_to_all(slot_request, 'ingest', split_axis=0, concat_axis=0, tiled...]
    pallas_call x0 -> x2, Pallas kernels: none -> 22.1 us  [the longest x1 15.3 us: pair_counts(): pl.pallas_call(pair_kernel, grid=(books, slots // CHUNK), in_specs=[pl.Bl...]
    all_to_all x3 -> x1, starting transfers between devices: 26.3 us -> 7.47 us  [shards(): lax.all_to_all(sent, ('x', 'y'), split_axis=0, concat_axis=0, tiled=True)]
  transfers between devices with their start and end apart: 4 -> 18, of which waited for: 3 -> 12; matrix products, arithmetic and copies ran while one was open for 10% -> 19% of each run, Pallas kernels for 0% -> 9%
where the time goes in v2:
time: 238 us; the launch traced here: 235 us
  starting transfers between devices  89.2 us (37%)
  waiting for transfers between devices  50.8 us (21%)
  local copies, waits for them, and re-layouts  41.4 us (17%)
  Pallas kernels  22.1 us (9%)
  other arithmetic  17.5 us (7%)
  matrix products  12.9 us (5%)
    ppermute x9, starting transfers between devices, pull(): lax.ppermute(value, axis, [((i + step) % size, i) for i in range(size)])  50.3 us
    unnamed x93, local copies, waits for them, and re-layouts  33.4 us
    ppermute x8, starting transfers between devices, ring_pull(): return lax.ppermute(value, ('z', 'core'), pairs)  31.4 us
    ppermute x8, waiting for transfers between devices, ring_pull(): return lax.ppermute(value, ('z', 'core'), pairs)  27.2 us
    all_to_all x1, waiting for transfers between devices, shards(): lax.all_to_all(sent, ('x', 'y'), split_axis=0, concat_axis=0, tiled=True)  17.5 us
    pallas_call x1, Pallas kernels, pair_counts(): pl.pallas_call(pair_kernel, grid=(books, slots // CHUNK), in_specs=[pl.Bl...  15.3 us
    all_to_all x1, starting transfers between devices, shards(): lax.all_to_all(sent, ('x', 'y'), split_axis=0, concat_axis=0, tiled=True)  7.47 us
    pallas_call x1, Pallas kernels, gram_counts(): pl.pallas_call(gram_kernel, grid_spec=pltpu.PrefetchScalarGridSpec(num_sc...  6.81 us
  transfers between devices with their start and end apart: 18, of which 12 were waited for; matrix products, arithmetic and copies ran while one was open for 19% of the time, Pallas kernels for 9%

profile of v2, /device:TPU:6, one launch (start us, length us, event | category | flops | bytes accessed | tf_op | source)
XLA Modules:
  0.0 235.4 jit_solution(15298095714957756415)
XLA Ops:
  0.7 1.5 constant_dynamic-update-slice_fusion.36
  2.2 0.9 fusion.31
  3.1 1.9 collective-permute-start.4
  5.0 15.7 %collective-permute-start = (s32[1,8,256]{2,1,0:T(8,128)}, s32[1,8,256]{2,1,0:T(8,128)S(1)}, u32[]{:S(2)}, u32[]{:S(2)}) collective-permute-start(s32[1,8,256]{2,1,0:T(8,128)} %bitcast.336), channel_id=1, source_target_pairs={{256,0},{288,32},{320,64},{352,96},{384,128},{416,160},{448,192},{... | collective-permute-start | bytes 24584 | tf_op jit(solution)/shard_map/ppermute | solution.py:27
  20.8 1.6 constant_dynamic-update-slice_fusion.88
  22.3 1.3 constant_dynamic-update-slice_fusion.56
  23.6 0.7 concatenate.83
  25.3 0.7 pad_add_fusion.4
  26.0 7.0 %collective-permute-start.1 = (s32[2,8,256]{2,1,0:T(8,128)S(1)}, s32[2,8,256]{2,1,0:T(8,128)S(1)}, u32[]{:S(2)}, u32[]{:S(2)}) collective-permute-start(s32[2,8,256]{2,1,0:T(8,128)S(1)} %pad_add_fusion.4), channel_id=1, source_target_pairs={{128,0},{160,32},{192,64},{224,96},{256,128},{288,160},{320,192},{... | collective-permute-start | bytes 49160 | tf_op jit(solution)/shard_map/ppermute | solution.py:27
  34.2 1.4 collective-permute-done.1
  36.3 6.0 %collective-permute-start.2 = (s32[4,8,256]{2,1,0:T(8,128)S(1)}, s32[4,8,256]{2,1,0:T(8,128)S(1)}, u32[]{:S(2)}, u32[]{:S(2)}) collective-permute-start(s32[4,8,256]{2,1,0:T(8,128)S(1)} %pad_add_fusion.2), channel_id=1, source_target_pairs={{64,0},{96,32},{128,64},{160,96},{192,128},{224,160},{256,192},{28... | collective-permute-start | bytes 98312 | tf_op jit(solution)/shard_map/ppermute | solution.py:27
  44.6 5.9 %collective-permute-start.3 = (s32[8,8,256]{2,1,0:T(8,128)S(1)}, s32[8,8,256]{2,1,0:T(8,128)S(1)}, u32[]{:S(2)}, u32[]{:S(2)}) collective-permute-start(s32[8,8,256]{2,1,0:T(8,128)S(1)} %pad_add_fusion), channel_id=1, source_target_pairs={{32,0},{64,32},{96,64},{128,96},{160,128},{192,160},{224,192},{256... | collective-permute-start | bytes 196616 | tf_op jit(solution)/shard_map/ppermute | solution.py:27
  53.0 5.1 %collective-permute-start.15 = (s32[16,8,256]{2,1,0:T(8,128)S(1)}, s32[16,8,256]{2,1,0:T(8,128)S(1)}, u32[]{:S(2)}, u32[]{:S(2)}) collective-permute-start(s32[16,8,256]{2,1,0:T(8,128)S(1)} %get-tuple-element.18), channel_id=1, source_target_pairs={{16,0},{24,8},{0,16},{8,24},{17,1},{25,9},{1,17},{9,25},{18,2},{26... | collective-permute-start | bytes 393224 | tf_op jit(solution)/shard_map/ppermute | solution.py:27
  58.7 2.6 %collective-permute-done.15 = s32[16,8,256]{2,1,0:T(8,128)S(1)} collective-permute-done((s32[16,8,256]{2,1,0:T(8,128)S(1)}, s32[16,8,256]{2,1,0:T(8,128)S(1)}, u32[]{:S(2)}, u32[]{:S(2)}) %collective-permute-start.15) | collective-permute-done | bytes 131104 | tf_op jit(solution)/shard_map/ppermute | solution.py:27
  62.0 4.9 %collective-permute-start.16 = (s32[32,8,256]{2,1,0:T(8,128)}, s32[32,8,256]{2,1,0:T(8,128)S(1)}, u32[]{:S(2)}, u32[]{:S(2)}) collective-permute-start(s32[32,8,256]{2,1,0:T(8,128)} %get-tuple-element.15), channel_id=1, source_target_pairs={{8,0},{16,8},{24,16},{0,24},{9,1},{17,9},{25,17},{1,25},{10,2},{18... | collective-permute-start | bytes 786440 | tf_op jit(solution)/shard_map/ppermute | solution.py:27
  67.7 1.7 bitcast_compare_fusion.2
  69.4 5.7 %collective-permute-start.5 = (bf16[2,96,1024]{2,1,0:T(8,128)(2,1)S(1)}, bf16[2,96,1024]{2,1,0:T(8,128)(2,1)S(1)}, u32[]{:S(2)}, u32[]{:S(2)}) collective-permute-start(bf16[2,96,1024]{2,1,0:T(8,128)(2,1)S(1)} %pad_maximum_fusion.2), channel_id=1, source_target_pairs={{32,0},{481,1},{64,32},{1,33},{96,64},{33,65},{128,96},{65,97},{16... | collective-permute-start | bytes 1179656 | tf_op jit(solution)/shard_map/ppermute | solution.py:35
  75.3 1.3 fusion.6
  76.8 1.4 and_select_fusion
  78.2 4.5 %convert_reduce_fusion.1 = s32[64,4,4]{2,1,0:T(4,128)S(1)} fusion(s32[64,4,256]{2,1,0:T(4,128)S(1)} %bitcast.321), kind=kLoop, calls=%fused_computation.12 | loop fusion | flops 785408 | bytes 266240 | tf_op jit(solution)/shard_map/reduce_sum | solution.py:88
  84.1 2.5 %fusion.4 = s32[64,16,128]{2,1,0:T(8,128)S(1)} fusion(s32[128]{0:T(128)S(1)} %lt.140, s32[64,16,256]{2,1,0:T(8,128)S(1)} %fusion.3, bf16[64,8,256]{2,1,0:T(8,128)(2,1)} %get-tuple-element.9, bf16[64,8,256]{2,1,0:T(8,128)(2,1)} %get-tuple-element.8), kind=kOutput, calls=%fused_computation.11 | convolution fusion | flops 70385664 | bytes 2097664 | tf_op jit(solution)/shard_map/dot_general | solution.py:85
  88.9 1.9 collective-permute-start.6
  90.9 1.2 and_select_fusion.10
  92.1 6.5 %collective-permute-done.6 = bf16[2,96,1024]{2,1,0:T(8,128)(2,1)S(1)} collective-permute-done((bf16[2,96,1024]{2,1,0:T(8,128)(2,1)S(1)}, bf16[2,96,1024]{2,1,0:T(8,128)(2,1)S(1)}, u32[]{:S(2)}, u32[]{:S(2)}) %collective-permute-start.6) | collective-permute-done | bytes 393248 | tf_op jit(solution)/shard_map/ppermute | solution.py:35
  98.6 3.3 %collective-permute-start.7 = (bf16[2,96,1024]{2,1,0:T(8,128)(2,1)S(1)}, bf16[2,96,1024]{2,1,0:T(8,128)(2,1)S(1)}, u32[]{:S(2)}, u32[]{:S(2)}) collective-permute-start(bf16[2,96,1024]{2,1,0:T(8,128)(2,1)S(1)} %collective-permute-done.6), channel_id=1, source_target_pairs={{32,0},{481,1},{64,32},{1,33},{96,64},{33,65},{128,96},{65,97},{16... | collective-permute-start | bytes 1179656 | tf_op jit(solution)/shard_map/ppermute | solution.py:35
  103.2 15.3 %pair_counts.1 = bf16[4,256,2048]{2,1,0:T(8,128)(2,1)} custom-call(s32[4,1,2048]{2,1,0:T(1,128)} %compare_select_fusion.11.row_ref, s32[4,2,2048]{2,1,0:T(2,128)} %pad_add_fusion.1.column_ref), custom_call_target="tpu_custom_call" | custom-call | tf_op jit(solution)/shard_map/pair_counts/pallas_call | solution.py:124
  118.5 1.9 collective-permute-start.8
  121.7 6.4 %collective-permute-done.8 = bf16[2,96,1024]{2,1,0:T(8,128)(2,1)S(1)} collective-permute-done((bf16[2,96,1024]{2,1,0:T(8,128)(2,1)S(1)}, bf16[2,96,1024]{2,1,0:T(8,128)(2,1)S(1)}, u32[]{:S(2)}, u32[]{:S(2)}) %collective-permute-start.8) | collective-permute-done | bytes 393248 | tf_op jit(solution)/shard_map/ppermute | solution.py:35
  128.2 3.1 %collective-permute-start.9 = (bf16[2,96,1024]{2,1,0:T(8,128)(2,1)S(1)}, bf16[2,96,1024]{2,1,0:T(8,128)(2,1)S(1)}, u32[]{:S(2)}, u32[]{:S(2)}) collective-permute-start(bf16[2,96,1024]{2,1,0:T(8,128)(2,1)S(1)} %collective-permute-done.8), channel_id=1, source_target_pairs={{32,0},{481,1},{64,32},{1,33},{96,64},{33,65},{128,96},{65,97},{16... | collective-permute-start | bytes 1179656 | tf_op jit(solution)/shard_map/ppermute | solution.py:35
  132.6 5.2 %collective-permute-done.9 = bf16[2,96,1024]{2,1,0:T(8,128)(2,1)S(1)} collective-permute-done((bf16[2,96,1024]{2,1,0:T(8,128)(2,1)S(1)}, bf16[2,96,1024]{2,1,0:T(8,128)(2,1)S(1)}, u32[]{:S(2)}, u32[]{:S(2)}) %collective-permute-start.9) | collective-permute-done | bytes 393248 | tf_op jit(solution)/shard_map/ppermute | solution.py:35
  137.8 4.3 %collective-permute-start.10 = (bf16[2,96,1024]{2,1,0:T(8,128)(2,1)S(1)}, bf16[2,96,1024]{2,1,0:T(8,128)(2,1)S(1)}, u32[]{:S(2)}, u32[]{:S(2)}) collective-permute-start(bf16[2,96,1024]{2,1,0:T(8,128)(2,1)S(1)} %collective-permute-done.9), channel_id=1, source_target_pairs={{32,0},{481,1},{64,32},{1,33},{96,64},{33,65},{128,96},{65,97},{16... | collective-permute-start | bytes 1179656 | tf_op jit(solution)/shard_map/ppermute | solution.py:35
  143.7 1.9 collective-permute-start.14
  145.6 1.9 collective-permute-done.10
  147.5 5.5 %collective-permute-start.11 = (bf16[2,96,1024]{2,1,0:T(8,128)(2,1)S(1)}, bf16[2,96,1024]{2,1,0:T(8,128)(2,1)S(1)}, u32[]{:S(2)}, u32[]{:S(2)}) collective-permute-start(bf16[2,96,1024]{2,1,0:T(8,128)(2,1)S(1)} %collective-permute-done.10), channel_id=1, source_target_pairs={{32,0},{481,1},{64,32},{1,33},{96,64},{33,65},{128,96},{65,97},{16... | collective-permute-start | bytes 1179656 | tf_op jit(solution)/shard_map/ppermute | solution.py:35
  153.7 4.6 %collective-permute-done.11 = bf16[2,96,1024]{2,1,0:T(8,128)(2,1)S(1)} collective-permute-done((bf16[2,96,1024]{2,1,0:T(8,128)(2,1)S(1)}, bf16[2,96,1024]{2,1,0:T(8,128)(2,1)S(1)}, u32[]{:S(2)}, u32[]{:S(2)}) %collective-permute-start.11) | collective-permute-done | bytes 393248 | tf_op jit(solution)/shard_map/ppermute | solution.py:35
  158.3 5.6 %collective-permute-start.12 = (bf16[96,1024]{1,0:T(8,128)(2,1)S(1)}, bf16[96,1024]{1,0:T(8,128)(2,1)S(1)}, u32[]{:S(2)}, u32[]{:S(2)}) collective-permute-start(bf16[96,1024]{1,0:T(8,128)(2,1)S(1)} %slice_bitcast_fusion), channel_id=1, source_target_pairs={{32,0},{481,1},{64,32},{1,33},{96,64},{33,65},{128,96},{65,97},{16... | collective-permute-start | bytes 589832 | tf_op jit(solution)/shard_map/ppermute | solution.py:35
  164.6 2.5 %collective-permute-done.12 = bf16[96,1024]{1,0:T(8,128)(2,1)S(1)} collective-permute-done((bf16[96,1024]{1,0:T(8,128)(2,1)S(1)}, bf16[96,1024]{1,0:T(8,128)(2,1)S(1)}, u32[]{:S(2)}, u32[]{:S(2)}) %collective-permute-start.12) | collective-permute-done | bytes 196640 | tf_op jit(solution)/shard_map/ppermute | solution.py:35
  167.3 1.9 collective-permute-start.13
  171.3 1.1 collective-permute-done.13
  187.4 6.3 %fusion.33 = f32[1024,1024]{1,0:T(8,128)S(1)} fusion(bf16[1024,2048]{1,0:T(8,128)(2,1)S(1)} %bitcast.320, bf16[2048,1024]{1,0:T(8,128)(2,1)} %constant_dynamic-update-slice_fusion.57), kind=kOutput, calls=%fused_computation.269 | convolution fusion | flops 4294967296 | bytes 12582912 | tf_op jit(solution)/shard_map/dot_general | solution.py:224
  194.1 0.9 copy-done.3
  195.0 3.7 %subtract_convert_fusion = bf16[1024,1024]{1,0:T(8,128)(2,1)} fusion(f32[1024,1024]{1,0:T(8,128)S(1)} %fusion.33, pred[1024,1024]{1,0:T(32,128)(4,1)S(1)} %copy-done.3, bf16[1024,1024]{1,0:T(8,128)(2,1)S(1)} %constant_dynamic-update-slice_fusion.5), kind=kOutput, calls=%fused_computation.4 | convolution fusion | flops 2149580800 | bytes 9437184 | tf_op jit(solution)/shard_map/dot_general | solution.py:223
  198.7 7.5 %all-to-all-start = ((bf16[16,64,1024]{2,1,0:T(8,128)(2,1)}), bf16[16,64,1024]{2,1,0:T(8,128)(2,1)S(1)}, u32[]{:S(2)}, u32[]{:S(2)}) async-start(bf16[16,64,1024]{2,1,0:T(8,128)(2,1)} %bitcast.323), calls=%async_computation | async-start | bytes 4194304 | tf_op jit(solution)/shard_map/all_to_all | solution.py:226
  207.0 1.2 reshape.342
  208.2 0.8 dynamic-slice_reduce_fusion
  209.8 6.8 %gram_counts.1 = f32[64,8192]{1,0:T(8,128)} custom-call(s32[64]{0:T(128)} %get-tuple-element.32.book_ref, s32[64]{0:T(128)} %get-tuple-element.31.start_ref, s32[1,512]{1,0:T(1,128)} %compare_select_fusion.12.row_ref, s32[8,512]{1,0:T(8,128)} %copy-done.5), custom_call_target="tpu_custom_call" | custom-call | tf_op jit(solution)/shard_map/gram_counts/pallas_call | solution.py:153
  216.7 17.5 %all-to-all-done = bf16[16,64,1024]{2,1,0:T(8,128)(2,1)S(1)} async-done(((bf16[16,64,1024]{2,1,0:T(8,128)(2,1)}), bf16[16,64,1024]{2,1,0:T(8,128)(2,1)S(1)}, u32[]{:S(2)}, u32[]{:S(2)}) %all-to-all-start) | async-done | bytes 2097184 | tf_op jit(solution)/shard_map/all_to_all | solution.py:226
  234.6 0.8 convert_add_fusion
  (164 shorter events, 39.9 us)
Async XLA Ops:
  0.6 205.5 %copy-start = (s32[256,64]{0,1:T(8,128)S(1)}, s32[256,64]{0,1:T(8,128)}, u32[]{:S(2)}) copy-start(s32[256,64]{0,1:T(8,128)} %param.7) | copy-start | bytes 196612
  3.1 66.3 %collective-permute-start.4 = (bf16[96,1024]{1,0:T(8,128)(2,1)S(1)}, bf16[96,1024]{1,0:T(8,128)(2,1)S(1)}, u32[]{:S(2)}, u32[]{:S(2)}) collective-permute-start(bf16[96,1024]{1,0:T(8,128)(2,1)S(1)} %get-tuple-element.13), channel_id=1, source_target_pairs={{1,0},{0,1},{3,2},{2,3},{5,4},{4,5},{7,6},{6,7},{9,8},{8,9},{11,10... | collective-permute-start | bytes 589832 | tf_op jit(solution)/shard_map/ppermute | solution.py:27
  5.0 20.2 %collective-permute-start = (s32[1,8,256]{2,1,0:T(8,128)}, s32[1,8,256]{2,1,0:T(8,128)S(1)}, u32[]{:S(2)}, u32[]{:S(2)}) collective-permute-start(s32[1,8,256]{2,1,0:T(8,128)} %bitcast.336), channel_id=1, source_target_pairs={{256,0},{288,32},{320,64},{352,96},{384,128},{416,160},{448,192},{... | collective-permute-start | bytes 24584 | tf_op jit(solution)/shard_map/ppermute | solution.py:27
  26.0 9.6 %collective-permute-start.1 = (s32[2,8,256]{2,1,0:T(8,128)S(1)}, s32[2,8,256]{2,1,0:T(8,128)S(1)}, u32[]{:S(2)}, u32[]{:S(2)}) collective-permute-start(s32[2,8,256]{2,1,0:T(8,128)S(1)} %pad_add_fusion.4), channel_id=1, source_target_pairs={{128,0},{160,32},{192,64},{224,96},{256,128},{288,160},{320,192},{... | collective-permute-start | bytes 49160 | tf_op jit(solution)/shard_map/ppermute | solution.py:27
  36.3 7.6 %collective-permute-start.2 = (s32[4,8,256]{2,1,0:T(8,128)S(1)}, s32[4,8,256]{2,1,0:T(8,128)S(1)}, u32[]{:S(2)}, u32[]{:S(2)}) collective-permute-start(s32[4,8,256]{2,1,0:T(8,128)S(1)} %pad_add_fusion.2), channel_id=1, source_target_pairs={{64,0},{96,32},{128,64},{160,96},{192,128},{224,160},{256,192},{28... | collective-permute-start | bytes 98312 | tf_op jit(solution)/shard_map/ppermute | solution.py:27
  44.6 7.8 %collective-permute-start.3 = (s32[8,8,256]{2,1,0:T(8,128)S(1)}, s32[8,8,256]{2,1,0:T(8,128)S(1)}, u32[]{:S(2)}, u32[]{:S(2)}) collective-permute-start(s32[8,8,256]{2,1,0:T(8,128)S(1)} %pad_add_fusion), channel_id=1, source_target_pairs={{32,0},{64,32},{96,64},{128,96},{160,128},{192,160},{224,192},{256... | collective-permute-start | bytes 196616 | tf_op jit(solution)/shard_map/ppermute | solution.py:27
  53.0 8.4 %collective-permute-start.15 = (s32[16,8,256]{2,1,0:T(8,128)S(1)}, s32[16,8,256]{2,1,0:T(8,128)S(1)}, u32[]{:S(2)}, u32[]{:S(2)}) collective-permute-start(s32[16,8,256]{2,1,0:T(8,128)S(1)} %get-tuple-element.18), channel_id=1, source_target_pairs={{16,0},{24,8},{0,16},{8,24},{17,1},{25,9},{1,17},{9,25},{18,2},{26... | collective-permute-start | bytes 393224 | tf_op jit(solution)/shard_map/ppermute | solution.py:27
  62.0 13.2 %collective-permute-start.16 = (s32[32,8,256]{2,1,0:T(8,128)}, s32[32,8,256]{2,1,0:T(8,128)S(1)}, u32[]{:S(2)}, u32[]{:S(2)}) collective-permute-start(s32[32,8,256]{2,1,0:T(8,128)} %get-tuple-element.15), channel_id=1, source_target_pairs={{8,0},{16,8},{24,16},{0,24},{9,1},{17,9},{25,17},{1,25},{10,2},{18... | collective-permute-start | bytes 786440 | tf_op jit(solution)/shard_map/ppermute | solution.py:27
  67.6 7.7 %copy-start.4 = (s32[64,4,2,256]{3,2,1,0:T(2,128)S(1)}, s32[64,4,2,256]{3,2,1,0:T(2,128)}, u32[]{:S(2)}) copy-start(s32[64,4,2,256]{3,2,1,0:T(2,128)} %constant_dynamic-update-slice_fusion.45) | copy-start | bytes 1572868
  69.4 19.5 %collective-permute-start.5 = (bf16[2,96,1024]{2,1,0:T(8,128)(2,1)S(1)}, bf16[2,96,1024]{2,1,0:T(8,128)(2,1)S(1)}, u32[]{:S(2)}, u32[]{:S(2)}) collective-permute-start(bf16[2,96,1024]{2,1,0:T(8,128)(2,1)S(1)} %pad_maximum_fusion.2), channel_id=1, source_target_pairs={{32,0},{481,1},{64,32},{1,33},{96,64},{33,65},{128,96},{65,97},{16... | collective-permute-start | bytes 1179656 | tf_op jit(solution)/shard_map/ppermute | solution.py:35
  88.9 9.7 %collective-permute-start.6 = (bf16[2,96,1024]{2,1,0:T(8,128)(2,1)S(1)}, bf16[2,96,1024]{2,1,0:T(8,128)(2,1)S(1)}, u32[]{:S(2)}, u32[]{:S(2)}) collective-permute-start(bf16[2,96,1024]{2,1,0:T(8,128)(2,1)S(1)} %collective-permute-done.5), channel_id=1, source_target_pairs={{32,0},{481,1},{64,32},{1,33},{96,64},{33,65},{128,96},{65,97},{16... | collective-permute-start | bytes 1179656 | tf_op jit(solution)/shard_map/ppermute | solution.py:35
  98.6 19.9 %collective-permute-start.7 = (bf16[2,96,1024]{2,1,0:T(8,128)(2,1)S(1)}, bf16[2,96,1024]{2,1,0:T(8,128)(2,1)S(1)}, u32[]{:S(2)}, u32[]{:S(2)}) collective-permute-start(bf16[2,96,1024]{2,1,0:T(8,128)(2,1)S(1)} %collective-permute-done.6), channel_id=1, source_target_pairs={{32,0},{481,1},{64,32},{1,33},{96,64},{33,65},{128,96},{65,97},{16... | collective-permute-start | bytes 1179656 | tf_op jit(solution)/shard_map/ppermute | solution.py:35
  118.5 9.7 %collective-permute-start.8 = (bf16[2,96,1024]{2,1,0:T(8,128)(2,1)S(1)}, bf16[2,96,1024]{2,1,0:T(8,128)(2,1)S(1)}, u32[]{:S(2)}, u32[]{:S(2)}) collective-permute-start(bf16[2,96,1024]{2,1,0:T(8,128)(2,1)S(1)} %collective-permute-done.7), channel_id=1, source_target_pairs={{32,0},{481,1},{64,32},{1,33},{96,64},{33,65},{128,96},{65,97},{16... | collective-permute-start | bytes 1179656 | tf_op jit(solution)/shard_map/ppermute | solution.py:35
  128.2 9.7 %collective-permute-start.9 = (bf16[2,96,1024]{2,1,0:T(8,128)(2,1)S(1)}, bf16[2,96,1024]{2,1,0:T(8,128)(2,1)S(1)}, u32[]{:S(2)}, u32[]{:S(2)}) collective-permute-start(bf16[2,96,1024]{2,1,0:T(8,128)(2,1)S(1)} %collective-permute-done.8), channel_id=1, source_target_pairs={{32,0},{481,1},{64,32},{1,33},{96,64},{33,65},{128,96},{65,97},{16... | collective-permute-start | bytes 1179656 | tf_op jit(solution)/shard_map/ppermute | solution.py:35
  137.8 9.7 %collective-permute-start.10 = (bf16[2,96,1024]{2,1,0:T(8,128)(2,1)S(1)}, bf16[2,96,1024]{2,1,0:T(8,128)(2,1)S(1)}, u32[]{:S(2)}, u32[]{:S(2)}) collective-permute-start(bf16[2,96,1024]{2,1,0:T(8,128)(2,1)S(1)} %collective-permute-done.9), channel_id=1, source_target_pairs={{32,0},{481,1},{64,32},{1,33},{96,64},{33,65},{128,96},{65,97},{16... | collective-permute-start | bytes 1179656 | tf_op jit(solution)/shard_map/ppermute | solution.py:35
  142.8 10.2 %copy-start.7 = (bf16[1024,1024]{1,0:T(8,128)(2,1)S(1)}, bf16[1024,1024]{1,0:T(8,128)(2,1)}, u32[]{:S(2)}) copy-start(bf16[1024,1024]{1,0:T(8,128)(2,1)} %constant_dynamic-update-slice_fusion.33) | copy-start | bytes 6291460
  143.7 30.6 %collective-permute-start.14 = (bf16[4,2,96,1024]{3,2,1,0:T(8,128)(2,1)S(1)}, bf16[4,2,96,1024]{3,2,1,0:T(8,128)(2,1)S(1)}, u32[]{:S(2)}, u32[]{:S(2)}) collective-permute-start(bf16[4,2,96,1024]{3,2,1,0:T(8,128)(2,1)S(1)} %pad_maximum_fusion), channel_id=1, source_target_pairs={{1,0},{0,1},{3,2},{2,3},{5,4},{4,5},{7,6},{6,7},{9,8},{8,9},{11,10... | collective-permute-start | bytes 4718600 | tf_op jit(solution)/shard_map/ppermute | solution.py:27
  147.5 10.8 %collective-permute-start.11 = (bf16[2,96,1024]{2,1,0:T(8,128)(2,1)S(1)}, bf16[2,96,1024]{2,1,0:T(8,128)(2,1)S(1)}, u32[]{:S(2)}, u32[]{:S(2)}) collective-permute-start(bf16[2,96,1024]{2,1,0:T(8,128)(2,1)S(1)} %collective-permute-done.10), channel_id=1, source_target_pairs={{32,0},{481,1},{64,32},{1,33},{96,64},{33,65},{128,96},{65,97},{16... | collective-permute-start | bytes 1179656 | tf_op jit(solution)/shard_map/ppermute | solution.py:35
  158.3 8.8 %collective-permute-start.12 = (bf16[96,1024]{1,0:T(8,128)(2,1)S(1)}, bf16[96,1024]{1,0:T(8,128)(2,1)S(1)}, u32[]{:S(2)}, u32[]{:S(2)}) collective-permute-start(bf16[96,1024]{1,0:T(8,128)(2,1)S(1)} %slice_bitcast_fusion), channel_id=1, source_target_pairs={{32,0},{481,1},{64,32},{1,33},{96,64},{33,65},{128,96},{65,97},{16... | collective-permute-start | bytes 589832 | tf_op jit(solution)/shard_map/ppermute | solution.py:35
  167.3 5.0 %collective-permute-start.13 = (bf16[7,96,1024]{2,1,0:T(8,128)(2,1)S(1)}, bf16[7,96,1024]{2,1,0:T(8,128)(2,1)S(1)}, u32[]{:S(2)}, u32[]{:S(2)}) collective-permute-start(bf16[7,96,1024]{2,1,0:T(8,128)(2,1)S(1)} %pad_maximum_fusion.1), channel_id=1, source_target_pairs={{1,0},{0,1},{3,2},{2,3},{5,4},{4,5},{7,6},{6,7},{9,8},{8,9},{11,10... | collective-permute-start | bytes 4128776 | tf_op jit(solution)/shard_map/ppermute | solution.py:27
  176.9 10.5 %copy-start.1 = (bf16[4,256,2048]{2,1,0:T(8,128)(2,1)S(1)}, bf16[4,256,2048]{2,1,0:T(8,128)(2,1)}, u32[]{:S(2)}) copy-start(bf16[4,256,2048]{2,1,0:T(8,128)(2,1)} %pair_counts.1) | copy-start | bytes 12582916
  193.7 1.2 copy-start.3
  198.7 35.5 %all-to-all-start = ((bf16[16,64,1024]{2,1,0:T(8,128)(2,1)}), bf16[16,64,1024]{2,1,0:T(8,128)(2,1)S(1)}, u32[]{:S(2)}, u32[]{:S(2)}) async-start(bf16[16,64,1024]{2,1,0:T(8,128)(2,1)} %bitcast.323), calls=%async_computation | async-start | bytes 4194304 | tf_op jit(solution)/shard_map/all_to_all | solution.py:226
  209.2 0.6 copy-start.5
  209.8 6.8 %copy-start.6 = (s32[1,512]{1,0:T(1,128)S(1)}, s32[1,512]{1,0:T(1,128)}, u32[]{:S(2)}) copy-start(s32[1,512]{1,0:T(1,128)} %compare_select_fusion.12.row_ref) | copy-start | bytes 6148
  209.8 24.8 %copy-start.2 = (bf16[1,64,1024]{2,1,0:T(8,128)(2,1)S(1)}, bf16[1,64,1024]{2,1,0:T(8,128)(2,1)}, u32[]{:S(2)}) copy-start(bf16[1,64,1024]{2,1,0:T(8,128)(2,1)} %param.6) | copy-start | bytes 393220

commit v3 on v2

--- a/solution.py
+++ b/solution.py
@@ -1,5 +1,3 @@
-import functools
-
 import jax
 import jax.numpy as jnp
 from jax import lax
@@ -36,32 +34,32 @@
 
 
 def gather_codes(codes):
-    held = codes[None]
-    for step in (8, 4, 2, 1):
-        held = jnp.concatenate([held, pull(held, "z", step)])
-    by_z = held
-    for step in (2, 1):
-        held = jnp.concatenate([held, pull(held, "y", step)])
-    return by_z, held
+    copies = jnp.broadcast_to(codes.astype(jnp.int16)[None], (Z * Y,) + codes.shape)
+    return lax.all_to_all(copies, ("z", "y"), split_axis=0, concat_axis=0, tiled=True)
 
 
 def gather_rows(piece):
-    start = jnp.stack([piece, pull(piece, "core", 1)])
-    chain = [start]
+    chain = [jnp.stack([piece, pull(piece, "core", 1)])]
     for _ in range(7):
         chain.append(ring_pull(chain[-1]))
     last = ring_pull(chain[7][0])
     early = pull(jnp.stack(chain[1:5]), "core", 1)
     late = pull(jnp.concatenate(chain[5:8] + [last[None]]), "core", 1)
-    other = [None] + [early[i] for i in range(4)] + [late[2 * i : 2 * i + 2] for i in range(3)]
-    ends = (last, late[6])
-    order = []
-    for e in range(2):
-        order += [chain[t][e] for t in range(8)] + [ends[e]]
-        order += [other[16 - t][1 - e] for t in range(9, 16)]
-    book = jnp.concatenate([unit[:OWN] for unit in order])
-    vectors = jnp.concatenate([unit[OWN:] for unit in order])
-    return book, vectors
+    return chain, last, early, late
+
+
+def unit_places():
+    places = []
+    for e in range(C):
+        places += [(t, (e,)) for t in range(8)]
+        places.append((8, ()) if e == 0 else (10, (6,)))
+        for t in range(9, 16):
+            back = 16 - t
+            if back < 5:
+                places.append((9, (back - 1, 1 - e)))
+            else:
+                places.append((10, (2 * (back - 5) + 1 - e,)))
+    return places
 
 
 def compact(all_codes, local):
@@ -81,13 +79,14 @@
     slots = jnp.arange(CAP, dtype=jnp.int32)
     chosen = (rank[:, :, None, :] == slots[None, None, :, None]).astype(jnp.bfloat16)
     chosen = chosen.reshape(blocks, X * Y * CAP, length)
-    digits = jnp.concatenate([all_codes // BLK, all_codes % BLK], axis=1).astype(jnp.bfloat16)
+    ones = jnp.ones_like(all_codes[:, :1])
+    digits = jnp.concatenate([all_codes // BLK, all_codes % BLK, ones], axis=1)
+    digits = digits.astype(jnp.bfloat16)
     packed = lax.dot_general(
         digits, chosen, (((2,), (2,)), ((0,), (0,))), preferred_element_type=jnp.float32
     ).astype(jnp.int32)
-    filled = slots < jnp.sum(hit.astype(jnp.int32), axis=2)[:, :, None]
-    filled = filled.reshape(blocks, 1, X * Y * CAP)
-    tuples = jnp.where(filled, packed[:, :codebooks] * BLK + packed[:, codebooks:], -1)
+    high, low = packed[:, :codebooks], packed[:, codebooks : 2 * codebooks]
+    tuples = jnp.where(packed[:, 2 * codebooks :] > 0, high * BLK + low, -1)
     tuples = tuples.reshape(blocks, codebooks, X, Y * CAP)
     return tuples.transpose(2, 1, 0, 3)
 
@@ -98,41 +97,99 @@
 
 
 def pair_kernel(row_ref, column_ref, out_ref, total_ref):
-    step = pl.program_id(1)
+    step = pl.program_id(0)
 
     @pl.when(step == 0)
     def _():
         total_ref[...] = jnp.zeros_like(total_ref)
 
-    member = match(row_ref[0], PLANE)
+    member = match(row_ref[...], PLANE)
     width = Z * OWN
     for e in range(C):
-        table = match(column_ref[0, e : e + 1, :], width)
+        table = match(column_ref[e : e + 1, :], width)
         span = slice(e * width, (e + 1) * width)
         total_ref[:, span] += lax.dot_general(
             member, table, NT, preferred_element_type=jnp.float32
         )
 
-    @pl.when(step == pl.num_programs(1) - 1)
+    @pl.when(step == pl.num_programs(0) - 1)
     def _():
-        out_ref[0] = total_ref[...].astype(out_ref.dtype)
+        out_ref[...] = total_ref[...].astype(out_ref.dtype)
 
 
 def pair_counts(row_index, column_index):
-    books, _, slots = row_index.shape
+    slots = row_index.shape[1]
     columns = C * Z * OWN
     return pl.pallas_call(
         pair_kernel,
-        grid=(books, slots // CHUNK),
+        grid=(slots // CHUNK,),
         in_specs=[
-            pl.BlockSpec((1, 1, CHUNK), lambda i, s: (i, 0, s)),
-            pl.BlockSpec((1, C, CHUNK), lambda i, s: (i, 0, s)),
+            pl.BlockSpec((1, CHUNK), lambda s: (0, s)),
+            pl.BlockSpec((C, CHUNK), lambda s: (0, s)),
         ],
-        out_specs=pl.BlockSpec((1, PLANE, columns), lambda i, s: (i, 0, 0)),
-        out_shape=jax.ShapeDtypeStruct((books, PLANE, columns), jnp.bfloat16),
+        out_specs=pl.BlockSpec((PLANE, columns), lambda s: (0, 0)),
+        out_shape=jax.ShapeDtypeStruct((PLANE, columns), jnp.bfloat16),
         scratch_shapes=[pltpu.VMEM((PLANE, columns), jnp.float32)],
+        cost_estimate=pl.CostEstimate(
+            flops=2 * PLANE * columns * slots, transcendentals=0, bytes_accessed=1 << 20
+        ),
         name="pair_counts",
     )(row_index, column_index)
+
+
+def merge_kernel(*refs):
+    pieces, refs = refs[:11], refs[11:]
+    assigned_ref, *count_refs = refs[: 1 + X]
+    out_ref, book_ref, vector_ref, sems = refs[1 + X :]
+    copies = []
+    for unit, (source, where) in enumerate(unit_places()):
+        piece = pieces[source].at[where] if where else pieces[source]
+        copies.append(
+            pltpu.make_async_copy(
+                piece.at[pl.ds(0, OWN)],
+                book_ref.at[pl.ds(unit * OWN, OWN)],
+                sems.at[2 * unit],
+            )
+        )
+        copies.append(
+            pltpu.make_async_copy(
+                piece.at[pl.ds(OWN, HALF)],
+                vector_ref.at[pl.ds(unit * HALF, HALF)],
+                sems.at[2 * unit + 1],
+            )
+        )
+    for copy in copies:
+        copy.start()
+    for copy in copies:
+        copy.wait()
+    for i in range(X):
+        span = slice(i * PLANE, (i + 1) * PLANE)
+        total = lax.dot_general(
+            assigned_ref[span, :], vector_ref[...], NN, preferred_element_type=jnp.float32
+        )
+        total -= lax.dot_general(
+            count_refs[i][...], book_ref[...], NN, preferred_element_type=jnp.float32
+        )
+        out_ref[span, :] = total.astype(out_ref.dtype)
+
+
+def merge(chain, last, early, late, assigned, counts):
+    pieces = chain + [last, early, late]
+    features = last.shape[1]
+    units = C * Z
+    return pl.pallas_call(
+        merge_kernel,
+        in_specs=[pl.BlockSpec(memory_space=pl.ANY)] * len(pieces)
+        + [pl.BlockSpec(memory_space=pltpu.VMEM)] * (1 + X),
+        out_specs=pl.BlockSpec(memory_space=pltpu.VMEM),
+        out_shape=jax.ShapeDtypeStruct((X * PLANE, features), jnp.bfloat16),
+        scratch_shapes=[
+            pltpu.VMEM((units * OWN, features), jnp.bfloat16),
+            pltpu.VMEM((units * HALF, features), jnp.bfloat16),
+            pltpu.SemaphoreType.DMA((2 * units,)),
+        ],
+        name="merge",
+    )(*pieces, assigned, *counts)
 
 
 def gram_kernel(book_ref, start_ref, row_ref, codes_ref, out_ref):
@@ -188,19 +245,18 @@
     return row_index, jnp.stack(columns, axis=1)
 
 
-def vector_rows(by_z, z, x, core):
-    codes = by_z.reshape(2, 2, 2, 2, X * C, -1).transpose(3, 2, 1, 0, 4, 5)
-    codes = by_z_order(codes)
-    portion = lax.dynamic_slice_in_dim(codes, 2 * HALF * x, 2 * HALF, 2)
+def vector_rows(all_codes, z, y, x, core):
+    mine = all_codes.reshape(Z, Y, X * C, -1)
+    mine = lax.dynamic_index_in_dim(mine, y, 1, keepdims=False)
+    portion = lax.dynamic_slice_in_dim(mine, 2 * HALF * x, 2 * HALF, 2)
     portion = by_parity(portion, core).reshape(Z, X, C, HALF)
-    plus = portion.transpose(1, 2, 0, 3)
-    minus = jnp.concatenate([portion[:1], portion[:0:-1]]).transpose(1, 2, 0, 3)[:, ::-1]
+    plus = lax.dynamic_slice_in_dim(jnp.concatenate([portion, portion]), z, Z, 0)
+    back = portion[::-1]
+    minus = lax.dynamic_slice_in_dim(jnp.concatenate([back, back]), Z - 1 - z, Z, 0)
+    plus = plus.transpose(1, 2, 0, 3)
+    minus = minus.transpose(1, 2, 0, 3)[:, ::-1]
     chosen = jnp.where(core == 0, plus, minus).reshape(X, 1, C * Z * HALF)
     return chosen - PLANE * z
-
-
-def by_z_order(codes):
-    return codes.reshape(Z, X * C, codes.shape[-1])
 
 
 def shards(vectors, codes, codebook, pairs):
@@ -210,19 +266,17 @@
     owner = z * Y + y
     book = x * C + core
     mine = lax.dynamic_slice_in_dim(vectors, 2 * HALF * x + HALF * core, HALF, 0)
-    by_z, all_codes = gather_codes(codes)
-    rows, spread = gather_rows(jnp.concatenate([codebook[0], mine]))
+    pieces = gather_rows(jnp.concatenate([codebook[0], mine]))
+    all_codes = gather_codes(codes).astype(jnp.int32)
     local = by_parity(all_codes, core) - PLANE * z
     tuples = compact(all_codes, local)
     tuples = tuples.reshape(X, tuples.shape[1], -1)
     row_index, column_index = slot_indices(tuples, z, y, x, core)
-    counts = pair_counts(row_index, column_index).reshape(X * PLANE, -1)
+    counts = [pair_counts(row_index[i], column_index[i]) for i in range(X)]
     ids = jnp.arange(PLANE, dtype=jnp.int32)[None, :, None]
-    assigned = (vector_rows(by_z, z, x, core) == ids).astype(jnp.bfloat16)
-    assigned = assigned.reshape(X * PLANE, -1)
-    partial = lax.dot_general(assigned, spread, NN, preferred_element_type=jnp.float32)
-    partial -= lax.dot_general(counts, rows, NN, preferred_element_type=jnp.float32)
-    sent = partial.astype(jnp.bfloat16).reshape(X * Y, OWN, features)
+    assigned = (vector_rows(all_codes, z, y, x, core) == ids).astype(jnp.bfloat16)
+    partial = merge(*pieces, assigned.reshape(X * PLANE, -1), counts)
+    sent = partial.reshape(X * Y, OWN, features)
     received = lax.all_to_all(sent, ("x", "y"), split_axis=0, concat_axis=0, tiled=True)
     right_side = jnp.sum(received.astype(jnp.float32), axis=0)
     held = lax.dynamic_index_in_dim(tuples, x, 0, keepdims=False)

time: 238 us -> 198 us (0.83)
  local copies, waits for them, and re-layouts: 41.4 us -> 18.2 us
  Pallas kernels: 22.1 us -> 41 us
  starting transfers between devices: 89.2 us -> 73.3 us
  matrix products: 12.9 us -> 1.95 us
  waiting for transfers between devices: 50.8 us -> 45.3 us
  other arithmetic: 17.5 us -> 14.5 us
    ppermute x9 -> x3, starting transfers between devices: 50.3 us -> 6.4 us  [pull(): lax.ppermute(value, axis, [((i + step) % size, i) for i in range(size)])]
    unnamed x93 -> x39, local copies, waits for them, and re-layouts: 33.4 us -> 3.53 us
    pallas_call x1 -> x5, Pallas kernels: 15.3 us -> 34.3 us  [the longest x4 20.1 us: pair_counts(): pl.pallas_call(pair_kernel, grid=(slots // CHUNK,), in_specs=[pl.BlockSpe...]
    all_to_all x0 -> x1, starting transfers between devices: none -> 18.7 us  [gather_codes(): lax.all_to_all(copies, ('z', 'y'), split_axis=0, concat_axis=0, tiled=True)]
    dot_general x2 -> x0, matrix products: 10 us -> none  [the longest x1 6.3 us: shards(): lax.dot_general(counts, rows, NN, preferred_element_type=jnp.float32)]
    ppermute x8, starting transfers between devices: 31.4 us -> 40.8 us  [ring_pull(): return lax.ppermute(value, ('z', 'core'), pairs)]
    ppermute x9 -> x3, waiting for transfers between devices: 6.11 us -> 0.01 us  [pull(): lax.ppermute(value, axis, [((i + step) % size, i) for i in range(size)])]
    reduce_sum x1 -> x0, other arithmetic: 4.5 us -> none  [compact(): filled = slots < jnp.sum(hit.astype(jnp.int32), axis=2)[:, :, None]]
  transfers between devices with their start and end apart: 18 -> 13, of which waited for: 12 -> 6; matrix products, arithmetic and copies ran while one was open for 19% -> 16% of each run, Pallas kernels for 9% -> 14%
where the time goes in v3:
time: 198 us; the launch traced here: 196 us
  starting transfers between devices  73.3 us (37%)
  waiting for transfers between devices  45.3 us (23%)
  Pallas kernels  41 us (21%)
  local copies, waits for them, and re-layouts  18.2 us (9%)
  other arithmetic  14.5 us (7%)
    ppermute x8, starting transfers between devices, ring_pull(): return lax.ppermute(value, ('z', 'core'), pairs)  40.8 us
    ppermute x8, waiting for transfers between devices, ring_pull(): return lax.ppermute(value, ('z', 'core'), pairs)  31 us
    pallas_call x4, Pallas kernels, pair_counts(): pl.pallas_call(pair_kernel, grid=(slots // CHUNK,), in_specs=[pl.BlockSpe...  20.1 us
    all_to_all x1, starting transfers between devices, gather_codes(): lax.all_to_all(copies, ('z', 'y'), split_axis=0, concat_axis=0, tiled=True)  18.7 us
    all_to_all x1, waiting for transfers between devices, shards(): lax.all_to_all(sent, ('x', 'y'), split_axis=0, concat_axis=0, tiled=True)  14.4 us
    pallas_call x1, Pallas kernels, merge(): pl.pallas_call(merge_kernel, in_specs=[pl.BlockSpec(memory_space=pl.ANY)]...  14.2 us
    all_to_all x1, starting transfers between devices, shards(): lax.all_to_all(sent, ('x', 'y'), split_axis=0, concat_axis=0, tiled=True)  7.3 us
    pallas_call x1, Pallas kernels, gram_counts(): pl.pallas_call(gram_kernel, grid_spec=pltpu.PrefetchScalarGridSpec(num_sc...  6.68 us
  transfers between devices with their start and end apart: 13, of which 6 were waited for; matrix products, arithmetic and copies ran while one was open for 16% of the time, Pallas kernels for 14%

profile of v3, /device:TPU:6, one launch (start us, length us, event | category | flops | bytes accessed | tf_op | source)
XLA Modules:
  0.0 195.5 jit_solution(16962902457508334717)
XLA Ops:
  0.7 1.0 copy-done
  1.7 0.9 fusion.45
  2.6 1.9 collective-permute-start
  4.6 0.7 convert_element_type.31
  5.3 0.7 broadcast_in_dim.55
  6.0 18.7 %all-to-all-start = ((s16[64,8,256]{2,1,0:T(8,128)(2,1)}), s16[64,8,256]{2,1,0:T(8,128)(2,1)S(1)}, u32[]{:S(2)}, u32[]{:S(2)}) async-start(s16[64,8,256]{2,1,0:T(8,128)(2,1)} %broadcast_in_dim.55), calls=%async_computation | async-start | bytes 524288 | tf_op jit(solution)/shard_map/all_to_all | solution.py:38
  24.8 5.0 %collective-permute-start.1 = (bf16[2,96,1024]{2,1,0:T(8,128)(2,1)S(1)}, bf16[2,96,1024]{2,1,0:T(8,128)(2,1)S(1)}, u32[]{:S(2)}, u32[]{:S(2)}) collective-permute-start(bf16[2,96,1024]{2,1,0:T(8,128)(2,1)S(1)} %pad_maximum_fusion.2.refs_0_), channel_id=1, source_target_pairs={{32,0},{481,1},{64,32},{1,33},{96,64},{33,65},{128,96},{65,97},{16... | collective-permute-start | bytes 1179656 | tf_op jit(solution)/shard_map/ppermute | solution.py:33
  29.8 12.6 %collective-permute-done.1.refs_1_ = bf16[2,96,1024]{2,1,0:T(8,128)(2,1)S(1)} collective-permute-done((bf16[2,96,1024]{2,1,0:T(8,128)(2,1)S(1)}, bf16[2,96,1024]{2,1,0:T(8,128)(2,1)S(1)}, u32[]{:S(2)}, u32[]{:S(2)}) %collective-permute-start.1) | collective-permute-done | bytes 393248 | tf_op jit(solution)/shard_map/ppermute | solution.py:33
  42.4 3.7 %collective-permute-start.2 = (bf16[2,96,1024]{2,1,0:T(8,128)(2,1)S(1)}, bf16[2,96,1024]{2,1,0:T(8,128)(2,1)}, u32[]{:S(2)}, u32[]{:S(2)}) collective-permute-start(bf16[2,96,1024]{2,1,0:T(8,128)(2,1)S(1)} %collective-permute-done.1.refs_1_), channel_id=1, source_target_pairs={{32,0},{481,1},{64,32},{1,33},{96,64},{33,65},{128,96},{65,97},{16... | collective-permute-start | bytes 1179656 | tf_op jit(solution)/shard_map/ppermute | solution.py:33
  47.1 5.0 %collective-permute-done.2.refs_2_ = bf16[2,96,1024]{2,1,0:T(8,128)(2,1)} collective-permute-done((bf16[2,96,1024]{2,1,0:T(8,128)(2,1)S(1)}, bf16[2,96,1024]{2,1,0:T(8,128)(2,1)}, u32[]{:S(2)}, u32[]{:S(2)}) %collective-permute-start.2) | collective-permute-done | bytes 393248 | tf_op jit(solution)/shard_map/ppermute | solution.py:33
  52.1 4.9 %collective-permute-start.3 = (bf16[2,96,1024]{2,1,0:T(8,128)(2,1)}, bf16[2,96,1024]{2,1,0:T(8,128)(2,1)}, u32[]{:S(2)}, u32[]{:S(2)}) collective-permute-start(bf16[2,96,1024]{2,1,0:T(8,128)(2,1)} %collective-permute-done.2.refs_2_), channel_id=1, source_target_pairs={{32,0},{481,1},{64,32},{1,33},{96,64},{33,65},{128,96},{65,97},{16... | collective-permute-start | bytes 1179656 | tf_op jit(solution)/shard_map/ppermute | solution.py:33
  57.6 0.6 copy.45
  58.2 1.4 and_select_fusion
  61.3 1.6 fusion.5
  62.8 5.4 %collective-permute-start.4 = (bf16[2,96,1024]{2,1,0:T(8,128)(2,1)}, bf16[2,96,1024]{2,1,0:T(8,128)(2,1)S(1)}, u32[]{:S(2)}, u32[]{:S(2)}) collective-permute-start(bf16[2,96,1024]{2,1,0:T(8,128)(2,1)} %collective-permute-done.3.refs_3_), channel_id=1, source_target_pairs={{32,0},{481,1},{64,32},{1,33},{96,64},{33,65},{128,96},{65,97},{16... | collective-permute-start | bytes 1179656 | tf_op jit(solution)/shard_map/ppermute | solution.py:33
  69.0 4.9 %collective-permute-done.4.refs_4_ = bf16[2,96,1024]{2,1,0:T(8,128)(2,1)S(1)} collective-permute-done((bf16[2,96,1024]{2,1,0:T(8,128)(2,1)}, bf16[2,96,1024]{2,1,0:T(8,128)(2,1)S(1)}, u32[]{:S(2)}, u32[]{:S(2)}) %collective-permute-start.4) | collective-permute-done | bytes 393248 | tf_op jit(solution)/shard_map/ppermute | solution.py:33
  73.9 5.5 %collective-permute-start.5 = (bf16[2,96,1024]{2,1,0:T(8,128)(2,1)S(1)}, bf16[2,96,1024]{2,1,0:T(8,128)(2,1)S(1)}, u32[]{:S(2)}, u32[]{:S(2)}) collective-permute-start(bf16[2,96,1024]{2,1,0:T(8,128)(2,1)S(1)} %collective-permute-done.4.refs_4_), channel_id=1, source_target_pairs={{32,0},{481,1},{64,32},{1,33},{96,64},{33,65},{128,96},{65,97},{16... | collective-permute-start | bytes 1179656 | tf_op jit(solution)/shard_map/ppermute | solution.py:33
  79.3 0.7 fusion.46
  80.1 1.0 copy.38
  81.3 1.0 copy.41
  82.6 0.8 squeeze.64
  84.1 0.9 dynamic-slice_bitcast_fusion
  85.1 5.1 %collective-permute-start.6 = (bf16[2,96,1024]{2,1,0:T(8,128)(2,1)S(1)}, bf16[2,96,1024]{2,1,0:T(8,128)(2,1)S(1)}, u32[]{:S(2)}, u32[]{:S(2)}) collective-permute-start(bf16[2,96,1024]{2,1,0:T(8,128)(2,1)S(1)} %collective-permute-done.5.refs_5_), channel_id=1, source_target_pairs={{32,0},{481,1},{64,32},{1,33},{96,64},{33,65},{128,96},{65,97},{16... | collective-permute-start | bytes 1179656 | tf_op jit(solution)/shard_map/ppermute | solution.py:33
  90.2 1.2 and_select_fusion.10
  91.4 4.0 %collective-permute-done.6.refs_6_ = bf16[2,96,1024]{2,1,0:T(8,128)(2,1)S(1)} collective-permute-done((bf16[2,96,1024]{2,1,0:T(8,128)(2,1)S(1)}, bf16[2,96,1024]{2,1,0:T(8,128)(2,1)S(1)}, u32[]{:S(2)}, u32[]{:S(2)}) %collective-permute-start.6) | collective-permute-done | bytes 393248 | tf_op jit(solution)/shard_map/ppermute | solution.py:33
  95.5 5.6 %collective-permute-start.7 = (bf16[2,96,1024]{2,1,0:T(8,128)(2,1)S(1)}, bf16[2,96,1024]{2,1,0:T(8,128)(2,1)S(1)}, u32[]{:S(2)}, u32[]{:S(2)}) collective-permute-start(bf16[2,96,1024]{2,1,0:T(8,128)(2,1)S(1)} %collective-permute-done.6.refs_6_), channel_id=1, source_target_pairs={{32,0},{481,1},{64,32},{1,33},{96,64},{33,65},{128,96},{65,97},{16... | collective-permute-start | bytes 1179656 | tf_op jit(solution)/shard_map/ppermute | solution.py:33
  101.3 0.7 fusion.39
  102.0 4.4 %collective-permute-done.7.refs_7_ = bf16[2,96,1024]{2,1,0:T(8,128)(2,1)S(1)} collective-permute-done((bf16[2,96,1024]{2,1,0:T(8,128)(2,1)S(1)}, bf16[2,96,1024]{2,1,0:T(8,128)(2,1)S(1)}, u32[]{:S(2)}, u32[]{:S(2)}) %collective-permute-start.7) | collective-permute-done | bytes 393248 | tf_op jit(solution)/shard_map/ppermute | solution.py:33
  106.4 5.6 %collective-permute-start.8 = (bf16[96,1024]{1,0:T(8,128)(2,1)S(1)}, bf16[96,1024]{1,0:T(8,128)(2,1)S(1)}, u32[]{:S(2)}, u32[]{:S(2)}) collective-permute-start(bf16[96,1024]{1,0:T(8,128)(2,1)S(1)} %slice_bitcast_fusion), channel_id=1, source_target_pairs={{32,0},{481,1},{64,32},{1,33},{96,64},{33,65},{128,96},{65,97},{16... | collective-permute-start | bytes 589832 | tf_op jit(solution)/shard_map/ppermute | solution.py:33
  112.1 2.4 %fusion.3.refs_11_ = bf16[1024,1024]{1,0:T(8,128)(2,1)} fusion(s32[1024]{0:T(1024)} %bitcast.107, s32[4,1024]{1,0:T(4,128)S(1)} %sub.106), kind=kLoop, calls=%fused_computation.6 | loop fusion | flops 2097152 | bytes 2117632 | tf_op jit(solution)/shard_map/convert_element_type | solution.py:277
  114.6 2.6 %pad_maximum_fusion = bf16[4,2,96,1024]{3,2,1,0:T(8,128)(2,1)} fusion(bf16[1,2,96,1024]{3,2,1,0:T(8,128)(2,1)S(1)} %bitcast.98, bf16[1,2,96,1024]{3,2,1,0:T(8,128)(2,1)} %bitcast.6, bf16[1,2,96,1024]{3,2,1,0:T(8,128)(2,1)} %bitcast.5, bf16[1,2,96,1024]{3,2,1,0:T(8,128)(2,1)S(1)} %bitcast.97), kind=kLoop, calls=%fused_computation.7 | loop fusion | flops 2359296 | bytes 3145728 | tf_op jit(solution)/shard_map/stack | solution.py:46
  117.2 1.9 collective-permute-start.9
  119.1 1.3 pad_maximum_fusion.1
  120.4 2.6 %collective-permute-start.10 = (bf16[7,96,1024]{2,1,0:T(8,128)(2,1)}, bf16[7,96,1024]{2,1,0:T(8,128)(2,1)}, u32[]{:S(2)}, u32[]{:S(2)}) collective-permute-start(bf16[7,96,1024]{2,1,0:T(8,128)(2,1)} %pad_maximum_fusion.1), channel_id=1, source_target_pairs={{1,0},{0,1},{3,2},{2,3},{5,4},{4,5},{7,6},{6,7},{9,8},{8,9},{11,10... | collective-permute-start | bytes 4128776 | tf_op jit(solution)/shard_map/ppermute | solution.py:25
  123.1 0.6 slice_bitcast_fusion.1
  123.7 5.0 %pair_counts.7.refs_15_ = bf16[256,2048]{1,0:T(8,128)(2,1)} custom-call(s32[1,2048]{1,0:T(1,128)} %get-tuple-element.16.row_ref, s32[2,2048]{1,0:T(2,128)} %get-tuple-element.12.column_ref), custom_call_target="tpu_custom_call" | custom-call | flops 2147483648 | bytes 1048576 | tf_op jit(solution)/shard_map/pair_counts/pallas_call | solution.py:123
  128.7 5.1 %pair_counts.4.refs_12_ = bf16[256,2048]{1,0:T(8,128)(2,1)} custom-call(s32[1,2048]{1,0:T(1,128)} %get-tuple-element.19.row_ref, s32[2,2048]{1,0:T(2,128)} %get-tuple-element.13.column_ref), custom_call_target="tpu_custom_call" | custom-call | flops 2147483648 | bytes 1048576 | tf_op jit(solution)/shard_map/pair_counts/pallas_call | solution.py:123
  133.8 5.1 %pair_counts.5.refs_13_ = bf16[256,2048]{1,0:T(8,128)(2,1)} custom-call(s32[1,2048]{1,0:T(1,128)} %get-tuple-element.18.row_ref, s32[2,2048]{1,0:T(2,128)} %get-tuple-element.14.column_ref), custom_call_target="tpu_custom_call" | custom-call | flops 2147483648 | bytes 1048576 | tf_op jit(solution)/shard_map/pair_counts/pallas_call | solution.py:123
  138.8 5.0 %pair_counts.6.refs_14_ = bf16[256,2048]{1,0:T(8,128)(2,1)} custom-call(s32[1,2048]{1,0:T(1,128)} %get-tuple-element.17.row_ref, s32[2,2048]{1,0:T(2,128)} %get-tuple-element.15.column_ref), custom_call_target="tpu_custom_call" | custom-call | flops 2147483648 | bytes 1048576 | tf_op jit(solution)/shard_map/pair_counts/pallas_call | solution.py:123
  143.8 1.1 copy-done.2
  145.0 14.2 %merge.1 = bf16[1024,1024]{1,0:T(8,128)(2,1)} custom-call(bf16[2,96,1024]{2,1,0:T(8,128)(2,1)} %copy-done.5, bf16[2,96,1024]{2,1,0:T(8,128)(2,1)} %copy-done.3, bf16[2,96,1024]{2,1,0:T(8,128)(2,1)} %collective-permute-done.2.refs_2_, bf16[2,96,1024]{2,1,0:T(8,128)(2,1)} %collective-permute-done.3.refs_3_, bf16[2,96,1024]{2,1,0:T(8,128)(2,1)} %copy-done.4, ...), custom_call_target="tpu_custom_call" | custom-call | tf_op jit(solution)/shard_map/merge/pallas_call | solution.py:180
  159.2 7.3 %all-to-all-start.1 = ((bf16[16,64,1024]{2,1,0:T(8,128)(2,1)}), bf16[16,64,1024]{2,1,0:T(8,128)(2,1)S(1)}, u32[]{:S(2)}, u32[]{:S(2)}) async-start(bf16[16,64,1024]{2,1,0:T(8,128)(2,1)} %bitcast.92), calls=%async_computation.1 | async-start | bytes 4194304 | tf_op jit(solution)/shard_map/all_to_all | solution.py:280
  167.3 0.8 constant_dynamic-slice_fusion.1
  168.1 2.2 %reshape.236 = s32[8,64,4,8]{3,2,1,0:T(4,128)} reshape(s32[1,8,2048]{2,1,0:T(8,128)S(1)} %constant_dynamic-slice_fusion.1) | data formatting | bytes 131072 | tf_op jit(solution)/shard_map/reshape | solution.py:283
  170.4 2.0 %dynamic-slice_reduce_fusion = s32[8,64,8]{2,1,0:T(8,128)S(1)} fusion(s32[8,64,4,8]{3,2,1,0:T(4,128)} %reshape.236, s32[]{:T(128)S(6)} %select_n.196), kind=kLoop, calls=%fused_computation.42 | loop fusion | bytes 32772 | tf_op jit(solution)/shard_map/jit(dynamic_index_in_dim)/dynamic_slice | solution.py:284
  173.2 6.7 %gram_counts.1 = f32[64,8192]{1,0:T(8,128)} custom-call(s32[64]{0:T(128)} %get-tuple-element.21.book_ref, s32[64]{0:T(128)} %get-tuple-element.20.start_ref, s32[1,512]{1,0:T(1,128)} %compare_select_fusion.12.row_ref, s32[8,512]{1,0:T(8,128)} %copy-done.14), custom_call_target="tpu_custom_call" | custom-call | tf_op jit(solution)/shard_map/gram_counts/pallas_call | solution.py:210
  180.0 14.4 %all-to-all-done.1 = bf16[16,64,1024]{2,1,0:T(8,128)(2,1)S(1)} async-done(((bf16[16,64,1024]{2,1,0:T(8,128)(2,1)}), bf16[16,64,1024]{2,1,0:T(8,128)(2,1)S(1)}, u32[]{:S(2)}, u32[]{:S(2)}) %all-to-all-start.1) | async-done | bytes 2097184 | tf_op jit(solution)/shard_map/all_to_all | solution.py:280
  194.7 0.8 convert_add_fusion
  (86 shorter events, 7.5 us)
Async XLA Ops:
  0.6 1.0 copy-start
  2.6 22.1 %collective-permute-start = (bf16[96,1024]{1,0:T(8,128)(2,1)S(1)}, bf16[96,1024]{1,0:T(8,128)(2,1)S(1)}, u32[]{:S(2)}, u32[]{:S(2)}) collective-permute-start(bf16[96,1024]{1,0:T(8,128)(2,1)S(1)} %get-tuple-element.11), channel_id=1, source_target_pairs={{1,0},{0,1},{3,2},{2,3},{5,4},{4,5},{7,6},{6,7},{9,8},{8,9},{11,10... | collective-permute-start | bytes 589832 | tf_op jit(solution)/shard_map/ppermute | solution.py:25
  6.0 51.1 %all-to-all-start = ((s16[64,8,256]{2,1,0:T(8,128)(2,1)}), s16[64,8,256]{2,1,0:T(8,128)(2,1)S(1)}, u32[]{:S(2)}, u32[]{:S(2)}) async-start(s16[64,8,256]{2,1,0:T(8,128)(2,1)} %broadcast_in_dim.55), calls=%async_computation | async-start | bytes 524288 | tf_op jit(solution)/shard_map/all_to_all | solution.py:38
  24.8 32.3 %copy-start.5 = (bf16[2,96,1024]{2,1,0:T(8,128)(2,1)}, bf16[2,96,1024]{2,1,0:T(8,128)(2,1)S(1)}, u32[]{:S(2)}) copy-start(bf16[2,96,1024]{2,1,0:T(8,128)(2,1)S(1)} %pad_maximum_fusion.2.refs_0_) | copy-start | bytes 1179652
  24.8 17.6 %collective-permute-start.1 = (bf16[2,96,1024]{2,1,0:T(8,128)(2,1)S(1)}, bf16[2,96,1024]{2,1,0:T(8,128)(2,1)S(1)}, u32[]{:S(2)}, u32[]{:S(2)}) collective-permute-start(bf16[2,96,1024]{2,1,0:T(8,128)(2,1)S(1)} %pad_maximum_fusion.2.refs_0_), channel_id=1, source_target_pairs={{32,0},{481,1},{64,32},{1,33},{96,64},{33,65},{128,96},{65,97},{16... | collective-permute-start | bytes 1179656 | tf_op jit(solution)/shard_map/ppermute | solution.py:33
  42.4 72.2 %copy-start.3 = (bf16[2,96,1024]{2,1,0:T(8,128)(2,1)}, bf16[2,96,1024]{2,1,0:T(8,128)(2,1)S(1)}, u32[]{:S(2)}) copy-start(bf16[2,96,1024]{2,1,0:T(8,128)(2,1)S(1)} %collective-permute-done.1.refs_1_) | copy-start | bytes 1179652
  42.4 9.8 %collective-permute-start.2 = (bf16[2,96,1024]{2,1,0:T(8,128)(2,1)S(1)}, bf16[2,96,1024]{2,1,0:T(8,128)(2,1)}, u32[]{:S(2)}, u32[]{:S(2)}) collective-permute-start(bf16[2,96,1024]{2,1,0:T(8,128)(2,1)S(1)} %collective-permute-done.1.refs_1_), channel_id=1, source_target_pairs={{32,0},{481,1},{64,32},{1,33},{96,64},{33,65},{128,96},{65,97},{16... | collective-permute-start | bytes 1179656 | tf_op jit(solution)/shard_map/ppermute | solution.py:33
  52.1 10.7 %collective-permute-start.3 = (bf16[2,96,1024]{2,1,0:T(8,128)(2,1)}, bf16[2,96,1024]{2,1,0:T(8,128)(2,1)}, u32[]{:S(2)}, u32[]{:S(2)}) collective-permute-start(bf16[2,96,1024]{2,1,0:T(8,128)(2,1)} %collective-permute-done.2.refs_2_), channel_id=1, source_target_pairs={{32,0},{481,1},{64,32},{1,33},{96,64},{33,65},{128,96},{65,97},{16... | collective-permute-start | bytes 1179656 | tf_op jit(solution)/shard_map/ppermute | solution.py:33
  62.8 11.0 %collective-permute-start.4 = (bf16[2,96,1024]{2,1,0:T(8,128)(2,1)}, bf16[2,96,1024]{2,1,0:T(8,128)(2,1)S(1)}, u32[]{:S(2)}, u32[]{:S(2)}) collective-permute-start(bf16[2,96,1024]{2,1,0:T(8,128)(2,1)} %collective-permute-done.3.refs_3_), channel_id=1, source_target_pairs={{32,0},{481,1},{64,32},{1,33},{96,64},{33,65},{128,96},{65,97},{16... | collective-permute-start | bytes 1179656 | tf_op jit(solution)/shard_map/ppermute | solution.py:33
  73.8 40.7 %copy-start.4 = (bf16[2,96,1024]{2,1,0:T(8,128)(2,1)}, bf16[2,96,1024]{2,1,0:T(8,128)(2,1)S(1)}, u32[]{:S(2)}) copy-start(bf16[2,96,1024]{2,1,0:T(8,128)(2,1)S(1)} %collective-permute-done.4.refs_4_) | copy-start | bytes 1179652
  73.9 11.2 %collective-permute-start.5 = (bf16[2,96,1024]{2,1,0:T(8,128)(2,1)S(1)}, bf16[2,96,1024]{2,1,0:T(8,128)(2,1)S(1)}, u32[]{:S(2)}, u32[]{:S(2)}) collective-permute-start(bf16[2,96,1024]{2,1,0:T(8,128)(2,1)S(1)} %collective-permute-done.4.refs_4_), channel_id=1, source_target_pairs={{32,0},{481,1},{64,32},{1,33},{96,64},{33,65},{128,96},{65,97},{16... | collective-permute-start | bytes 1179656 | tf_op jit(solution)/shard_map/ppermute | solution.py:33
  82.3 18.8 %copy-start.13 = (s32[16,1,8,64]{3,0,2,1:T(8,128)S(1)}, s32[16,1,8,64]{3,0,2,1:T(8,128)}, u32[]{:S(2)}) copy-start(s32[16,1,8,64]{3,0,2,1:T(8,128)} %copy.45) | copy-start | bytes 98308
  84.1 30.4 %copy-start.11 = (s32[4,8,2048]{2,1,0:T(8,128)}, s32[4,8,2048]{2,1,0:T(8,128)S(1)}, u32[]{:S(2)}) copy-start(s32[4,8,2048]{2,1,0:T(8,128)S(1)} %reshape.234) | copy-start | bytes 786436
  85.1 29.5 %copy-start.6 = (bf16[2,96,1024]{2,1,0:T(8,128)(2,1)}, bf16[2,96,1024]{2,1,0:T(8,128)(2,1)S(1)}, u32[]{:S(2)}) copy-start(bf16[2,96,1024]{2,1,0:T(8,128)(2,1)S(1)} %collective-permute-done.5.refs_5_) | copy-start | bytes 1179652
  85.1 10.4 %collective-permute-start.6 = (bf16[2,96,1024]{2,1,0:T(8,128)(2,1)S(1)}, bf16[2,96,1024]{2,1,0:T(8,128)(2,1)S(1)}, u32[]{:S(2)}, u32[]{:S(2)}) collective-permute-start(bf16[2,96,1024]{2,1,0:T(8,128)(2,1)S(1)} %collective-permute-done.5.refs_5_), channel_id=1, source_target_pairs={{32,0},{481,1},{64,32},{1,33},{96,64},{33,65},{128,96},{65,97},{16... | collective-permute-start | bytes 1179656 | tf_op jit(solution)/shard_map/ppermute | solution.py:33
  95.5 19.1 %copy-start.8 = (bf16[2,96,1024]{2,1,0:T(8,128)(2,1)}, bf16[2,96,1024]{2,1,0:T(8,128)(2,1)S(1)}, u32[]{:S(2)}) copy-start(bf16[2,96,1024]{2,1,0:T(8,128)(2,1)S(1)} %collective-permute-done.6.refs_6_) | copy-start | bytes 1179652
  95.5 10.9 %collective-permute-start.7 = (bf16[2,96,1024]{2,1,0:T(8,128)(2,1)S(1)}, bf16[2,96,1024]{2,1,0:T(8,128)(2,1)S(1)}, u32[]{:S(2)}, u32[]{:S(2)}) collective-permute-start(bf16[2,96,1024]{2,1,0:T(8,128)(2,1)S(1)} %collective-permute-done.6.refs_6_), channel_id=1, source_target_pairs={{32,0},{481,1},{64,32},{1,33},{96,64},{33,65},{128,96},{65,97},{16... | collective-permute-start | bytes 1179656 | tf_op jit(solution)/shard_map/ppermute | solution.py:33
  106.4 12.7 %copy-start.1 = (bf16[2,96,1024]{2,1,0:T(8,128)(2,1)}, bf16[2,96,1024]{2,1,0:T(8,128)(2,1)S(1)}, u32[]{:S(2)}) copy-start(bf16[2,96,1024]{2,1,0:T(8,128)(2,1)S(1)} %collective-permute-done.7.refs_7_) | copy-start | bytes 1179652
  106.4 12.7 %collective-permute-start.8 = (bf16[96,1024]{1,0:T(8,128)(2,1)S(1)}, bf16[96,1024]{1,0:T(8,128)(2,1)S(1)}, u32[]{:S(2)}, u32[]{:S(2)}) collective-permute-start(bf16[96,1024]{1,0:T(8,128)(2,1)S(1)} %slice_bitcast_fusion), channel_id=1, source_target_pairs={{32,0},{481,1},{64,32},{1,33},{96,64},{33,65},{128,96},{65,97},{16... | collective-permute-start | bytes 589832 | tf_op jit(solution)/shard_map/ppermute | solution.py:33
  114.6 4.5 %copy-start.7 = (bf16[2,96,1024]{2,1,0:T(8,128)(2,1)S(1)}, bf16[2,96,1024]{2,1,0:T(8,128)(2,1)}, u32[]{:S(2)}) copy-start(bf16[2,96,1024]{2,1,0:T(8,128)(2,1)} %copy-done.6) | copy-start | bytes 1179652
  114.6 4.5 %copy-start.9 = (bf16[2,96,1024]{2,1,0:T(8,128)(2,1)S(1)}, bf16[2,96,1024]{2,1,0:T(8,128)(2,1)}, u32[]{:S(2)}) copy-start(bf16[2,96,1024]{2,1,0:T(8,128)(2,1)} %copy-done.8) | copy-start | bytes 1179652
  117.2 26.7 %collective-permute-start.9 = (bf16[4,2,96,1024]{3,2,1,0:T(8,128)(2,1)}, bf16[4,2,96,1024]{3,2,1,0:T(8,128)(2,1)S(1)}, u32[]{:S(2)}, u32[]{:S(2)}) collective-permute-start(bf16[4,2,96,1024]{3,2,1,0:T(8,128)(2,1)} %pad_maximum_fusion), channel_id=1, source_target_pairs={{1,0},{0,1},{3,2},{2,3},{5,4},{4,5},{7,6},{6,7},{9,8},{8,9},{11,10... | collective-permute-start | bytes 4718600 | tf_op jit(solution)/shard_map/ppermute | solution.py:25
  119.1 9.6 %copy-start.10 = (bf16[96,1024]{1,0:T(8,128)(2,1)}, bf16[96,1024]{1,0:T(8,128)(2,1)S(1)}, u32[]{:S(2)}) copy-start(bf16[96,1024]{1,0:T(8,128)(2,1)S(1)} %collective-permute-done.8.refs_8_) | copy-start | bytes 589828
  120.4 23.4 %collective-permute-start.10 = (bf16[7,96,1024]{2,1,0:T(8,128)(2,1)}, bf16[7,96,1024]{2,1,0:T(8,128)(2,1)}, u32[]{:S(2)}, u32[]{:S(2)}) collective-permute-start(bf16[7,96,1024]{2,1,0:T(8,128)(2,1)} %pad_maximum_fusion.1), channel_id=1, source_target_pairs={{1,0},{0,1},{3,2},{2,3},{5,4},{4,5},{7,6},{6,7},{9,8},{8,9},{11,10... | collective-permute-start | bytes 4128776 | tf_op jit(solution)/shard_map/ppermute | solution.py:25
  143.8 1.1 copy-start.2
  159.2 7.3 %copy-start.16 = (s32[256,64]{0,1:T(8,128)S(1)}, s32[256,64]{0,1:T(8,128)}, u32[]{:S(2)}) copy-start(s32[256,64]{0,1:T(8,128)} %param.7) | copy-start | bytes 196612
  159.2 35.2 %all-to-all-start.1 = ((bf16[16,64,1024]{2,1,0:T(8,128)(2,1)}), bf16[16,64,1024]{2,1,0:T(8,128)(2,1)S(1)}, u32[]{:S(2)}, u32[]{:S(2)}) async-start(bf16[16,64,1024]{2,1,0:T(8,128)(2,1)} %bitcast.92), calls=%async_computation.1 | async-start | bytes 4194304 | tf_op jit(solution)/shard_map/all_to_all | solution.py:280
  172.6 0.6 copy-start.14
  173.2 6.7 %copy-start.15 = (s32[1,512]{1,0:T(1,128)S(1)}, s32[1,512]{1,0:T(1,128)}, u32[]{:S(2)}) copy-start(s32[1,512]{1,0:T(1,128)} %compare_select_fusion.12.row_ref) | copy-start | bytes 6148
  179.8 14.9 %copy-start.12 = (bf16[1,64,1024]{2,1,0:T(8,128)(2,1)S(1)}, bf16[1,64,1024]{2,1,0:T(8,128)(2,1)}, u32[]{:S(2)}) copy-start(bf16[1,64,1024]{2,1,0:T(8,128)(2,1)} %param.6) | copy-start | bytes 393220

commit v4 on v3

--- a/solution.py
+++ b/solution.py
@@ -10,7 +10,6 @@
 P_SIZE = 64
 KB = 32
 Z, Y, X, C = 16, 4, 4, 2
-SIZES = {"z": Z, "y": Y, "x": X, "core": C}
 OWN = 64
 CAP = 8
 HALF = 32
@@ -20,46 +19,9 @@
 NN = (((1,), (0,)), ((), ()))
 
 
-def pull(value, axis, step):
-    size = SIZES[axis]
-    return lax.ppermute(value, axis, [((i + step) % size, i) for i in range(size)])
-
-
-def ring_pull(value):
-    pairs = []
-    for z in range(Z):
-        pairs.append((((z + 1) % Z) * C, z * C))
-        pairs.append((((z - 1) % Z) * C + 1, z * C + 1))
-    return lax.ppermute(value, ("z", "core"), pairs)
-
-
 def gather_codes(codes):
     copies = jnp.broadcast_to(codes.astype(jnp.int16)[None], (Z * Y,) + codes.shape)
     return lax.all_to_all(copies, ("z", "y"), split_axis=0, concat_axis=0, tiled=True)
-
-
-def gather_rows(piece):
-    chain = [jnp.stack([piece, pull(piece, "core", 1)])]
-    for _ in range(7):
-        chain.append(ring_pull(chain[-1]))
-    last = ring_pull(chain[7][0])
-    early = pull(jnp.stack(chain[1:5]), "core", 1)
-    late = pull(jnp.concatenate(chain[5:8] + [last[None]]), "core", 1)
-    return chain, last, early, late
-
-
-def unit_places():
-    places = []
-    for e in range(C):
-        places += [(t, (e,)) for t in range(8)]
-        places.append((8, ()) if e == 0 else (10, (6,)))
-        for t in range(9, 16):
-            back = 16 - t
-            if back < 5:
-                places.append((9, (back - 1, 1 - e)))
-            else:
-                places.append((10, (2 * (back - 5) + 1 - e,)))
-    return places
 
 
 def compact(all_codes, local):
@@ -137,59 +99,60 @@
     )(row_index, column_index)
 
 
-def merge_kernel(*refs):
-    pieces, refs = refs[:11], refs[11:]
-    assigned_ref, *count_refs = refs[: 1 + X]
-    out_ref, book_ref, vector_ref, sems = refs[1 + X :]
+def merge_kernel(rows_ref, assigned_ref, *refs):
+    count_refs, (out_ref, book_ref, vector_ref, total_ref, sems) = refs[:X], refs[X:]
     copies = []
-    for unit, (source, where) in enumerate(unit_places()):
-        piece = pieces[source].at[where] if where else pieces[source]
+    for core in range(C):
+        half = rows_ref.at[:, core]
         copies.append(
             pltpu.make_async_copy(
-                piece.at[pl.ds(0, OWN)],
-                book_ref.at[pl.ds(unit * OWN, OWN)],
-                sems.at[2 * unit],
+                half.at[:, pl.ds(OWN, HALF)], vector_ref.at[core], sems.at[core]
             )
         )
+    for core in range(C):
+        half = rows_ref.at[:, core]
         copies.append(
             pltpu.make_async_copy(
-                piece.at[pl.ds(OWN, HALF)],
-                vector_ref.at[pl.ds(unit * HALF, HALF)],
-                sems.at[2 * unit + 1],
+                half.at[:, pl.ds(0, OWN)], book_ref.at[core], sems.at[C + core]
             )
         )
     for copy in copies:
         copy.start()
-    for copy in copies:
+    features = out_ref.shape[1]
+    spans = [slice(i * PLANE, (i + 1) * PLANE) for i in range(X)]
+    for copy in copies[:C]:
         copy.wait()
-    for i in range(X):
-        span = slice(i * PLANE, (i + 1) * PLANE)
-        total = lax.dot_general(
-            assigned_ref[span, :], vector_ref[...], NN, preferred_element_type=jnp.float32
-        )
-        total -= lax.dot_general(
-            count_refs[i][...], book_ref[...], NN, preferred_element_type=jnp.float32
+    held = vector_ref[...].reshape(C * Z * HALF, features)
+    for span in spans:
+        total_ref[span, :] = lax.dot_general(
+            assigned_ref[span, :], held, NN, preferred_element_type=jnp.float32
+        )
+    for copy in copies[C:]:
+        copy.wait()
+    held = book_ref[...].reshape(C * Z * OWN, features)
+    for span, count_ref in zip(spans, count_refs):
+        total = total_ref[span, :] - lax.dot_general(
+            count_ref[...], held, NN, preferred_element_type=jnp.float32
         )
         out_ref[span, :] = total.astype(out_ref.dtype)
 
 
-def merge(chain, last, early, late, assigned, counts):
-    pieces = chain + [last, early, late]
-    features = last.shape[1]
-    units = C * Z
+def merge(rows, assigned, counts):
+    features = rows.shape[-1]
+    whole = pl.BlockSpec(memory_space=pltpu.VMEM)
     return pl.pallas_call(
         merge_kernel,
-        in_specs=[pl.BlockSpec(memory_space=pl.ANY)] * len(pieces)
-        + [pl.BlockSpec(memory_space=pltpu.VMEM)] * (1 + X),
-        out_specs=pl.BlockSpec(memory_space=pltpu.VMEM),
+        in_specs=[pl.BlockSpec(memory_space=pl.ANY)] + [whole] * (1 + X),
+        out_specs=whole,
         out_shape=jax.ShapeDtypeStruct((X * PLANE, features), jnp.bfloat16),
         scratch_shapes=[
-            pltpu.VMEM((units * OWN, features), jnp.bfloat16),
-            pltpu.VMEM((units * HALF, features), jnp.bfloat16),
-            pltpu.SemaphoreType.DMA((2 * units,)),
+            pltpu.VMEM((C, Z, OWN, features), jnp.bfloat16),
+            pltpu.VMEM((C, Z, HALF, features), jnp.bfloat16),
+            pltpu.VMEM((X * PLANE, features), jnp.float32),
+            pltpu.SemaphoreType.DMA((2 * C,)),
         ],
         name="merge",
-    )(*pieces, assigned, *counts)
+    )(rows, assigned, *counts)
 
 
 def gram_kernel(book_ref, start_ref, row_ref, codes_ref, out_ref):
@@ -230,33 +193,22 @@
 
 
 def slot_indices(tuples, z, y, x, core):
-    sign = 1 - 2 * core
     own = jnp.stack(
         [lax.dynamic_index_in_dim(tuples[i], i * C + core, 0, keepdims=True) for i in range(X)]
     )
     row_index = jnp.where(own >= 0, own - PLANE * z, -1)
-    columns = []
-    for e in range(C):
-        book = x * C + (core + e) % C
-        code = lax.dynamic_index_in_dim(tuples, book, 1, keepdims=False)
-        place = ((code // PLANE - z) * sign) % Z * OWN + code % OWN
-        inside = (code >= 0) & (code // OWN % Y == y)
-        columns.append(jnp.where(inside, place, -1))
-    return row_index, jnp.stack(columns, axis=1)
+    code = lax.dynamic_slice_in_dim(tuples, x * C, C, 1)
+    place = code // PLANE * OWN + code % OWN
+    inside = (code >= 0) & (code // OWN % Y == y)
+    return row_index, jnp.where(inside, place, -1)
 
 
 def vector_rows(all_codes, z, y, x, core):
     mine = all_codes.reshape(Z, Y, X * C, -1)
     mine = lax.dynamic_index_in_dim(mine, y, 1, keepdims=False)
-    portion = lax.dynamic_slice_in_dim(mine, 2 * HALF * x, 2 * HALF, 2)
+    portion = lax.dynamic_slice_in_dim(mine, C * HALF * x, C * HALF, 2)
     portion = by_parity(portion, core).reshape(Z, X, C, HALF)
-    plus = lax.dynamic_slice_in_dim(jnp.concatenate([portion, portion]), z, Z, 0)
-    back = portion[::-1]
-    minus = lax.dynamic_slice_in_dim(jnp.concatenate([back, back]), Z - 1 - z, Z, 0)
-    plus = plus.transpose(1, 2, 0, 3)
-    minus = minus.transpose(1, 2, 0, 3)[:, ::-1]
-    chosen = jnp.where(core == 0, plus, minus).reshape(X, 1, C * Z * HALF)
-    return chosen - PLANE * z
+    return portion.transpose(1, 2, 0, 3).reshape(X, 1, C * Z * HALF) - PLANE * z
 
 
 def shards(vectors, codes, codebook, pairs):
@@ -266,19 +218,17 @@
     owner = z * Y + y
     book = x * C + core
     mine = lax.dynamic_slice_in_dim(vectors, 2 * HALF * x + HALF * core, HALF, 0)
-    pieces = gather_rows(jnp.concatenate([codebook[0], mine]))
+    piece = jnp.concatenate([codebook[0], mine])
+    rows = lax.all_gather(piece, ("z", "core")).reshape(Z, C, OWN + HALF, features)
     all_codes = gather_codes(codes).astype(jnp.int32)
     local = by_parity(all_codes, core) - PLANE * z
     tuples = compact(all_codes, local)
     tuples = tuples.reshape(X, tuples.shape[1], -1)
     row_index, column_index = slot_indices(tuples, z, y, x, core)
-    counts = [pair_counts(row_index[i], column_index[i]) for i in range(X)]
     ids = jnp.arange(PLANE, dtype=jnp.int32)[None, :, None]
     assigned = (vector_rows(all_codes, z, y, x, core) == ids).astype(jnp.bfloat16)
-    partial = merge(*pieces, assigned.reshape(X * PLANE, -1), counts)
-    sent = partial.reshape(X * Y, OWN, features)
-    received = lax.all_to_all(sent, ("x", "y"), split_axis=0, concat_axis=0, tiled=True)
-    right_side = jnp.sum(received.astype(jnp.float32), axis=0)
+    assigned = assigned.reshape(X * PLANE, -1)
+    counts = [pair_counts(row_index[i], column_index[i]) for i in range(X)]
     held = lax.dynamic_index_in_dim(tuples, x, 0, keepdims=False)
     held = held.reshape(X * C, -1, Y, CAP)
     held = lax.dynamic_index_in_dim(held, y, 2, keepdims=False).reshape(X * C, -1)
@@ -288,6 +238,10 @@
     gram = gram_counts(partner // KB, partner % KB * BLK, own_row, held)
     matched = own_row == jnp.arange(OWN, dtype=jnp.int32)[:, None]
     code_count = jnp.sum(matched.astype(jnp.float32), axis=1)
+    assigned, gram, code_count = lax.optimization_barrier((assigned, gram, code_count))
+    partial = merge(rows, assigned, counts).reshape(X * Y, OWN, features)
+    received = lax.all_to_all(partial, ("x", "y"), split_axis=0, concat_axis=0, tiled=True)
+    right_side = jnp.sum(received.astype(jnp.float32), axis=0)
     current = codebook[0].astype(jnp.float32)
     updated = current + (right_side - 2.0 * current) / (code_count[:, None] + 2.0)
     return updated[None], gram[None]

time: 198 us -> 158 us (0.80)
  starting transfers between devices: 73.3 us -> 26.1 us
  between operations: 1.25 us -> 14.4 us
  waiting for transfers between devices: 45.3 us -> 55.6 us
  local copies, waits for them, and re-layouts: 18.2 us -> 10 us
  other arithmetic: 14.5 us -> 9.15 us
    ppermute x11 -> x0, starting transfers between devices: 47.2 us -> none  [the longest x8 40.8 us: ring_pull(): return lax.ppermute(value, ('z', 'core'), pairs)]
    ppermute x11 -> x0, waiting for transfers between devices: 31 us -> none  [the longest x8 31 us: ring_pull(): return lax.ppermute(value, ('z', 'core'), pairs)]
    all_to_all x1, waiting for transfers between devices: 0.01 us -> 23.2 us  [gather_codes(): lax.all_to_all(copies, ('z', 'y'), split_axis=0, concat_axis=0, tiled=True)]
    all_to_all x1, waiting for transfers between devices: 14.4 us -> 28.6 us  [shards(): lax.all_to_all(partial, ('x', 'y'), split_axis=0, concat_axis=0, tiled=True)]
    all_gather x0 -> x1, waiting for transfers between devices: none -> 3.88 us  [shards(): lax.all_gather(piece, ('z', 'core')).reshape(Z, C, OWN + HALF, features)]
    another operation x4 -> x1, other arithmetic: 4.09 us -> 0.55 us  [the longest x1 2.57 us: gather_rows(): early = pull(jnp.stack(chain[1:5]), 'core', 1)]
    slice x5, local copies, waits for them, and re-layouts: 3.06 us -> 0.55 us  [slot_indices(): tuples[i]]
    unnamed x39 -> x13, local copies, waits for them, and re-layouts: 3.53 us -> 1.1 us
  transfers between devices with their start and end apart: 13 -> 3, of which waited for: 6 -> 3; matrix products, arithmetic and copies ran while one was open for 16% -> 11% of each run, Pallas kernels for 14% -> 17%
where the time goes in v4:
time: 158 us; the launch traced here: 157 us
  waiting for transfers between devices  55.6 us (35%)
  Pallas kernels  39.3 us (25%)
  starting transfers between devices  26.1 us (17%)
  between operations  14.4 us (9%)
  local copies, waits for them, and re-layouts  10 us (6%)
  other arithmetic  9.15 us (6%)
  matrix products  1.96 us (1%)
    all_to_all x1, waiting for transfers between devices, shards(): lax.all_to_all(partial, ('x', 'y'), split_axis=0, concat_axis=0, tiled=True)  28.6 us
    all_to_all x1, waiting for transfers between devices, gather_codes(): lax.all_to_all(copies, ('z', 'y'), split_axis=0, concat_axis=0, tiled=True)  23.2 us
    pallas_call x4, Pallas kernels, pair_counts(): pl.pallas_call(pair_kernel, grid=(slots // CHUNK,), in_specs=[pl.BlockSpe...  20.1 us
    all_to_all x1, starting transfers between devices, gather_codes(): lax.all_to_all(copies, ('z', 'y'), split_axis=0, concat_axis=0, tiled=True)  18.7 us
    pallas_call x1, Pallas kernels, merge(): pl.pallas_call(merge_kernel, in_specs=[pl.BlockSpec(memory_space=pl.ANY)]...  12.6 us
    all_to_all x1, starting transfers between devices, shards(): lax.all_to_all(partial, ('x', 'y'), split_axis=0, concat_axis=0, tiled=True)  7.36 us
    pallas_call x1, Pallas kernels, gram_counts(): pl.pallas_call(gram_kernel, grid_spec=pltpu.PrefetchScalarGridSpec(num_sc...  6.68 us
    all_gather x1, waiting for transfers between devices, shards(): lax.all_gather(piece, ('z', 'core')).reshape(Z, C, OWN + HALF, features)  3.88 us
  transfers between devices with their start and end apart: 3, of which 3 were waited for; matrix products, arithmetic and copies ran while one was open for 11% of the time, Pallas kernels for 17%

profile of v4, /device:TPU:6, one launch (start us, length us, event | category | flops | bytes accessed | tf_op | source)
XLA Modules:
  0.0 156.6 jit_solution(17554144053363081876)
XLA Ops:
  7.2 1.0 copy-done
  8.2 1.6 %pad_maximum_fusion = bf16[96,1024]{1,0:T(8,128)(2,1)} fusion(bf16[32,1024]{1,0:T(8,128)(2,1)S(1)} %constant_dynamic-slice_fusion.3, bf16[64,1024]{1,0:T(8,128)(2,1)} %bitcast.83), kind=kLoop, calls=%fused_computation.42 | loop fusion | flops 393216 | bytes 393216 | tf_op jit(solution)/shard_map/concatenate | solution.py:221
  9.8 0.7 convert_element_type.31
  10.5 0.7 broadcast_in_dim.50
  11.3 18.7 %all-to-all-start = ((s16[64,8,256]{2,1,0:T(8,128)(2,1)}), s16[64,8,256]{2,1,0:T(8,128)(2,1)S(1)}, u32[]{:S(2)}, u32[]{:S(2)}) async-start(s16[64,8,256]{2,1,0:T(8,128)(2,1)} %broadcast_in_dim.50), calls=%async_computation | async-start | bytes 524288 | tf_op jit(solution)/shard_map/all_to_all | solution.py:24
  30.4 0.9 dynamic-slice_reduce_fusion.1
  31.4 0.6 fusion.24
  32.0 23.2 %all-to-all-done = s16[64,8,256]{2,1,0:T(8,128)(2,1)S(1)} async-done(((s16[64,8,256]{2,1,0:T(8,128)(2,1)}), s16[64,8,256]{2,1,0:T(8,128)(2,1)S(1)}, u32[]{:S(2)}, u32[]{:S(2)}) %all-to-all-start) | async-done | bytes 262176 | tf_op jit(solution)/shard_map/all_to_all | solution.py:24
  55.2 0.3 reshape.231
  55.6 0.1 sub.85
  55.7 0.1 sub.87
  55.8 1.4 and_select_fusion
  57.3 0.3 eq.107
  57.6 0.4 eq.108
  58.0 0.5 fusion.11
  58.5 0.4 fusion.4
  58.9 1.6 %fusion.5 = s32[64,17,128]{2,1,0:T(8,128)S(1)} fusion(s32[128]{0:T(128)S(1)} %eq.120, s32[64,16,256]{2,1,0:T(8,128)S(1)} %fusion.4, bf16[64,8,256]{2,1,0:T(8,128)(2,1)S(1)} %get-tuple-element.13, bf16[64,8,256]{2,1,0:T(8,128)(2,1)S(1)} %get-tuple-element.12, bf16[17]{0:T(256)(128)(2,1)S(1)} %pad.6.clone), kind=kOutput, calls=%fused_computation.9 | convolution fusion | flops 75210752 | bytes 2130466 | tf_op jit(solution)/shard_map/dot_general | solution.py:47
  60.6 0.2 copy.26
  60.8 0.4 copy.27
  61.2 0.1 copy.28
  61.4 0.1 squeeze.56
  61.5 0.1 copy.31
  61.7 0.1 squeeze.59
  61.8 0.1 copy.30
  61.9 0.1 squeeze.58
  62.1 0.1 copy.29
  62.2 0.1 squeeze.57
  62.4 0.5 reshape.233
  62.9 1.2 reshape.234
  64.1 0.8 dynamic-slice_reduce_fusion
  64.9 0.2 reshape.235.codes_ref
  65.1 1.8 %fusion.3.assigned_ref = bf16[1024,1024]{1,0:T(8,128)(2,1)} fusion(s32[1024]{0:T(1024)S(1)} %bitcast.89, s32[4,1024]{1,0:T(4,128)S(1)} %sub.87), kind=kLoop, calls=%fused_computation.6 | loop fusion | flops 2097152 | bytes 2117632 | tf_op jit(solution)/shard_map/convert_element_type | solution.py:229
  66.8 0.6 compare_select_fusion.6.row_ref
  67.4 6.7 %gram_counts.1 = f32[64,8192]{1,0:T(8,128)} custom-call(s32[64]{0:T(128)} %get-tuple-element.23.book_ref, s32[64]{0:T(128)} %get-tuple-element.22.start_ref, s32[1,512]{1,0:T(1,128)} %compare_select_fusion.6.row_ref, s32[8,512]{1,0:T(8,128)} %copy-done.2), custom_call_target="tpu_custom_call" | custom-call | tf_op jit(solution)/shard_map/gram_counts/pallas_call | solution.py:173
  74.1 0.1 convert_reduce_fusion.1
  74.3 0.5 and_select_fusion.3
  74.8 0.6 slice_bitcast_fusion.4
  75.4 0.6 slice_bitcast_fusion
  76.1 5.0 %pair_counts.7.refs_3_ = bf16[256,2048]{1,0:T(8,128)(2,1)} custom-call(s32[1,2048]{1,0:T(1,128)} %get-tuple-element.18.row_ref, s32[2,2048]{1,0:T(2,128)} %get-tuple-element.14.column_ref), custom_call_target="tpu_custom_call" | custom-call | flops 2147483648 | bytes 1048576 | tf_op jit(solution)/shard_map/pair_counts/pallas_call | solution.py:85
  81.1 5.0 %pair_counts.6.refs_2_ = bf16[256,2048]{1,0:T(8,128)(2,1)} custom-call(s32[1,2048]{1,0:T(1,128)} %get-tuple-element.19.row_ref, s32[2,2048]{1,0:T(2,128)} %get-tuple-element.15.column_ref), custom_call_target="tpu_custom_call" | custom-call | flops 2147483648 | bytes 1048576 | tf_op jit(solution)/shard_map/pair_counts/pallas_call | solution.py:85
  86.1 5.1 %pair_counts.5.refs_1_ = bf16[256,2048]{1,0:T(8,128)(2,1)} custom-call(s32[1,2048]{1,0:T(1,128)} %get-tuple-element.20.row_ref, s32[2,2048]{1,0:T(2,128)} %get-tuple-element.16.column_ref), custom_call_target="tpu_custom_call" | custom-call | flops 2147483648 | bytes 1048576 | tf_op jit(solution)/shard_map/pair_counts/pallas_call | solution.py:85
  91.1 5.0 %pair_counts.4.refs_0_ = bf16[256,2048]{1,0:T(8,128)(2,1)} custom-call(s32[1,2048]{1,0:T(1,128)} %get-tuple-element.21.row_ref, s32[2,2048]{1,0:T(2,128)} %get-tuple-element.17.column_ref), custom_call_target="tpu_custom_call" | custom-call | flops 2147483648 | bytes 1048576 | tf_op jit(solution)/shard_map/pair_counts/pallas_call | solution.py:85
  96.1 3.9 %all-gather.3.cloned.1.call-done = bf16[3072,1024]{1,0:T(8,128)(2,1)} async-done(((bf16[96,1024]{1,0:T(8,128)(2,1)}), bf16[3072,1024]{1,0:T(8,128)(2,1)}) %all-gather.3.cloned.1.call-update) | async-done | bytes 6291472 | tf_op jit(solution)/shard_map/all_gather | solution.py:222
  100.0 12.6 %merge.1 = bf16[1024,1024]{1,0:T(8,128)(2,1)} custom-call(bf16[16,2,96,1024]{3,2,1,0:T(8,128)(2,1)} %bitcast.77, bf16[1024,1024]{1,0:T(8,128)(2,1)} %fusion.3.assigned_ref, bf16[256,2048]{1,0:T(8,128)(2,1)} %pair_counts.4.refs_0_, bf16[256,2048]{1,0:T(8,128)(2,1)} %pair_counts.5.refs_1_, bf16[256,2048]{1,0:T(8,128)(2,1)} %pair_counts.6.refs_2_, ...), custom_call_target="tpu_custom_call" | custom-call | tf_op jit(solution)/shard_map/merge/pallas_call | solution.py:143
  112.6 7.4 %all-to-all-start.1 = ((bf16[16,64,1024]{2,1,0:T(8,128)(2,1)}), bf16[16,64,1024]{2,1,0:T(8,128)(2,1)S(1)}, u32[]{:S(2)}, u32[]{:S(2)}) async-start(bf16[16,64,1024]{2,1,0:T(8,128)(2,1)} %bitcast.76), calls=%async_computation.1 | async-start | bytes 4194304 | tf_op jit(solution)/shard_map/all_to_all | solution.py:243
  120.0 28.6 %all-to-all-done.1 = bf16[16,64,1024]{2,1,0:T(8,128)(2,1)S(1)} async-done(((bf16[16,64,1024]{2,1,0:T(8,128)(2,1)}), bf16[16,64,1024]{2,1,0:T(8,128)(2,1)S(1)}, u32[]{:S(2)}, u32[]{:S(2)}) %all-to-all-start.1) | async-done | bytes 2097184 | tf_op jit(solution)/shard_map/all_to_all | solution.py:243
  148.5 0.4 convert_reduce_fusion
  148.9 0.8 convert_add_fusion
  (34 shorter events, 0.9 us)
Async XLA Ops:
  7.2 1.0 copy-start
  7.2 92.8 %all-gather.3.cloned.1.call-start = ((), (), s32[]{:S(2)}) async-start(), calls=%async_computation.2 | async-start | bytes 6488064 | tf_op jit(solution)/shard_map/all_gather | solution.py:222
  11.3 43.8 %all-to-all-start = ((s16[64,8,256]{2,1,0:T(8,128)(2,1)}), s16[64,8,256]{2,1,0:T(8,128)(2,1)S(1)}, u32[]{:S(2)}, u32[]{:S(2)}) async-start(s16[64,8,256]{2,1,0:T(8,128)(2,1)} %broadcast_in_dim.50), calls=%async_computation | async-start | bytes 524288 | tf_op jit(solution)/shard_map/all_to_all | solution.py:24
  65.1 2.3 %copy-start.2 = (s32[8,512]{1,0:T(8,128)}, s32[8,512]{1,0:T(8,128)S(1)}, u32[]{:S(2)}) copy-start(s32[8,512]{1,0:T(8,128)S(1)} %reshape.235.codes_ref) | copy-start | bytes 49156
  67.4 6.7 %copy-start.3 = (s32[1,512]{1,0:T(1,128)S(1)}, s32[1,512]{1,0:T(1,128)}, u32[]{:S(2)}) copy-start(s32[1,512]{1,0:T(1,128)} %compare_select_fusion.6.row_ref) | copy-start | bytes 6148
  112.6 35.9 %all-to-all-start.1 = ((bf16[16,64,1024]{2,1,0:T(8,128)(2,1)}), bf16[16,64,1024]{2,1,0:T(8,128)(2,1)S(1)}, u32[]{:S(2)}, u32[]{:S(2)}) async-start(bf16[16,64,1024]{2,1,0:T(8,128)(2,1)} %bitcast.76), calls=%async_computation.1 | async-start | bytes 4194304 | tf_op jit(solution)/shard_map/all_to_all | solution.py:243
  119.9 29.0 %copy-start.1 = (bf16[1,64,1024]{2,1,0:T(8,128)(2,1)S(1)}, bf16[1,64,1024]{2,1,0:T(8,128)(2,1)}, u32[]{:S(2)}) copy-start(bf16[1,64,1024]{2,1,0:T(8,128)(2,1)} %param.6) | copy-start | bytes 393220
Sparse Core Ops, SparseCore 0:
  10.1 89.8 all-gather.2

commit v5 on v4

--- a/solution.py
+++ b/solution.py
@@ -15,13 +15,19 @@
 HALF = 32
 PLANE = Y * OWN
 CHUNK = 512
+PARTS = 4
 NT = (((1,), (1,)), ((), ()))
 NN = (((1,), (0,)), ((), ()))
 
 
-def gather_codes(codes):
-    copies = jnp.broadcast_to(codes.astype(jnp.int16)[None], (Z * Y,) + codes.shape)
-    return lax.all_to_all(copies, ("z", "y"), split_axis=0, concat_axis=0, tiled=True)
+def gather_codes(codes, book):
+    mine = lax.dynamic_slice_in_dim(codes.astype(jnp.int16), book, 1, 0)
+    copies = jnp.broadcast_to(mine[None], (Z * Y,) + mine.shape)
+    whole = lax.all_to_all(copies, ("z", "y"), split_axis=0, concat_axis=0, tiled=True)
+    whole = whole.reshape(Z * Y, codes.shape[1])
+    copies = jnp.broadcast_to(whole[None], (X * C,) + whole.shape)
+    books = lax.all_to_all(copies, ("x", "core"), split_axis=0, concat_axis=0, tiled=True)
+    return books.astype(jnp.int32).transpose(1, 0, 2)
 
 
 def compact(all_codes, local):
@@ -59,100 +65,111 @@
 
 
 def pair_kernel(row_ref, column_ref, out_ref, total_ref):
-    step = pl.program_id(0)
+    step = pl.program_id(1)
 
     @pl.when(step == 0)
     def _():
         total_ref[...] = jnp.zeros_like(total_ref)
 
-    member = match(row_ref[...], PLANE)
+    member = match(row_ref[0], PLANE)
     width = Z * OWN
     for e in range(C):
-        table = match(column_ref[e : e + 1, :], width)
+        table = match(column_ref[0, e : e + 1, :], width)
         span = slice(e * width, (e + 1) * width)
         total_ref[:, span] += lax.dot_general(
             member, table, NT, preferred_element_type=jnp.float32
         )
 
-    @pl.when(step == pl.num_programs(0) - 1)
+    @pl.when(step == pl.num_programs(1) - 1)
     def _():
         out_ref[...] = total_ref[...].astype(out_ref.dtype)
 
 
 def pair_counts(row_index, column_index):
-    slots = row_index.shape[1]
+    books, _, slots = row_index.shape
     columns = C * Z * OWN
     return pl.pallas_call(
         pair_kernel,
-        grid=(slots // CHUNK,),
+        grid=(books, slots // CHUNK),
         in_specs=[
-            pl.BlockSpec((1, CHUNK), lambda s: (0, s)),
-            pl.BlockSpec((C, CHUNK), lambda s: (0, s)),
+            pl.BlockSpec((1, 1, CHUNK), lambda i, s: (i, 0, s)),
+            pl.BlockSpec((1, C, CHUNK), lambda i, s: (i, 0, s)),
         ],
-        out_specs=pl.BlockSpec((PLANE, columns), lambda s: (0, 0)),
-        out_shape=jax.ShapeDtypeStruct((PLANE, columns), jnp.bfloat16),
+        out_specs=pl.BlockSpec((PLANE, columns), lambda i, s: (i, 0)),
+        out_shape=jax.ShapeDtypeStruct((books * PLANE, columns), jnp.bfloat16),
         scratch_shapes=[pltpu.VMEM((PLANE, columns), jnp.float32)],
-        cost_estimate=pl.CostEstimate(
-            flops=2 * PLANE * columns * slots, transcendentals=0, bytes_accessed=1 << 20
-        ),
+        compiler_params=pltpu.CompilerParams(vmem_limit_bytes=20 << 20),
         name="pair_counts",
     )(row_index, column_index)
 
 
-def merge_kernel(rows_ref, assigned_ref, *refs):
-    count_refs, (out_ref, book_ref, vector_ref, total_ref, sems) = refs[:X], refs[X:]
-    copies = []
-    for core in range(C):
-        half = rows_ref.at[:, core]
-        copies.append(
-            pltpu.make_async_copy(
-                half.at[:, pl.ds(OWN, HALF)], vector_ref.at[core], sems.at[core]
+def merge_kernel(
+    rows_ref, counts_ref, assigned_ref, out_ref, table_ref, book_ref, vector_ref, sems
+):
+    features = out_ref.shape[1]
+    width = features // PARTS
+    tables = pltpu.make_async_copy(counts_ref, table_ref, sems.at[2 * C * PARTS])
+    vectors, books = [], []
+    for part in range(PARTS):
+        lanes = pl.ds(part * width, width)
+        for core in range(C):
+            half = rows_ref.at[:, core]
+            slot = (part * C + core) * 2
+            vectors.append(
+                pltpu.make_async_copy(
+                    half.at[:, pl.ds(OWN, HALF), lanes],
+                    vector_ref.at[part, core],
+                    sems.at[slot],
+                )
             )
-        )
-    for core in range(C):
-        half = rows_ref.at[:, core]
-        copies.append(
-            pltpu.make_async_copy(
-                half.at[:, pl.ds(0, OWN)], book_ref.at[core], sems.at[C + core]
+            books.append(
+                pltpu.make_async_copy(
+                    half.at[:, pl.ds(0, OWN), lanes],
+                    book_ref.at[part, core],
+                    sems.at[slot + 1],
+                )
             )
-        )
-    for copy in copies:
+    for copy in vectors[:C] + [tables] + books[:C]:
         copy.start()
-    features = out_ref.shape[1]
-    spans = [slice(i * PLANE, (i + 1) * PLANE) for i in range(X)]
-    for copy in copies[:C]:
-        copy.wait()
-    held = vector_ref[...].reshape(C * Z * HALF, features)
-    for span in spans:
-        total_ref[span, :] = lax.dot_general(
-            assigned_ref[span, :], held, NN, preferred_element_type=jnp.float32
-        )
-    for copy in copies[C:]:
-        copy.wait()
-    held = book_ref[...].reshape(C * Z * OWN, features)
-    for span, count_ref in zip(spans, count_refs):
-        total = total_ref[span, :] - lax.dot_general(
-            count_ref[...], held, NN, preferred_element_type=jnp.float32
-        )
-        out_ref[span, :] = total.astype(out_ref.dtype)
+    for part in range(1, PARTS):
+        for copy in vectors[part * C : (part + 1) * C] + books[part * C : (part + 1) * C]:
+            copy.start()
+    for part in range(PARTS):
+        for copy in vectors[part * C : (part + 1) * C]:
+            copy.wait()
+        held = vector_ref[part].reshape(C * Z * HALF, width)
+        total = lax.dot_general(
+            assigned_ref[...], held, NN, preferred_element_type=jnp.float32
+        )
+        if part == 0:
+            tables.wait()
+        for copy in books[part * C : (part + 1) * C]:
+            copy.wait()
+        held = book_ref[part].reshape(C * Z * OWN, width)
+        total -= lax.dot_general(
+            table_ref[...], held, NN, preferred_element_type=jnp.float32
+        )
+        out_ref[:, part * width : (part + 1) * width] = total.astype(out_ref.dtype)
 
 
 def merge(rows, assigned, counts):
     features = rows.shape[-1]
     whole = pl.BlockSpec(memory_space=pltpu.VMEM)
+    placed = pl.BlockSpec(memory_space=pltpu.HBM)
     return pl.pallas_call(
         merge_kernel,
-        in_specs=[pl.BlockSpec(memory_space=pl.ANY)] + [whole] * (1 + X),
+        in_specs=[placed, placed, whole],
         out_specs=whole,
         out_shape=jax.ShapeDtypeStruct((X * PLANE, features), jnp.bfloat16),
         scratch_shapes=[
-            pltpu.VMEM((C, Z, OWN, features), jnp.bfloat16),
-            pltpu.VMEM((C, Z, HALF, features), jnp.bfloat16),
-            pltpu.VMEM((X * PLANE, features), jnp.float32),
-            pltpu.SemaphoreType.DMA((2 * C,)),
+            pltpu.VMEM(counts.shape, counts.dtype),
+            pltpu.VMEM((PARTS, C, Z, OWN, features // PARTS), jnp.bfloat16),
+            pltpu.VMEM((PARTS, C, Z, HALF, features // PARTS), jnp.bfloat16),
+            pltpu.SemaphoreType.DMA((2 * C * PARTS + 1,)),
         ],
+        compiler_params=pltpu.CompilerParams(vmem_limit_bytes=28 << 20),
         name="merge",
-    )(rows, assigned, *counts)
+    )(*(pltpu.with_memory_space_constraint(a, pltpu.HBM) for a in (rows, counts)), assigned)
 
 
 def gram_kernel(book_ref, start_ref, row_ref, codes_ref, out_ref):
@@ -182,6 +199,7 @@
             out_specs=pl.BlockSpec((OWN, width), lambda g, b, s: (0, g)),
         ),
         out_shape=jax.ShapeDtypeStruct((OWN, P_SIZE * BLK), jnp.float32),
+        compiler_params=pltpu.CompilerParams(vmem_limit_bytes=12 << 20),
         name="gram_counts",
     )(partner_book, partner_start, row_index, tuples)
 
@@ -220,7 +238,7 @@
     mine = lax.dynamic_slice_in_dim(vectors, 2 * HALF * x + HALF * core, HALF, 0)
     piece = jnp.concatenate([codebook[0], mine])
     rows = lax.all_gather(piece, ("z", "core")).reshape(Z, C, OWN + HALF, features)
-    all_codes = gather_codes(codes).astype(jnp.int32)
+    all_codes = gather_codes(codes, book)
     local = by_parity(all_codes, core) - PLANE * z
     tuples = compact(all_codes, local)
     tuples = tuples.reshape(X, tuples.shape[1], -1)
@@ -228,7 +246,7 @@
     ids = jnp.arange(PLANE, dtype=jnp.int32)[None, :, None]
     assigned = (vector_rows(all_codes, z, y, x, core) == ids).astype(jnp.bfloat16)
     assigned = assigned.reshape(X * PLANE, -1)
-    counts = [pair_counts(row_index[i], column_index[i]) for i in range(X)]
+    counts = pair_counts(row_index, column_index)
     held = lax.dynamic_index_in_dim(tuples, x, 0, keepdims=False)
     held = held.reshape(X * C, -1, Y, CAP)
     held = lax.dynamic_index_in_dim(held, y, 2, keepdims=False).reshape(X * C, -1)
@@ -238,13 +256,14 @@
     gram = gram_counts(partner // KB, partner % KB * BLK, own_row, held)
     matched = own_row == jnp.arange(OWN, dtype=jnp.int32)[:, None]
     code_count = jnp.sum(matched.astype(jnp.float32), axis=1)
-    assigned, gram, code_count = lax.optimization_barrier((assigned, gram, code_count))
+    divisor = jnp.broadcast_to(code_count[:, None] + 2.0, (OWN, features))
+    current = codebook[0].astype(jnp.float32)
+    base = current - 2.0 * current / divisor
+    assigned, gram, divisor, base = lax.optimization_barrier((assigned, gram, divisor, base))
     partial = merge(rows, assigned, counts).reshape(X * Y, OWN, features)
     received = lax.all_to_all(partial, ("x", "y"), split_axis=0, concat_axis=0, tiled=True)
     right_side = jnp.sum(received.astype(jnp.float32), axis=0)
-    current = codebook[0].astype(jnp.float32)
-    updated = current + (right_side - 2.0 * current) / (code_count[:, None] + 2.0)
-    return updated[None], gram[None]
+    return (base + right_side / divisor)[None], gram[None]
 
 
 def solution(mesh):

time: 158 us -> 152 us (0.962)
  blocking collectives: 0 us -> 67.2 us
  waiting for transfers between devices: 55.6 us -> 4.92 us
  starting transfers between devices: 26.1 us -> 4.83 us
  Pallas kernels: 39.3 us -> 35 us
  local copies, waits for them, and re-layouts: 10 us -> 13.7 us
    all_to_all x0 -> x2, blocking collectives: none -> 67.2 us  [the longest x1 33.6 us: shards(): lax.all_to_all(partial, ('x', 'y'), split_axis=0, concat_axis=0, tiled=True)]
    all_to_all x2 -> x1, waiting for transfers between devices: 51.7 us -> 4.91 us  [gather_codes(): lax.all_to_all(copies, ('x', 'core'), split_axis=0, concat_axis=0, tiled=...]
    all_to_all x2 -> x1, starting transfers between devices: 26.1 us -> 4.8 us  [gather_codes(): lax.all_to_all(copies, ('x', 'core'), split_axis=0, concat_axis=0, tiled=...]
    all_gather x1, waiting for transfers between devices: 3.88 us -> 0.01 us  [shards(): lax.all_gather(piece, ('z', 'core')).reshape(Z, C, OWN + HALF, features)]
    pallas_call x5 -> x2, Pallas kernels: 32.6 us -> 29.2 us  [the longest x1 15.7 us: merge(): pl.pallas_call(merge_kernel, in_specs=[placed, placed, whole], out_specs=...]
    unnamed x13 -> x16, local copies, waits for them, and re-layouts: 1.1 us -> 3.15 us
    another operation x2, local copies, waits for them, and re-layouts: 0.04 us -> 1.73 us  [slot_indices(): jnp.stack([lax.dynamic_index_in_dim(tuples[i], i * C + core, 0, keepdims=...]
  transfers between devices with their start and end apart: 3 -> 2, of which waited for: 3 -> 1; matrix products, arithmetic and copies ran while one was open for 11% -> 12% of each run, Pallas kernels for 17% -> 13%
where the time goes in v5:
time: 152 us; the launch traced here: 150 us
  blocking collectives  67.2 us (44%)
  Pallas kernels  35 us (23%)
  between operations  14.4 us (9%)
  local copies, waits for them, and re-layouts  13.7 us (9%)
  other arithmetic  7.75 us (5%)
  waiting for transfers between devices  4.92 us (3%)
  starting transfers between devices  4.83 us (3%)
  matrix products  1.95 us (1%)
    all_to_all x1, blocking collectives, shards(): lax.all_to_all(partial, ('x', 'y'), split_axis=0, concat_axis=0, tiled=True)  33.6 us
    all_to_all x1, blocking collectives, gather_codes(): lax.all_to_all(copies, ('z', 'y'), split_axis=0, concat_axis=0, tiled=True)  33.6 us
    pallas_call x1, Pallas kernels, merge(): pl.pallas_call(merge_kernel, in_specs=[placed, placed, whole], out_specs=...  15.7 us
    pallas_call x1, Pallas kernels, pair_counts(): pl.pallas_call(pair_kernel, grid=(books, slots // CHUNK), in_specs=[pl.Bl...  13.5 us
    pallas_call x1, Pallas kernels, gram_counts(): pl.pallas_call(gram_kernel, grid_spec=pltpu.PrefetchScalarGridSpec(num_sc...  5.81 us
    all_to_all x1, waiting for transfers between devices, gather_codes(): lax.all_to_all(copies, ('x', 'core'), split_axis=0, concat_axis=0, tiled=...  4.91 us
    all_to_all x1, starting transfers between devices, gather_codes(): lax.all_to_all(copies, ('x', 'core'), split_axis=0, concat_axis=0, tiled=...  4.8 us
    unnamed x16, local copies, waits for them, and re-layouts  3.15 us
  transfers between devices with their start and end apart: 2, of which 1 were waited for; matrix products, arithmetic and copies ran while one was open for 12% of the time, Pallas kernels for 13%

profile of v5, /device:TPU:6, one launch (start us, length us, event | category | flops | bytes accessed | tf_op | source)
XLA Modules:
  0.0 149.7 jit_solution(2560952106071032587)
XLA Ops:
  7.2 1.0 copy-done
  8.2 1.6 %pad_maximum_fusion = bf16[96,1024]{1,0:T(8,128)(2,1)} fusion(bf16[32,1024]{1,0:T(8,128)(2,1)S(1)} %constant_dynamic-slice_fusion, bf16[64,1024]{1,0:T(8,128)(2,1)} %bitcast.79), kind=kLoop, calls=%fused_computation.43 | loop fusion | flops 393216 | bytes 393216 | tf_op jit(solution)/shard_map/concatenate | solution.py:239
  9.8 0.7 fusion.25
  10.6 0.5 broadcast.157
  11.1 0.8 reduce.8
  12.0 33.6 %all_to_all.15 = s16[64,2,128]{2,1,0:T(2,128)(2,1)S(1)} all-to-all(s16[64,2,128]{2,1,0:T(2,128)(2,1)S(1)} %reshape.249), channel_id=1, replica_groups=mesh['z'=16,'y'=4,'x'=4,'core'=2] {'z','y'}, dimensions={0} | all-to-all | bytes 65536 | tf_op jit(solution)/shard_map/all_to_all | solution.py:26
  45.6 0.7 broadcast_in_dim.69
  46.3 4.8 %all-to-all-start.1 = ((s16[8,64,256]{2,1,0:T(8,128)(2,1)}), s16[8,64,256]{2,1,0:T(8,128)(2,1)S(1)}, u32[]{:S(2)}, u32[]{:S(2)}) async-start(s16[8,64,256]{2,1,0:T(8,128)(2,1)} %broadcast_in_dim.69), calls=%async_computation.1 | async-start | bytes 524288 | tf_op jit(solution)/shard_map/all_to_all | solution.py:29
  51.5 0.2 dynamic-slice_reduce_fusion.1
  51.7 4.9 %all-to-all-done.1 = s16[8,64,256]{2,1,0:T(8,128)(2,1)S(1)} async-done(((s16[8,64,256]{2,1,0:T(8,128)(2,1)}), s16[8,64,256]{2,1,0:T(8,128)(2,1)S(1)}, u32[]{:S(2)}, u32[]{:S(2)}) %all-to-all-start.1) | async-done | bytes 262176 | tf_op jit(solution)/shard_map/all_to_all | solution.py:29
  56.6 0.2 fusion.21
  56.8 0.3 reshape.229
  57.1 1.4 and_select_fusion
  58.5 0.1 constant_dynamic-slice_fusion.3
  58.7 0.1 sub.84
  58.8 0.1 sub.86
  58.9 0.3 eq.107
  59.2 0.4 eq.108
  59.6 0.6 fusion.11
  60.2 0.4 fusion.4
  60.6 1.6 %fusion.5 = s32[64,17,128]{2,1,0:T(8,128)S(1)} fusion(s32[128]{0:T(128)S(1)} %eq.120, s32[64,16,256]{2,1,0:T(8,128)S(1)} %fusion.4, bf16[64,8,256]{2,1,0:T(8,128)(2,1)S(1)} %get-tuple-element.15, bf16[64,8,256]{2,1,0:T(8,128)(2,1)S(1)} %get-tuple-element.14, bf16[17]{0:T(256)(128)(2,1)S(1)} %pad.8.clone), kind=kOutput, calls=%fused_computation.9 | convolution fusion | flops 75210752 | bytes 2130466 | tf_op jit(solution)/shard_map/dot_general | solution.py:53
  62.3 0.2 copy.47
  62.5 0.4 copy.48
  62.9 0.1 copy.49
  63.0 0.1 squeeze.32
  63.2 0.1 copy.52
  63.3 0.1 squeeze.35
  63.5 0.1 copy.51
  63.6 0.8 squeeze.34
  64.4 0.1 copy.50
  64.5 0.8 squeeze.33
  65.3 0.5 reshape.231
  65.8 1.2 reshape.232
  67.0 0.8 dynamic-slice_reduce_fusion
  67.8 0.2 reshape.233.codes_ref
  68.0 0.4 fusion.3.assigned_ref
  68.4 5.8 %gram_counts.1 = f32[64,8192]{1,0:T(8,128)} custom-call(s32[64]{0:T(128)S(1)} %get-tuple-element.19.book_ref, s32[64]{0:T(128)S(1)} %get-tuple-element.18.start_ref, s32[1,512]{1,0:T(1,128)S(1)} %compare_select_fusion.6.row_ref, s32[8,512]{1,0:T(8,128)S(1)} %reshape.233.codes_ref), custom_call_target="tpu_custom_call" | custom-call | tf_op jit(solution)/shard_map/gram_counts/pallas_call | solution.py:190
  74.2 0.1 convert_reduce_fusion.1
  74.4 0.1 convert_subtract_fusion
  74.6 0.9 dynamic-slice_bitcast_fusion
  75.4 0.9 dynamic-slice_bitcast_fusion.2
  76.3 0.5 and_select_fusion.3.column_ref
  76.8 13.5 %pair_counts.1.counts_ref = bf16[1024,2048]{1,0:T(8,128)(2,1)S(1)} custom-call(s32[4,1,2048]{2,1,0:T(1,128)S(1)} %compare_select_fusion.5.row_ref, s32[4,2,2048]{2,1,0:T(2,128)S(1)} %and_select_fusion.3.column_ref), custom_call_target="tpu_custom_call" | custom-call | tf_op jit(solution)/shard_map/pair_counts/pallas_call | solution.py:91
  90.3 2.0 %copy-done.1 = bf16[1024,2048]{1,0:T(8,128)(2,1)} copy-done((bf16[1024,2048]{1,0:T(8,128)(2,1)}, bf16[1024,2048]{1,0:T(8,128)(2,1)S(1)}, u32[]{:S(2)}) %copy-start.1) | copy-done | bytes 4194328
  92.4 15.7 %merge.1 = bf16[1024,1024]{1,0:T(8,128)(2,1)S(1)} custom-call(bf16[16,2,96,1024]{3,2,1,0:T(8,128)(2,1)} %bitcast.73, bf16[1024,2048]{1,0:T(8,128)(2,1)} %copy-done.1, bf16[1024,1024]{1,0:T(8,128)(2,1)S(1)} %fusion.3.assigned_ref), custom_call_target="tpu_custom_call" | custom-call | tf_op jit(solution)/shard_map/merge/pallas_call | solution.py:159
  108.1 33.6 %all_to_all.16 = bf16[16,64,1024]{2,1,0:T(8,128)(2,1)S(1)} all-to-all(bf16[16,64,1024]{2,1,0:T(8,128)(2,1)S(1)} %bitcast.71), channel_id=1, replica_groups=mesh['z'=16,'y'=4,'x'=4,'core'=2] {'x','y'}, dimensions={0} | all-to-all | bytes 4194304 | tf_op jit(solution)/shard_map/all_to_all | solution.py:264
  141.7 0.4 convert_reduce_fusion
  142.1 0.8 add_bitcast_fusion
  (37 shorter events, 0.9 us)
Async XLA Ops:
  7.2 1.0 copy-start
  7.2 44.3 %copy-start.3 = (s32[256,64]{0,1:T(8,128)S(1)}, s32[256,64]{0,1:T(8,128)}, u32[]{:S(2)}) copy-start(s32[256,64]{0,1:T(8,128)} %param.7) | copy-start | bytes 196612
  7.2 85.2 %all-gather.3.cloned.1.call-start = ((), (), s32[]{:S(2)}) async-start(), calls=%async_computation.3 | async-start | bytes 6488064 | tf_op jit(solution)/shard_map/all_gather | solution.py:240
  46.3 10.3 %all-to-all-start.1 = ((s16[8,64,256]{2,1,0:T(8,128)(2,1)}), s16[8,64,256]{2,1,0:T(8,128)(2,1)S(1)}, u32[]{:S(2)}, u32[]{:S(2)}) async-start(s16[8,64,256]{2,1,0:T(8,128)(2,1)} %broadcast_in_dim.69), calls=%async_computation.1 | async-start | bytes 524288 | tf_op jit(solution)/shard_map/all_to_all | solution.py:29
  68.0 6.4 %copy-start.2 = (bf16[1,64,1024]{2,1,0:T(8,128)(2,1)S(1)}, bf16[1,64,1024]{2,1,0:T(8,128)(2,1)}, u32[]{:S(2)}) copy-start(bf16[1,64,1024]{2,1,0:T(8,128)(2,1)} %param.6) | copy-start | bytes 393220
  90.3 2.0 %copy-start.1 = (bf16[1024,2048]{1,0:T(8,128)(2,1)}, bf16[1024,2048]{1,0:T(8,128)(2,1)S(1)}, u32[]{:S(2)}) copy-start(bf16[1024,2048]{1,0:T(8,128)(2,1)S(1)} %pair_counts.1.counts_ref) | copy-start | bytes 12582916
Sparse Core Ops, SparseCore 0:
  10.1 82.1 all-gather.2

commit v6 on v5

v6 whole, which is shorter than its diff:
```python
import jax
import jax.numpy as jnp
from jax import lax
from jax.experimental import pallas as pl
from jax.experimental.pallas import tpu as pltpu
from jax.sharding import Mesh, PartitionSpec as P

K = 4096
BLK = 128
P_SIZE = 64
KB = 32
Z, Y, X, C = 16, 4, 4, 2
OWN = 64
CAP = 8
HALF = 32
PLANE = Y * OWN
NT = (((1,), (1,)), ((), ()))
NN = (((1,), (0,)), ((), ()))


def gather_codes(codes, book):
    mine = lax.dynamic_slice_in_dim(codes.astype(jnp.int16), book, 1, 0)
    copies = jnp.broadcast_to(mine[None], (Z * Y,) + mine.shape)
    whole = lax.all_to_all(copies, ("z", "y"), split_axis=0, concat_axis=0, tiled=True)
    whole = whole.reshape(Z * Y, codes.shape[1])
    copies = jnp.broadcast_to(whole[None], (X * C,) + whole.shape)
    books = lax.all_to_all(copies, ("x", "core"), split_axis=0, concat_axis=0, tiled=True)
    return books.astype(jnp.int32).transpose(1, 0, 2)


def compact(all_codes, local):
    blocks, codebooks, length = all_codes.shape
    ranges = local // OWN
    hit = ranges[:, :, None, :] == jnp.arange(Y, dtype=jnp.int32)[None, None, :, None]
    hit = hit.reshape(blocks, X * Y, length)
    lane = jnp.arange(length)
    upper = (lane[:, None] < lane[None, :]).astype(jnp.bfloat16)
    rank = lax.dot_general(
        hit.astype(jnp.bfloat16).reshape(blocks * X * Y, length),
        upper,
        NN,
        preferred_element_type=jnp.float32,
    )
    rank = jnp.where(hit, rank.reshape(hit.shape).astype(jnp.int32), -1)
    slots = jnp.arange(CAP, dtype=jnp.int32)
    chosen = (rank[:, :, None, :] == slots[None, None, :, None]).astype(jnp.bfloat16)
    chosen = chosen.reshape(blocks, X * Y * CAP, length)
    ones = jnp.ones_like(all_codes[:, :1])
    digits = jnp.concatenate([all_codes // BLK, all_codes % BLK, ones], axis=1)
    digits = digits.astype(jnp.bfloat16)
    packed = lax.dot_general(
        digits, chosen, (((2,), (2,)), ((0,), (0,))), preferred_element_type=jnp.float32
    ).astype(jnp.int32)
    high, low = packed[:, :codebooks], packed[:, codebooks : 2 * codebooks]
    tuples = jnp.where(packed[:, 2 * codebooks :] > 0, high * BLK + low, -1)
    tuples = tuples.reshape(blocks, codebooks, X, Y * CAP)
    return tuples.transpose(2, 1, 0, 3)


def match(index_row, count):
    ids = lax.broadcasted_iota(jnp.int32, (count, index_row.shape[1]), 0)
    return jnp.where(ids == index_row, 1.0, 0.0).astype(jnp.bfloat16)


def weight_kernel(row_ref, column_ref, vector_ref, out_ref):
    member = match(row_ref[0], PLANE)
    slots = member.shape[1]
    group = 4
    width = group * (OWN + HALF)
    for first in range(0, Z * C, group):
        tables = []
        for unit in range(first, first + group):
            z, core = divmod(unit, C)
            tables.append(match(column_ref[0, core : core + 1, :] - z * OWN, OWN))
            tables.append(jnp.zeros((HALF, slots), jnp.bfloat16))
        counts = lax.dot_general(
            member, jnp.concatenate(tables), NT, preferred_element_type=jnp.float32
        )
        lanes = slice(first // group * width, (first // group + 1) * width)
        assigned = match(vector_ref[0, :, lanes], PLANE).astype(jnp.float32)
        out_ref[:, lanes] = (assigned - counts).astype(out_ref.dtype)


def weights(row_index, column_index, vector_index):
    books, _, slots = row_index.shape
    columns = vector_index.shape[2]
    return pl.pallas_call(
        weight_kernel,
        grid=(books,),
        in_specs=[
            pl.BlockSpec((1, 1, slots), lambda i: (i, 0, 0)),
            pl.BlockSpec((1, C, slots), lambda i: (i, 0, 0)),
            pl.BlockSpec((1, 1, columns), lambda i: (i, 0, 0)),
        ],
        out_specs=pl.BlockSpec((PLANE, columns), lambda i: (i, 0)),
        out_shape=jax.ShapeDtypeStruct((books * PLANE, columns), jnp.bfloat16),
        compiler_params=pltpu.CompilerParams(vmem_limit_bytes=56 << 20),
        name="weights",
    )(row_index, column_index, vector_index)


def gram_kernel(book_ref, start_ref, row_ref, codes_ref, out_ref):
    group = pl.program_id(0)
    member = match(row_ref[...], OWN)
    per_step = out_ref.shape[1] // BLK
    for j in range(per_step):
        p = group * per_step + j
        offset = codes_ref[pl.ds(book_ref[p], 1), :] - start_ref[p]
        out_ref[:, j * BLK : (j + 1) * BLK] = lax.dot_general(
            member, match(offset, BLK), NT, preferred_element_type=jnp.float32
        )


def gram_counts(partner_book, partner_start, row_index, tuples):
    slots = tuples.shape[1]
    width = 8 * BLK
    return pl.pallas_call(
        gram_kernel,
        grid_spec=pltpu.PrefetchScalarGridSpec(
            num_scalar_prefetch=2,
            grid=(P_SIZE * BLK // width,),
            in_specs=[
                pl.BlockSpec((1, slots), lambda g, b, s: (0, 0)),
                pl.BlockSpec(tuples.shape, lambda g, b, s: (0, 0)),
            ],
            out_specs=pl.BlockSpec((OWN, width), lambda g, b, s: (0, g)),
        ),
        out_shape=jax.ShapeDtypeStruct((OWN, P_SIZE * BLK), jnp.float32),
        compiler_params=pltpu.CompilerParams(vmem_limit_bytes=12 << 20),
        name="gram_counts",
    )(partner_book, partner_start, row_index, tuples)


def by_parity(rows, core):
    shape = rows.shape
    grouped = rows.reshape(shape[:-2] + (X, C, shape[-1]))
    return lax.dynamic_index_in_dim(grouped, core, len(shape) - 1, keepdims=False)


def slot_indices(tuples, z, y, x, core):
    own = jnp.stack(
        [lax.dynamic_index_in_dim(tuples[i], i * C + core, 0, keepdims=True) for i in range(X)]
    )
    row_index = jnp.where(own >= 0, own - PLANE * z, -1)
    code = lax.dynamic_slice_in_dim(tuples, x * C, C, 1)
    place = code // PLANE * OWN + code % OWN
    inside = (code >= 0) & (code // OWN % Y == y)
    return row_index, jnp.where(inside, place, -1)


def vector_rows(all_codes, z, y, x, core):
    mine = all_codes.reshape(Z, Y, X * C, -1)
    mine = lax.dynamic_index_in_dim(mine, y, 1, keepdims=False)
    portion = lax.dynamic_slice_in_dim(mine, C * HALF * x, C * HALF, 2)
    portion = by_parity(portion, core).reshape(Z, X, C, HALF) - PLANE * z
    portion = jnp.pad(
        portion.transpose(1, 0, 2, 3), ((0, 0), (0, 0), (0, 0), (OWN, 0)), constant_values=-1
    )
    return portion.reshape(X, 1, Z * C * (OWN + HALF))


def shards(vectors, codes, codebook, pairs):
    z, y = lax.axis_index("z"), lax.axis_index("y")
    x, core = lax.axis_index("x"), lax.axis_index("core")
    features = codebook.shape[2]
    owner = z * Y + y
    book = x * C + core
    mine = lax.dynamic_slice_in_dim(vectors, 2 * HALF * x + HALF * core, HALF, 0)
    piece = jnp.concatenate([codebook[0], mine])
    rows = lax.all_gather(piece, ("z", "core"), tiled=True)
    all_codes = gather_codes(codes, book)
    local = by_parity(all_codes, core) - PLANE * z
    tuples = compact(all_codes, local)
    tuples = tuples.reshape(X, tuples.shape[1], -1)
    row_index, column_index = slot_indices(tuples, z, y, x, core)
    table = weights(row_index, column_index, vector_rows(all_codes, z, y, x, core))
    held = lax.dynamic_index_in_dim(tuples, x, 0, keepdims=False)
    held = held.reshape(X * C, -1, Y, CAP)
    held = lax.dynamic_index_in_dim(held, y, 2, keepdims=False).reshape(X * C, -1)
    own_row = lax.dynamic_index_in_dim(held, book, 0, keepdims=True)
    own_row = jnp.where(own_row >= 0, own_row - owner * OWN, -1)
    matched = own_row == jnp.arange(OWN, dtype=jnp.int32)[:, None]
    code_count = jnp.sum(matched.astype(jnp.float32), axis=1)
    divisor = jnp.broadcast_to(code_count[:, None] + 2.0, (OWN, features))
    current = codebook[0].astype(jnp.float32)
    base = current - 2.0 * current / divisor
    table, divisor, base = lax.optimization_barrier((table, divisor, base))
    partial = lax.dot_general(table, rows, NN, preferred_element_type=jnp.float32)
    partial = partial.astype(jnp.bfloat16)
    partial, held, own_row = lax.optimization_barrier((partial, held, own_row))
    partial = partial.reshape(X * Y, OWN, features)
    received = lax.all_to_all(partial, ("x", "y"), split_axis=0, concat_axis=0, tiled=True)
    partner = lax.dynamic_index_in_dim(pairs, (book * K + owner * OWN) // BLK, 0, keepdims=False)
    gram = gram_counts(partner // KB, partner % KB * BLK, own_row, held)
    right_side = jnp.sum(received.astype(jnp.float32), axis=0)
    return (base + right_side / divisor)[None], gram[None]


def solution(mesh):
    grid = Mesh(mesh.devices.reshape(Z, Y, X, C), ("z", "y", "x", "core"))
    rows, books = ("z", "y"), ("x", "core")
    in_specs = (P(rows, None), P(None, rows), P(books, rows, None), P())
    out_specs = (P(books, rows, None), P(books, rows, None))
    return jax.shard_map(shards, mesh=grid, in_specs=in_specs, out_specs=out_specs, check_vma=False)
```

time: 152 us -> 150 us (0.987)
  blocking collectives: 67.2 us -> 33.2 us
  waiting for transfers between devices: 4.92 us -> 30.5 us
  matrix products: 1.95 us -> 13.5 us
  Pallas kernels: 35 us -> 25.8 us
  starting transfers between devices: 4.83 us -> 13 us
  local copies, waits for them, and re-layouts: 13.7 us -> 9.51 us
    all_to_all x1 -> x0, blocking collectives: 33.6 us -> none  [shards(): lax.all_to_all(partial, ('x', 'y'), split_axis=0, concat_axis=0, tiled=True)]
    all_to_all x0 -> x1, waiting for transfers between devices: none -> 22.6 us  [shards(): lax.all_to_all(partial, ('x', 'y'), split_axis=0, concat_axis=0, tiled=True)]
    dot_general x0 -> x1, matrix products: none -> 11.6 us  [shards(): lax.dot_general(table, rows, NN, preferred_element_type=jnp.float32)]
    pallas_call x2 -> x1, Pallas kernels: 29.2 us -> 20 us  [weights(): pl.pallas_call(weight_kernel, grid=(books,), in_specs=[pl.BlockSpec((1, 1...]
    all_to_all x0 -> x1, starting transfers between devices: none -> 8.2 us  [shards(): lax.all_to_all(partial, ('x', 'y'), split_axis=0, concat_axis=0, tiled=True)]
    all_gather x1, waiting for transfers between devices: 0.01 us -> 2.78 us  [shards(): rows = lax.all_gather(piece, ('z', 'core'), tiled=True)]
    unnamed x16 -> x12, local copies, waits for them, and re-layouts: 3.15 us -> 1.13 us
    another operation x2, local copies, waits for them, and re-layouts: 1.73 us -> 0.04 us  [slot_indices(): jnp.stack([lax.dynamic_index_in_dim(tuples[i], i * C + core, 0, keepdims=...]
  transfers between devices with their start and end apart: 2 -> 3, of which waited for: 1 -> 3; matrix products, arithmetic and copies ran while one was open for 12% -> 11% of each run, Pallas kernels for 13% -> 17%
where the time goes in v6:
time: 150 us; the launch traced here: 149 us
  blocking collectives  33.2 us (22%)
  waiting for transfers between devices  30.5 us (20%)
  Pallas kernels  25.8 us (17%)
  between operations  14.3 us (10%)
  matrix products  13.5 us (9%)
  starting transfers between devices  13 us (9%)
  local copies, waits for them, and re-layouts  9.51 us (6%)
  other arithmetic  8.57 us (6%)
    all_to_all x1, blocking collectives, gather_codes(): lax.all_to_all(copies, ('z', 'y'), split_axis=0, concat_axis=0, tiled=True)  33.2 us
    all_to_all x1, waiting for transfers between devices, shards(): lax.all_to_all(partial, ('x', 'y'), split_axis=0, concat_axis=0, tiled=True)  22.6 us
    pallas_call x1, Pallas kernels, weights(): pl.pallas_call(weight_kernel, grid=(books,), in_specs=[pl.BlockSpec((1, 1...  20 us
    dot_general x1, matrix products, shards(): lax.dot_general(table, rows, NN, preferred_element_type=jnp.float32)  11.6 us
    all_to_all x1, starting transfers between devices, shards(): lax.all_to_all(partial, ('x', 'y'), split_axis=0, concat_axis=0, tiled=True)  8.2 us
    pallas_call x1, Pallas kernels, gram_counts(): pl.pallas_call(gram_kernel, grid_spec=pltpu.PrefetchScalarGridSpec(num_sc...  5.82 us
    all_to_all x1, waiting for transfers between devices, gather_codes(): lax.all_to_all(copies, ('x', 'core'), split_axis=0, concat_axis=0, tiled=...  5.12 us
    all_to_all x1, starting transfers between devices, gather_codes(): lax.all_to_all(copies, ('x', 'core'), split_axis=0, concat_axis=0, tiled=...  4.79 us
  transfers between devices with their start and end apart: 3, of which 3 were waited for; matrix products, arithmetic and copies ran while one was open for 11% of the time, Pallas kernels for 17%

profile of v6, /device:TPU:6, one launch (start us, length us, event | category | flops | bytes accessed | tf_op | source)
XLA Modules:
  0.0 148.5 jit_solution(12926695157961821890)
XLA Ops:
  7.2 1.0 copy-done
  8.2 1.6 %pad_maximum_fusion = bf16[96,1024]{1,0:T(8,128)(2,1)} fusion(bf16[32,1024]{1,0:T(8,128)(2,1)S(1)} %constant_dynamic-slice_fusion, bf16[64,1024]{1,0:T(8,128)(2,1)} %bitcast.70), kind=kLoop, calls=%fused_computation.42 | loop fusion | flops 393216 | bytes 393216 | tf_op jit(solution)/shard_map/concatenate | solution.py:169
  9.8 0.7 fusion.24
  10.6 0.5 broadcast.147
  11.1 0.8 reduce.8
  12.0 33.2 %all_to_all.15 = s16[64,2,128]{2,1,0:T(2,128)(2,1)S(1)} all-to-all(s16[64,2,128]{2,1,0:T(2,128)(2,1)S(1)} %reshape.234), channel_id=1, replica_groups=mesh['z'=16,'y'=4,'x'=4,'core'=2] {'z','y'}, dimensions={0} | all-to-all | bytes 65536 | tf_op jit(solution)/shard_map/all_to_all | solution.py:24
  45.2 0.7 broadcast_in_dim.68
  45.9 4.8 %all-to-all-start.1 = ((s16[8,64,256]{2,1,0:T(8,128)(2,1)}), s16[8,64,256]{2,1,0:T(8,128)(2,1)S(1)}, u32[]{:S(2)}, u32[]{:S(2)}) async-start(s16[8,64,256]{2,1,0:T(8,128)(2,1)} %broadcast_in_dim.68), calls=%async_computation.1 | async-start | bytes 524288 | tf_op jit(solution)/shard_map/all_to_all | solution.py:27
  51.1 5.1 %all-to-all-done.1 = s16[8,64,256]{2,1,0:T(8,128)(2,1)S(1)} async-done(((s16[8,64,256]{2,1,0:T(8,128)(2,1)}), s16[8,64,256]{2,1,0:T(8,128)(2,1)S(1)}, u32[]{:S(2)}, u32[]{:S(2)}) %all-to-all-start.1) | async-done | bytes 262176 | tf_op jit(solution)/shard_map/all_to_all | solution.py:27
  56.2 0.2 copy_convert_fusion
  56.4 0.1 constant_dynamic-slice_fusion.3
  56.5 0.1 sub.81
  56.6 0.1 pad.4
  56.8 0.8 reshape.219.vector_ref
  57.5 0.3 reshape.214
  57.8 1.4 and_select_fusion
  59.3 0.3 eq.81
  59.6 0.4 eq.82
  60.0 0.6 fusion.10
  60.6 0.4 fusion.3
  61.0 1.6 %fusion.4 = s32[64,17,128]{2,1,0:T(8,128)S(1)} fusion(s32[128]{0:T(128)S(1)} %eq.94, s32[64,16,256]{2,1,0:T(8,128)S(1)} %fusion.3, bf16[64,8,256]{2,1,0:T(8,128)(2,1)S(1)} %get-tuple-element.21, bf16[64,8,256]{2,1,0:T(8,128)(2,1)S(1)} %get-tuple-element.20, bf16[17]{0:T(256)(128)(2,1)S(1)} %pad.13.clone), kind=kOutput, calls=%fused_computation.8 | convolution fusion | flops 75210752 | bytes 2130466 | tf_op jit(solution)/shard_map/dot_general | solution.py:51
  62.7 0.2 copy.35
  62.9 0.4 copy.40
  63.3 0.1 copy.36
  63.4 0.1 squeeze.30
  63.6 0.1 copy.39
  63.7 0.1 squeeze.33
  63.9 0.1 copy.38
  64.0 0.1 squeeze.32
  64.1 0.1 copy.37
  64.3 0.1 squeeze.31
  64.4 0.5 reshape.216
  64.9 1.2 reshape.220
  66.2 0.8 dynamic-slice_reduce_fusion
  67.0 0.2 reshape.221.codes_ref
  67.2 0.6 compare_select_fusion.5.row_ref
  67.9 1.1 and_select_fusion.3.column_ref
  69.0 20.0 %weights.1 = bf16[1024,3072]{1,0:T(8,128)(2,1)} custom-call(s32[4,1,2048]{2,1,0:T(1,128)} %compare_select_fusion.5.row_ref, s32[4,2,2048]{2,1,0:T(2,128)} %and_select_fusion.3.column_ref, s32[4,1,3072]{2,1,0:T(1,128)} %reshape.219.vector_ref), custom_call_target="tpu_custom_call" | custom-call | tf_op jit(solution)/shard_map/weights/pallas_call | solution.py:87
  89.0 0.1 convert_reduce_fusion.1
  89.1 0.1 convert_subtract_fusion
  89.4 2.8 %all-gather.2.cloned.1.call-done = bf16[3072,1024]{1,0:T(8,128)(2,1)} async-done(((bf16[96,1024]{1,0:T(8,128)(2,1)}), bf16[3072,1024]{1,0:T(8,128)(2,1)}) %all-gather.2.cloned.1.call-update) | async-done | bytes 6291472 | tf_op jit(solution)/shard_map/all_gather | solution.py:170
  92.1 11.6 %convolution_convert_fusion = bf16[1024,1024]{1,0:T(8,128)(2,1)} fusion(bf16[1024,3072]{1,0:T(8,128)(2,1)} %weights.1, bf16[3072,1024]{1,0:T(8,128)(2,1)} %all-gather.2.cloned.1.call-done), kind=kOutput, calls=%fused_computation.5 | convolution fusion | flops 6443499520 | bytes 14680064 | tf_op jit(solution)/shard_map/dot_general | solution.py:188
  103.7 8.2 %all-to-all-start.2 = ((bf16[16,64,1024]{2,1,0:T(8,128)(2,1)}), bf16[16,64,1024]{2,1,0:T(8,128)(2,1)S(1)}, u32[]{:S(2)}, u32[]{:S(2)}) async-start(bf16[16,64,1024]{2,1,0:T(8,128)(2,1)} %bitcast.66), calls=%async_computation.2 | async-start | bytes 4194304 | tf_op jit(solution)/shard_map/all_to_all | solution.py:192
  111.9 0.2 dynamic-slice_reduce_fusion.1
  112.1 5.8 %gram_counts.1 = f32[64,8192]{1,0:T(8,128)} custom-call(s32[64]{0:T(128)S(1)} %get-tuple-element.23.book_ref, s32[64]{0:T(128)S(1)} %get-tuple-element.22.start_ref, s32[1,512]{1,0:T(1,128)S(1)} %compare_select_fusion.6.row_ref, s32[8,512]{1,0:T(8,128)S(1)} %reshape.221.codes_ref), custom_call_target="tpu_custom_call" | custom-call | tf_op jit(solution)/shard_map/gram_counts/pallas_call | solution.py:117
  118.0 22.6 %all-to-all-done.2 = bf16[16,64,1024]{2,1,0:T(8,128)(2,1)S(1)} async-done(((bf16[16,64,1024]{2,1,0:T(8,128)(2,1)}), bf16[16,64,1024]{2,1,0:T(8,128)(2,1)S(1)}, u32[]{:S(2)}, u32[]{:S(2)}) %all-to-all-start.2) | async-done | bytes 2097184 | tf_op jit(solution)/shard_map/all_to_all | solution.py:192
  140.6 0.4 convert_reduce_fusion
  140.9 0.8 add_bitcast_fusion
  (33 shorter events, 0.9 us)
Async XLA Ops:
  7.2 1.0 copy-start
  7.2 85.0 %all-gather.2.cloned.1.call-start = ((), (), s32[]{:S(2)}) async-start(), calls=%async_computation.3 | async-start | bytes 6488064 | tf_op jit(solution)/shard_map/all_gather | solution.py:170
  45.9 10.3 %all-to-all-start.1 = ((s16[8,64,256]{2,1,0:T(8,128)(2,1)}), s16[8,64,256]{2,1,0:T(8,128)(2,1)S(1)}, u32[]{:S(2)}, u32[]{:S(2)}) async-start(s16[8,64,256]{2,1,0:T(8,128)(2,1)} %broadcast_in_dim.68), calls=%async_computation.1 | async-start | bytes 524288 | tf_op jit(solution)/shard_map/all_to_all | solution.py:27
  64.9 24.2 %copy-start.1 = (bf16[1,64,1024]{2,1,0:T(8,128)(2,1)S(1)}, bf16[1,64,1024]{2,1,0:T(8,128)(2,1)}, u32[]{:S(2)}) copy-start(bf16[1,64,1024]{2,1,0:T(8,128)(2,1)} %param.6) | copy-start | bytes 393220
  103.7 8.2 %copy-start.2 = (s32[256,64]{0,1:T(8,128)S(1)}, s32[256,64]{0,1:T(8,128)}, u32[]{:S(2)}) copy-start(s32[256,64]{0,1:T(8,128)} %param.7) | copy-start | bytes 196612
  103.7 36.8 %all-to-all-start.2 = ((bf16[16,64,1024]{2,1,0:T(8,128)(2,1)}), bf16[16,64,1024]{2,1,0:T(8,128)(2,1)S(1)}, u32[]{:S(2)}, u32[]{:S(2)}) async-start(bf16[16,64,1024]{2,1,0:T(8,128)(2,1)} %bitcast.66), calls=%async_computation.2 | async-start | bytes 4194304 | tf_op jit(solution)/shard_map/all_to_all | solution.py:192
Sparse Core Ops, SparseCore 0:
  10.7 81.3 all-gather.1

commit v7 on v6

--- a/solution.py
+++ b/solution.py
@@ -12,6 +12,7 @@
 Z, Y, X, C = 16, 4, 4, 2
 OWN = 64
 CAP = 8
+PRODUCT_VMEM = 56 << 20
 HALF = 32
 PLANE = Y * OWN
 NT = (((1,), (1,)), ((), ()))
@@ -64,21 +65,14 @@
 
 def weight_kernel(row_ref, column_ref, vector_ref, out_ref):
     member = match(row_ref[0], PLANE)
-    slots = member.shape[1]
-    group = 4
-    width = group * (OWN + HALF)
-    for first in range(0, Z * C, group):
-        tables = []
-        for unit in range(first, first + group):
-            z, core = divmod(unit, C)
-            tables.append(match(column_ref[0, core : core + 1, :] - z * OWN, OWN))
-            tables.append(jnp.zeros((HALF, slots), jnp.bfloat16))
-        counts = lax.dot_general(
-            member, jnp.concatenate(tables), NT, preferred_element_type=jnp.float32
-        )
-        lanes = slice(first // group * width, (first // group + 1) * width)
-        assigned = match(vector_ref[0, :, lanes], PLANE).astype(jnp.float32)
-        out_ref[:, lanes] = (assigned - counts).astype(out_ref.dtype)
+    out_ref[...] = match(vector_ref[0], PLANE)
+    for core in range(C):
+        table = match(column_ref[0, core : core + 1, :], Z * OWN)
+        counts = lax.dot_general(member, table, NT, preferred_element_type=jnp.float32)
+        counts = (-counts).astype(out_ref.dtype)
+        for z in range(Z):
+            start = (z * C + core) * (OWN + HALF)
+            out_ref[:, start : start + OWN] = counts[:, z * OWN : (z + 1) * OWN]
 
 
 def weights(row_index, column_index, vector_index):
@@ -97,6 +91,55 @@
         compiler_params=pltpu.CompilerParams(vmem_limit_bytes=56 << 20),
         name="weights",
     )(row_index, column_index, vector_index)
+
+
+def product_kernel(left_ref, right_ref, out_ref):
+    total = lax.dot_general(
+        left_ref[...], right_ref[...], NN, preferred_element_type=jnp.float32
+    )
+    out_ref[...] = total.astype(out_ref.dtype)
+
+
+def product(left, right):
+    rows, depth = left.shape
+    features = right.shape[1]
+    width = features // 4
+    return pl.pallas_call(
+        product_kernel,
+        grid=(features // width,),
+        in_specs=[
+            pl.BlockSpec((rows, depth), lambda n: (0, 0)),
+            pl.BlockSpec((depth, width), lambda n: (0, n)),
+        ],
+        out_specs=pl.BlockSpec((rows, width), lambda n: (0, n)),
+        out_shape=jax.ShapeDtypeStruct((rows, features), jnp.bfloat16),
+        compiler_params=pltpu.CompilerParams(vmem_limit_bytes=PRODUCT_VMEM),
+        name="product",
+    )(left, right)
+
+
+def piece_kernel(index_ref, book_ref, vector_ref, out_ref):
+    out_ref[:OWN, :] = book_ref[...]
+    out_ref[OWN:, :] = vector_ref[...]
+
+
+def make_piece(book_rows, vectors, index):
+    features = vectors.shape[1]
+    return pl.pallas_call(
+        piece_kernel,
+        grid_spec=pltpu.PrefetchScalarGridSpec(
+            num_scalar_prefetch=1,
+            grid=(1,),
+            in_specs=[
+                pl.BlockSpec((OWN, features), lambda i, n: (0, 0)),
+                pl.BlockSpec((HALF, features), lambda i, n: (n[0], 0)),
+            ],
+            out_specs=pl.BlockSpec((OWN + HALF, features), lambda i, n: (0, 0)),
+        ),
+        out_shape=jax.ShapeDtypeStruct((OWN + HALF, features), jnp.bfloat16),
+        compiler_params=pltpu.CompilerParams(vmem_limit_bytes=4 << 20),
+        name="make_piece",
+    )(index, book_rows, vectors)
 
 
 def gram_kernel(book_ref, start_ref, row_ref, codes_ref, out_ref):
@@ -165,8 +208,8 @@
     features = codebook.shape[2]
     owner = z * Y + y
     book = x * C + core
-    mine = lax.dynamic_slice_in_dim(vectors, 2 * HALF * x + HALF * core, HALF, 0)
-    piece = jnp.concatenate([codebook[0], mine])
+    stored = (pltpu.with_memory_space_constraint(a, pltpu.HBM) for a in (codebook[0], vectors))
+    piece = make_piece(*stored, book.astype(jnp.int32)[None])
     rows = lax.all_gather(piece, ("z", "core"), tiled=True)
     all_codes = gather_codes(codes, book)
     local = by_parity(all_codes, core) - PLANE * z
@@ -185,8 +228,7 @@
     current = codebook[0].astype(jnp.float32)
     base = current - 2.0 * current / divisor
     table, divisor, base = lax.optimization_barrier((table, divisor, base))
-    partial = lax.dot_general(table, rows, NN, preferred_element_type=jnp.float32)
-    partial = partial.astype(jnp.bfloat16)
+    partial = product(table, rows)
     partial, held, own_row = lax.optimization_barrier((partial, held, own_row))
     partial = partial.reshape(X * Y, OWN, features)
     received = lax.all_to_all(partial, ("x", "y"), split_axis=0, concat_axis=0, tiled=True)

time: 150 us -> 150 us (level)
  matrix products: 13.5 us -> 1.96 us
  waiting for transfers between devices: 30.5 us -> 37.5 us
  Pallas kernels: 25.8 us -> 32.7 us
  other arithmetic: 8.57 us -> 6.97 us
    pallas_call x0 -> x2, Pallas kernels: none -> 12.9 us  [the longest x1 11.3 us: product(): pl.pallas_call(product_kernel, grid=(features // width,), in_specs=[pl.Bl...]
    dot_general x1 -> x0, matrix products: 11.6 us -> none  [shards(): lax.dot_general(table, rows, NN, preferred_element_type=jnp.float32)]
    all_gather x1, waiting for transfers between devices: 2.78 us -> 9.86 us  [shards(): rows = lax.all_gather(piece, ('z', 'core'), tiled=True)]
    pallas_call x1, Pallas kernels: 20 us -> 14 us  [weights(): pl.pallas_call(weight_kernel, grid=(books,), in_specs=[pl.BlockSpec((1, 1...]
    concatenate x1 -> x0, other arithmetic: 1.59 us -> none  [shards(): piece = jnp.concatenate([codebook[0], mine])]
  transfers between devices with their start and end apart: 3 -> 3, of which waited for: 3 -> 3; matrix products, arithmetic and copies ran while one was open for 11% -> 11% of each run, Pallas kernels for 17% -> 13%
where the time goes in v7:
time: 150 us; the launch traced here: 148 us
  waiting for transfers between devices  37.5 us (25%)
  blocking collectives  33.1 us (22%)
  Pallas kernels  32.7 us (22%)
  between operations  14.3 us (10%)
  starting transfers between devices  12.6 us (8%)
  local copies, waits for them, and re-layouts  8.51 us (6%)
  other arithmetic  6.97 us (5%)
  matrix products  1.96 us (1%)
    all_to_all x1, blocking collectives, gather_codes(): lax.all_to_all(copies, ('z', 'y'), split_axis=0, concat_axis=0, tiled=True)  33.1 us
    all_to_all x1, waiting for transfers between devices, shards(): lax.all_to_all(partial, ('x', 'y'), split_axis=0, concat_axis=0, tiled=True)  22.5 us
    pallas_call x1, Pallas kernels, weights(): pl.pallas_call(weight_kernel, grid=(books,), in_specs=[pl.BlockSpec((1, 1...  14 us
    pallas_call x1, Pallas kernels, product(): pl.pallas_call(product_kernel, grid=(features // width,), in_specs=[pl.Bl...  11.3 us
    all_gather x1, waiting for transfers between devices, shards(): rows = lax.all_gather(piece, ('z', 'core'), tiled=True)  9.86 us
    all_to_all x1, starting transfers between devices, shards(): lax.all_to_all(partial, ('x', 'y'), split_axis=0, concat_axis=0, tiled=True)  7.78 us
    pallas_call x1, Pallas kernels, gram_counts(): pl.pallas_call(gram_kernel, grid_spec=pltpu.PrefetchScalarGridSpec(num_sc...  5.82 us
    all_to_all x1, waiting for transfers between devices, gather_codes(): lax.all_to_all(copies, ('x', 'core'), split_axis=0, concat_axis=0, tiled=...  5.12 us
  transfers between devices with their start and end apart: 3, of which 3 were waited for; matrix products, arithmetic and copies ran while one was open for 11% of the time, Pallas kernels for 13%

profile of v7, /device:TPU:6, one launch (start us, length us, event | category | flops | bytes accessed | tf_op | source)
XLA Modules:
  0.0 147.8 jit_solution(8019631997061116290)
XLA Ops:
  7.2 1.6 %make_piece.1 = bf16[96,1024]{1,0:T(8,128)(2,1)} custom-call(s32[1]{0:T(128)} %bitcast.16.index_ref, bf16[64,1024]{1,0:T(8,128)(2,1)} %bitcast.69, bf16[256,1024]{1,0:T(8,128)(2,1)} %vector_ref.1), custom_call_target="tpu_custom_call" | custom-call | tf_op jit(solution)/shard_map/make_piece/pallas_call | solution.py:128
  8.9 0.7 fusion.24
  9.6 0.5 broadcast.147
  10.1 0.8 reduce.8
  11.0 33.1 %all_to_all.15 = s16[64,2,128]{2,1,0:T(2,128)(2,1)S(1)} all-to-all(s16[64,2,128]{2,1,0:T(2,128)(2,1)S(1)} %reshape.234), channel_id=1, replica_groups=mesh['z'=16,'y'=4,'x'=4,'core'=2] {'z','y'}, dimensions={0} | all-to-all | bytes 65536 | tf_op jit(solution)/shard_map/all_to_all | solution.py:25
  44.2 0.7 broadcast_in_dim.71
  44.9 4.8 %all-to-all-start.1 = ((s16[8,64,256]{2,1,0:T(8,128)(2,1)}), s16[8,64,256]{2,1,0:T(8,128)(2,1)S(1)}, u32[]{:S(2)}, u32[]{:S(2)}) async-start(s16[8,64,256]{2,1,0:T(8,128)(2,1)} %broadcast_in_dim.71), calls=%async_computation.1 | async-start | bytes 524288 | tf_op jit(solution)/shard_map/all_to_all | solution.py:28
  49.8 0.1 eq.94
  50.0 5.1 %all-to-all-done.1 = s16[8,64,256]{2,1,0:T(8,128)(2,1)S(1)} async-done(((s16[8,64,256]{2,1,0:T(8,128)(2,1)}), s16[8,64,256]{2,1,0:T(8,128)(2,1)S(1)}, u32[]{:S(2)}, u32[]{:S(2)}) %all-to-all-start.1) | async-done | bytes 262176 | tf_op jit(solution)/shard_map/all_to_all | solution.py:28
  55.1 0.2 copy_convert_fusion
  55.3 0.1 constant_dynamic-slice_fusion.2
  55.5 0.1 sub.81
  55.6 0.1 pad.4
  55.7 0.8 reshape.219.vector_ref
  56.5 0.3 reshape.214
  56.8 1.4 and_select_fusion
  58.2 0.3 eq.81
  58.6 0.4 eq.82
  58.9 0.6 fusion.10
  59.5 0.4 fusion.3
  59.9 1.6 %fusion.4 = s32[64,17,128]{2,1,0:T(8,128)S(1)} fusion(s32[128]{0:T(128)S(1)} %eq.94, s32[64,16,256]{2,1,0:T(8,128)S(1)} %fusion.3, bf16[64,8,256]{2,1,0:T(8,128)(2,1)S(1)} %get-tuple-element.21, bf16[64,8,256]{2,1,0:T(8,128)(2,1)S(1)} %get-tuple-element.20, bf16[17]{0:T(256)(128)(2,1)S(1)} %pad.11.clone), kind=kOutput, calls=%fused_computation.7 | convolution fusion | flops 75210752 | bytes 2130466 | tf_op jit(solution)/shard_map/dot_general | solution.py:52
  61.6 0.2 copy.35
  61.9 0.4 copy.40
  62.3 0.1 copy.36
  62.4 0.1 squeeze.30
  62.5 0.1 copy.39
  62.7 0.1 squeeze.33
  62.8 0.1 copy.38
  63.0 0.1 squeeze.32
  63.1 0.1 copy.37
  63.2 0.1 squeeze.31
  63.4 0.5 reshape.216
  63.9 1.2 reshape.220
  65.1 0.8 dynamic-slice_reduce_fusion
  65.9 0.2 reshape.221.codes_ref
  66.2 0.6 compare_select_fusion.5.row_ref
  66.8 1.1 and_select_fusion.3.column_ref
  67.9 14.0 %weights.1.left_ref = bf16[1024,3072]{1,0:T(8,128)(2,1)} custom-call(s32[4,1,2048]{2,1,0:T(1,128)} %compare_select_fusion.5.row_ref, s32[4,2,2048]{2,1,0:T(2,128)} %and_select_fusion.3.column_ref, s32[4,1,3072]{2,1,0:T(1,128)} %reshape.219.vector_ref), custom_call_target="tpu_custom_call" | custom-call | tf_op jit(solution)/shard_map/weights/pallas_call | solution.py:81
  81.9 0.1 convert_reduce_fusion.1
  82.0 0.1 convert_subtract_fusion
  82.2 9.9 %all-gather.2.cloned.1.call-done.right_ref = bf16[3072,1024]{1,0:T(8,128)(2,1)} async-done(((bf16[96,1024]{1,0:T(8,128)(2,1)}), bf16[3072,1024]{1,0:T(8,128)(2,1)}) %all-gather.2.cloned.1.call-update) | async-done | bytes 6291472 | tf_op jit(solution)/shard_map/all_gather | solution.py:213
  92.1 11.3 %product.1 = bf16[1024,1024]{1,0:T(8,128)(2,1)} custom-call(bf16[1024,3072]{1,0:T(8,128)(2,1)} %weights.1.left_ref, bf16[3072,1024]{1,0:T(8,128)(2,1)} %all-gather.2.cloned.1.call-done.right_ref), custom_call_target="tpu_custom_call" | custom-call | tf_op jit(solution)/shard_map/product/pallas_call | solution.py:107
  103.4 7.8 %all-to-all-start.2 = ((bf16[16,64,1024]{2,1,0:T(8,128)(2,1)}), bf16[16,64,1024]{2,1,0:T(8,128)(2,1)S(1)}, u32[]{:S(2)}, u32[]{:S(2)}) async-start(bf16[16,64,1024]{2,1,0:T(8,128)(2,1)} %bitcast.63), calls=%async_computation.2 | async-start | bytes 4194304 | tf_op jit(solution)/shard_map/all_to_all | solution.py:234
  111.2 0.2 dynamic-slice_reduce_fusion.1
  111.4 5.8 %gram_counts.1 = f32[64,8192]{1,0:T(8,128)} custom-call(s32[64]{0:T(128)S(1)} %get-tuple-element.23.book_ref, s32[64]{0:T(128)S(1)} %get-tuple-element.22.start_ref, s32[1,512]{1,0:T(1,128)S(1)} %compare_select_fusion.6.row_ref, s32[8,512]{1,0:T(8,128)S(1)} %reshape.221.codes_ref), custom_call_target="tpu_custom_call" | custom-call | tf_op jit(solution)/shard_map/gram_counts/pallas_call | solution.py:160
  117.2 22.5 %all-to-all-done.2 = bf16[16,64,1024]{2,1,0:T(8,128)(2,1)S(1)} async-done(((bf16[16,64,1024]{2,1,0:T(8,128)(2,1)}), bf16[16,64,1024]{2,1,0:T(8,128)(2,1)S(1)}, u32[]{:S(2)}, u32[]{:S(2)}) %all-to-all-start.2) | async-done | bytes 2097184 | tf_op jit(solution)/shard_map/all_to_all | solution.py:234
  139.8 0.4 convert_reduce_fusion
  140.2 0.8 add_bitcast_fusion
  (31 shorter events, 0.8 us)
Async XLA Ops:
  7.2 104.1 %copy-start = (s32[256,64]{0,1:T(8,128)S(1)}, s32[256,64]{0,1:T(8,128)}, u32[]{:S(2)}) copy-start(s32[256,64]{0,1:T(8,128)} %param.7) | copy-start | bytes 196612
  7.2 84.9 %all-gather.2.cloned.1.call-start = ((), (), s32[]{:S(2)}) async-start(), calls=%async_computation.3 | async-start | bytes 6488064 | tf_op jit(solution)/shard_map/all_gather | solution.py:213
  44.9 10.3 %all-to-all-start.1 = ((s16[8,64,256]{2,1,0:T(8,128)(2,1)}), s16[8,64,256]{2,1,0:T(8,128)(2,1)S(1)}, u32[]{:S(2)}, u32[]{:S(2)}) async-start(s16[8,64,256]{2,1,0:T(8,128)(2,1)} %broadcast_in_dim.71), calls=%async_computation.1 | async-start | bytes 524288 | tf_op jit(solution)/shard_map/all_to_all | solution.py:28
  67.9 14.1 %copy-start.1 = (bf16[1,64,1024]{2,1,0:T(8,128)(2,1)S(1)}, bf16[1,64,1024]{2,1,0:T(8,128)(2,1)}, u32[]{:S(2)}) copy-start(bf16[1,64,1024]{2,1,0:T(8,128)(2,1)} %param.6) | copy-start | bytes 393220
  103.4 36.3 %all-to-all-start.2 = ((bf16[16,64,1024]{2,1,0:T(8,128)(2,1)}), bf16[16,64,1024]{2,1,0:T(8,128)(2,1)S(1)}, u32[]{:S(2)}, u32[]{:S(2)}) async-start(bf16[16,64,1024]{2,1,0:T(8,128)(2,1)} %bitcast.63), calls=%async_computation.2 | async-start | bytes 4194304 | tf_op jit(solution)/shard_map/all_to_all | solution.py:234
Sparse Core Ops, SparseCore 0:
  10.7 81.3 all-gather.1

commit v8 on v7

--- a/solution.py
+++ b/solution.py
@@ -12,7 +12,7 @@
 Z, Y, X, C = 16, 4, 4, 2
 OWN = 64
 CAP = 8
-PRODUCT_VMEM = 56 << 20
+BANDS = 4
 HALF = 32
 PLANE = Y * OWN
 NT = (((1,), (1,)), ((), ()))
@@ -93,27 +93,52 @@
     )(row_index, column_index, vector_index)
 
 
-def product_kernel(left_ref, right_ref, out_ref):
-    total = lax.dot_general(
-        left_ref[...], right_ref[...], NN, preferred_element_type=jnp.float32
-    )
-    out_ref[...] = total.astype(out_ref.dtype)
+def product_kernel(left_ref, right_ref, out_ref, table_ref, rows_ref, sems):
+    parts, _, width = rows_ref.shape
+    height = table_ref.shape[0] // BANDS
+    bands = [slice(m * height, (m + 1) * height) for m in range(BANDS)]
+    tables = [
+        pltpu.make_async_copy(
+            left_ref.at[pl.ds(m * height, height)],
+            table_ref.at[pl.ds(m * height, height)],
+            sems.at[m],
+        )
+        for m in range(BANDS)
+    ]
+    rows = [
+        pltpu.make_async_copy(
+            right_ref.at[:, pl.ds(n * width, width)], rows_ref.at[n], sems.at[BANDS + n]
+        )
+        for n in range(parts)
+    ]
+    for copy in rows[:1] + tables + rows[1:]:
+        copy.start()
+    for n in range(parts):
+        rows[n].wait()
+        for m, band in enumerate(bands):
+            if n == 0:
+                tables[m].wait()
+            total = lax.dot_general(
+                table_ref[band, :], rows_ref[n], NN, preferred_element_type=jnp.float32
+            )
+            out_ref[band, n * width : (n + 1) * width] = total.astype(out_ref.dtype)
 
 
 def product(left, right):
-    rows, depth = left.shape
     features = right.shape[1]
-    width = features // 4
+    parts = 2
+    left, right = (pltpu.with_memory_space_constraint(a, pltpu.HBM) for a in (left, right))
     return pl.pallas_call(
         product_kernel,
-        grid=(features // width,),
-        in_specs=[
-            pl.BlockSpec((rows, depth), lambda n: (0, 0)),
-            pl.BlockSpec((depth, width), lambda n: (0, n)),
+        in_specs=[pl.BlockSpec(memory_space=pltpu.HBM)] * 2,
+        out_specs=pl.BlockSpec(memory_space=pltpu.VMEM),
+        out_shape=jax.ShapeDtypeStruct((left.shape[0], features), jnp.bfloat16),
+        scratch_shapes=[
+            pltpu.VMEM(left.shape, left.dtype),
+            pltpu.VMEM((parts, right.shape[0], features // parts), right.dtype),
+            pltpu.SemaphoreType.DMA((BANDS + parts,)),
         ],
-        out_specs=pl.BlockSpec((rows, width), lambda n: (0, n)),
-        out_shape=jax.ShapeDtypeStruct((rows, features), jnp.bfloat16),
-        compiler_params=pltpu.CompilerParams(vmem_limit_bytes=PRODUCT_VMEM),
+        compiler_params=pltpu.CompilerParams(vmem_limit_bytes=32 << 20),
         name="product",
     )(left, right)
 
@@ -227,13 +252,12 @@
     divisor = jnp.broadcast_to(code_count[:, None] + 2.0, (OWN, features))
     current = codebook[0].astype(jnp.float32)
     base = current - 2.0 * current / divisor
-    table, divisor, base = lax.optimization_barrier((table, divisor, base))
+    partner = lax.dynamic_index_in_dim(pairs, (book * K + owner * OWN) // BLK, 0, keepdims=False)
+    gram = gram_counts(partner // KB, partner % KB * BLK, own_row, held)
+    table, gram, divisor, base = lax.optimization_barrier((table, gram, divisor, base))
     partial = product(table, rows)
-    partial, held, own_row = lax.optimization_barrier((partial, held, own_row))
     partial = partial.reshape(X * Y, OWN, features)
     received = lax.all_to_all(partial, ("x", "y"), split_axis=0, concat_axis=0, tiled=True)
-    partner = lax.dynamic_index_in_dim(pairs, (book * K + owner * OWN) // BLK, 0, keepdims=False)
-    gram = gram_counts(partner // KB, partner % KB * BLK, own_row, held)
     right_side = jnp.sum(received.astype(jnp.float32), axis=0)
     return (base + right_side / divisor)[None], gram[None]
 

time: 150 us -> 145 us (0.967)
  blocking collectives: 33.1 us -> 66.8 us
  waiting for transfers between devices: 37.5 us -> 9.17 us
  starting transfers between devices: 12.6 us -> 4.85 us
  Pallas kernels: 32.7 us -> 31.1 us
    all_to_all x0 -> x1, blocking collectives: none -> 33.7 us  [shards(): lax.all_to_all(partial, ('x', 'y'), split_axis=0, concat_axis=0, tiled=True)]
    all_to_all x1 -> x0, waiting for transfers between devices: 22.5 us -> none  [shards(): lax.all_to_all(partial, ('x', 'y'), split_axis=0, concat_axis=0, tiled=True)]
    all_to_all x1 -> x0, starting transfers between devices: 7.78 us -> none  [shards(): lax.all_to_all(partial, ('x', 'y'), split_axis=0, concat_axis=0, tiled=True)]
    all_gather x1, waiting for transfers between devices: 9.86 us -> 4.24 us  [shards(): rows = lax.all_gather(piece, ('z', 'core'), tiled=True)]
    pallas_call x1, Pallas kernels: 11.3 us -> 9.72 us  [product(): pl.pallas_call(product_kernel, in_specs=[pl.BlockSpec(memory_space=pltpu....]
  transfers between devices with their start and end apart: 3 -> 2, of which waited for: 3 -> 2; matrix products, arithmetic and copies ran while one was open for 11% -> 11% of each run, Pallas kernels for 13% -> 14%
where the time goes in v8:
time: 145 us; the launch traced here: 144 us
  blocking collectives  66.8 us (46%)
  Pallas kernels  31.1 us (21%)
  between operations  14.3 us (10%)
  waiting for transfers between devices  9.17 us (6%)
  local copies, waits for them, and re-layouts  8.53 us (6%)
  other arithmetic  6.99 us (5%)
  starting transfers between devices  4.85 us (3%)
  matrix products  1.96 us (1%)
    all_to_all x1, blocking collectives, shards(): lax.all_to_all(partial, ('x', 'y'), split_axis=0, concat_axis=0, tiled=True)  33.7 us
    all_to_all x1, blocking collectives, gather_codes(): lax.all_to_all(copies, ('z', 'y'), split_axis=0, concat_axis=0, tiled=True)  33.1 us
    pallas_call x1, Pallas kernels, weights(): pl.pallas_call(weight_kernel, grid=(books,), in_specs=[pl.BlockSpec((1, 1...  14 us
    pallas_call x1, Pallas kernels, product(): pl.pallas_call(product_kernel, in_specs=[pl.BlockSpec(memory_space=pltpu....  9.72 us
    pallas_call x1, Pallas kernels, gram_counts(): pl.pallas_call(gram_kernel, grid_spec=pltpu.PrefetchScalarGridSpec(num_sc...  5.81 us
    all_to_all x1, waiting for transfers between devices, gather_codes(): lax.all_to_all(copies, ('x', 'core'), split_axis=0, concat_axis=0, tiled=...  4.92 us
    all_to_all x1, starting transfers between devices, gather_codes(): lax.all_to_all(copies, ('x', 'core'), split_axis=0, concat_axis=0, tiled=...  4.81 us
    all_gather x1, waiting for transfers between devices, shards(): rows = lax.all_gather(piece, ('z', 'core'), tiled=True)  4.24 us
  transfers between devices with their start and end apart: 2, of which 2 were waited for; matrix products, arithmetic and copies ran while one was open for 11% of the time, Pallas kernels for 14%

profile of v8, /device:TPU:6, one launch (start us, length us, event | category | flops | bytes accessed | tf_op | source)
XLA Modules:
  0.0 143.8 jit_solution(13661307256024262601)
XLA Ops:
  7.2 1.6 %make_piece.1 = bf16[96,1024]{1,0:T(8,128)(2,1)} custom-call(s32[1]{0:T(128)} %bitcast.16.index_ref, bf16[64,1024]{1,0:T(8,128)(2,1)} %bitcast.69, bf16[256,1024]{1,0:T(8,128)(2,1)} %vector_ref.1), custom_call_target="tpu_custom_call" | custom-call | tf_op jit(solution)/shard_map/make_piece/pallas_call | solution.py:153
  8.9 0.7 fusion.24
  9.6 0.5 broadcast.147
  10.1 0.8 reduce.8
  11.0 33.1 %all_to_all.15 = s16[64,2,128]{2,1,0:T(2,128)(2,1)S(1)} all-to-all(s16[64,2,128]{2,1,0:T(2,128)(2,1)S(1)} %reshape.234), channel_id=1, replica_groups=mesh['z'=16,'y'=4,'x'=4,'core'=2] {'z','y'}, dimensions={0} | all-to-all | bytes 65536 | tf_op jit(solution)/shard_map/all_to_all | solution.py:25
  44.2 0.7 broadcast_in_dim.71
  44.9 4.8 %all-to-all-start.1 = ((s16[8,64,256]{2,1,0:T(8,128)(2,1)}), s16[8,64,256]{2,1,0:T(8,128)(2,1)S(1)}, u32[]{:S(2)}, u32[]{:S(2)}) async-start(s16[8,64,256]{2,1,0:T(8,128)(2,1)} %broadcast_in_dim.71), calls=%async_computation.1 | async-start | bytes 524288 | tf_op jit(solution)/shard_map/all_to_all | solution.py:28
  49.7 0.1 eq.84
  49.8 0.1 eq.94
  50.1 0.2 dynamic-slice_reduce_fusion.1
  50.3 4.9 %all-to-all-done.1 = s16[8,64,256]{2,1,0:T(8,128)(2,1)S(1)} async-done(((s16[8,64,256]{2,1,0:T(8,128)(2,1)}), s16[8,64,256]{2,1,0:T(8,128)(2,1)S(1)}, u32[]{:S(2)}, u32[]{:S(2)}) %all-to-all-start.1) | async-done | bytes 262176 | tf_op jit(solution)/shard_map/all_to_all | solution.py:28
  55.2 0.2 copy_convert_fusion
  55.4 0.1 constant_dynamic-slice_fusion.2
  55.5 0.1 sub.81
  55.6 0.1 pad.4
  55.8 0.8 reshape.219.vector_ref
  56.5 0.3 reshape.214
  56.8 1.4 and_select_fusion
  58.3 0.3 eq.81
  58.6 0.4 eq.82
  59.0 0.6 fusion.10
  59.6 0.4 fusion.3
  60.0 1.6 %fusion.4 = s32[64,17,128]{2,1,0:T(8,128)S(1)} fusion(s32[128]{0:T(128)S(1)} %eq.94, s32[64,16,256]{2,1,0:T(8,128)S(1)} %fusion.3, bf16[64,8,256]{2,1,0:T(8,128)(2,1)S(1)} %get-tuple-element.17, bf16[64,8,256]{2,1,0:T(8,128)(2,1)S(1)} %get-tuple-element.16, bf16[17]{0:T(256)(128)(2,1)S(1)} %pad.11.clone), kind=kOutput, calls=%fused_computation.7 | convolution fusion | flops 75210752 | bytes 2130466 | tf_op jit(solution)/shard_map/dot_general | solution.py:52
  61.7 0.2 copy.35
  61.9 0.4 copy.40
  62.3 0.1 copy.36
  62.4 0.1 squeeze.30
  62.6 0.1 copy.39
  62.7 0.1 squeeze.33
  62.9 0.1 copy.38
  63.0 0.1 squeeze.32
  63.1 0.1 copy.37
  63.3 0.1 squeeze.31
  63.4 0.5 reshape.216
  63.9 1.3 reshape.220
  65.2 0.8 dynamic-slice_reduce_fusion
  66.0 0.2 reshape.221.codes_ref
  66.2 5.8 %gram_counts.1 = f32[64,8192]{1,0:T(8,128)} custom-call(s32[64]{0:T(128)S(1)} %get-tuple-element.19.book_ref, s32[64]{0:T(128)S(1)} %get-tuple-element.18.start_ref, s32[1,512]{1,0:T(1,128)S(1)} %compare_select_fusion.6.row_ref, s32[8,512]{1,0:T(8,128)S(1)} %reshape.221.codes_ref), custom_call_target="tpu_custom_call" | custom-call | tf_op jit(solution)/shard_map/gram_counts/pallas_call | solution.py:185
  72.0 0.7 compare_select_fusion.5.row_ref
  72.7 1.1 and_select_fusion.3.column_ref
  73.8 14.0 %weights.1.left_ref = bf16[1024,3072]{1,0:T(8,128)(2,1)} custom-call(s32[4,1,2048]{2,1,0:T(1,128)} %compare_select_fusion.5.row_ref, s32[4,2,2048]{2,1,0:T(2,128)} %and_select_fusion.3.column_ref, s32[4,1,3072]{2,1,0:T(1,128)} %reshape.219.vector_ref), custom_call_target="tpu_custom_call" | custom-call | tf_op jit(solution)/shard_map/weights/pallas_call | solution.py:81
  87.8 0.1 convert_reduce_fusion.1
  87.9 0.1 convert_subtract_fusion
  88.1 4.2 %all-gather.2.cloned.1.call-done.right_ref = bf16[3072,1024]{1,0:T(8,128)(2,1)} async-done(((bf16[96,1024]{1,0:T(8,128)(2,1)}), bf16[3072,1024]{1,0:T(8,128)(2,1)}) %all-gather.2.cloned.1.call-update) | async-done | bytes 6291472 | tf_op jit(solution)/shard_map/all_gather | solution.py:238
  92.4 9.7 %product.1 = bf16[1024,1024]{1,0:T(8,128)(2,1)S(1)} custom-call(bf16[1024,3072]{1,0:T(8,128)(2,1)} %weights.1.left_ref, bf16[3072,1024]{1,0:T(8,128)(2,1)} %all-gather.2.cloned.1.call-done.right_ref), custom_call_target="tpu_custom_call" | custom-call | tf_op jit(solution)/shard_map/product/pallas_call | solution.py:131
  102.1 33.7 %all_to_all.16 = bf16[16,64,1024]{2,1,0:T(8,128)(2,1)S(1)} all-to-all(bf16[16,64,1024]{2,1,0:T(8,128)(2,1)S(1)} %bitcast.62), channel_id=1, replica_groups=mesh['z'=16,'y'=4,'x'=4,'core'=2] {'x','y'}, dimensions={0} | all-to-all | bytes 4194304 | tf_op jit(solution)/shard_map/all_to_all | solution.py:260
  135.8 0.4 convert_reduce_fusion
  136.2 0.8 add_bitcast_fusion
  (30 shorter events, 0.7 us)
Async XLA Ops:
  7.2 42.9 %copy-start = (s32[256,64]{0,1:T(8,128)S(1)}, s32[256,64]{0,1:T(8,128)}, u32[]{:S(2)}) copy-start(s32[256,64]{0,1:T(8,128)} %param.7) | copy-start | bytes 196612
  7.2 85.2 %all-gather.2.cloned.1.call-start = ((), (), s32[]{:S(2)}) async-start(), calls=%async_computation.3 | async-start | bytes 6488064 | tf_op jit(solution)/shard_map/all_gather | solution.py:238
  44.9 10.3 %all-to-all-start.1 = ((s16[8,64,256]{2,1,0:T(8,128)(2,1)}), s16[8,64,256]{2,1,0:T(8,128)(2,1)S(1)}, u32[]{:S(2)}, u32[]{:S(2)}) async-start(s16[8,64,256]{2,1,0:T(8,128)(2,1)} %broadcast_in_dim.71), calls=%async_computation.1 | async-start | bytes 524288 | tf_op jit(solution)/shard_map/all_to_all | solution.py:28
  73.8 14.1 %copy-start.1 = (bf16[1,64,1024]{2,1,0:T(8,128)(2,1)S(1)}, bf16[1,64,1024]{2,1,0:T(8,128)(2,1)}, u32[]{:S(2)}) copy-start(bf16[1,64,1024]{2,1,0:T(8,128)(2,1)} %param.6) | copy-start | bytes 393220
Sparse Core Ops, SparseCore 0:
  10.1 82.1 all-gather.1

commit v9 on v8

--- a/solution.py
+++ b/solution.py
@@ -71,7 +71,7 @@
         counts = lax.dot_general(member, table, NT, preferred_element_type=jnp.float32)
         counts = (-counts).astype(out_ref.dtype)
         for z in range(Z):
-            start = (z * C + core) * (OWN + HALF)
+            start = (core * Z + z) * (OWN + HALF)
             out_ref[:, start : start + OWN] = counts[:, z * OWN : (z + 1) * OWN]
 
 
@@ -222,7 +222,7 @@
     portion = lax.dynamic_slice_in_dim(mine, C * HALF * x, C * HALF, 2)
     portion = by_parity(portion, core).reshape(Z, X, C, HALF) - PLANE * z
     portion = jnp.pad(
-        portion.transpose(1, 0, 2, 3), ((0, 0), (0, 0), (0, 0), (OWN, 0)), constant_values=-1
+        portion.transpose(1, 2, 0, 3), ((0, 0), (0, 0), (0, 0), (OWN, 0)), constant_values=-1
     )
     return portion.reshape(X, 1, Z * C * (OWN + HALF))
 
@@ -235,7 +235,7 @@
     book = x * C + core
     stored = (pltpu.with_memory_space_constraint(a, pltpu.HBM) for a in (codebook[0], vectors))
     piece = make_piece(*stored, book.astype(jnp.int32)[None])
-    rows = lax.all_gather(piece, ("z", "core"), tiled=True)
+    rows = lax.all_gather(piece, ("core", "z"), tiled=True)
     all_codes = gather_codes(codes, book)
     local = by_parity(all_codes, core) - PLANE * z
     tuples = compact(all_codes, local)

time: 145 us -> 145 us (level)
  transfers between devices with their start and end apart: 2 -> 2, of which waited for: 2 -> 2; matrix products, arithmetic and copies ran while one was open for 11% -> 11% of each run, Pallas kernels for 14% -> 13%
where the time goes in v9:
time: 145 us; the launch traced here: 144 us
  blocking collectives  66.9 us (46%)
  Pallas kernels  29.9 us (21%)
  between operations  14.3 us (10%)
  waiting for transfers between devices  10.3 us (7%)
  local copies, waits for them, and re-layouts  8.47 us (6%)
  other arithmetic  6.99 us (5%)
  starting transfers between devices  4.81 us (3%)
  matrix products  1.96 us (1%)
    all_to_all x1, blocking collectives, shards(): lax.all_to_all(partial, ('x', 'y'), split_axis=0, concat_axis=0, tiled=True)  33.7 us
    all_to_all x1, blocking collectives, gather_codes(): lax.all_to_all(copies, ('z', 'y'), split_axis=0, concat_axis=0, tiled=True)  33.2 us
    pallas_call x1, Pallas kernels, weights(): pl.pallas_call(weight_kernel, grid=(books,), in_specs=[pl.BlockSpec((1, 1...  12.8 us
    pallas_call x1, Pallas kernels, product(): pl.pallas_call(product_kernel, in_specs=[pl.BlockSpec(memory_space=pltpu....  9.72 us
    pallas_call x1, Pallas kernels, gram_counts(): pl.pallas_call(gram_kernel, grid_spec=pltpu.PrefetchScalarGridSpec(num_sc...  5.82 us
    all_gather x1, waiting for transfers between devices, shards(): rows = lax.all_gather(piece, ('core', 'z'), tiled=True)  5.4 us
    all_to_all x1, waiting for transfers between devices, gather_codes(): lax.all_to_all(copies, ('x', 'core'), split_axis=0, concat_axis=0, tiled=...  4.92 us
    all_to_all x1, starting transfers between devices, gather_codes(): lax.all_to_all(copies, ('x', 'core'), split_axis=0, concat_axis=0, tiled=...  4.77 us
  transfers between devices with their start and end apart: 2, of which 2 were waited for; matrix products, arithmetic and copies ran while one was open for 11% of the time, Pallas kernels for 13%

profile of v9, /device:TPU:6, one launch (start us, length us, event | category | flops | bytes accessed | tf_op | source)
XLA Modules:
  0.0 143.8 jit_solution(8103582844535871395)
XLA Ops:
  7.2 1.6 %make_piece.1 = bf16[96,1024]{1,0:T(8,128)(2,1)} custom-call(s32[1]{0:T(128)} %bitcast.16.index_ref, bf16[64,1024]{1,0:T(8,128)(2,1)} %bitcast.71, bf16[256,1024]{1,0:T(8,128)(2,1)} %vector_ref.1), custom_call_target="tpu_custom_call" | custom-call | tf_op jit(solution)/shard_map/make_piece/pallas_call | solution.py:153
  8.9 0.7 fusion.24
  9.6 0.5 broadcast.147
  10.1 0.8 reduce.8
  11.0 33.2 %all_to_all.15 = s16[64,2,128]{2,1,0:T(2,128)(2,1)S(1)} all-to-all(s16[64,2,128]{2,1,0:T(2,128)(2,1)S(1)} %reshape.234), channel_id=1, replica_groups=mesh['z'=16,'y'=4,'x'=4,'core'=2] {'z','y'}, dimensions={0} | all-to-all | bytes 65536 | tf_op jit(solution)/shard_map/all_to_all | solution.py:25
  44.2 0.7 broadcast_in_dim.71
  44.9 4.8 %all-to-all-start.1 = ((s16[8,64,256]{2,1,0:T(8,128)(2,1)}), s16[8,64,256]{2,1,0:T(8,128)(2,1)S(1)}, u32[]{:S(2)}, u32[]{:S(2)}) async-start(s16[8,64,256]{2,1,0:T(8,128)(2,1)} %broadcast_in_dim.71), calls=%async_computation.1 | async-start | bytes 524288 | tf_op jit(solution)/shard_map/all_to_all | solution.py:28
  49.7 0.1 eq.84
  49.8 0.1 eq.94
  49.9 0.1 copy.45
  50.1 0.2 dynamic-slice_reduce_fusion.1
  50.3 4.9 %all-to-all-done.1 = s16[8,64,256]{2,1,0:T(8,128)(2,1)S(1)} async-done(((s16[8,64,256]{2,1,0:T(8,128)(2,1)}), s16[8,64,256]{2,1,0:T(8,128)(2,1)S(1)}, u32[]{:S(2)}, u32[]{:S(2)}) %all-to-all-start.1) | async-done | bytes 262176 | tf_op jit(solution)/shard_map/all_to_all | solution.py:28
  55.2 0.2 copy_convert_fusion
  55.4 0.1 constant_dynamic-slice_fusion.2
  55.5 0.1 sub.81
  55.7 0.8 reshape.219.vector_ref
  56.5 0.3 reshape.214
  56.8 1.4 and_select_fusion
  58.2 0.3 eq.81
  58.5 0.4 eq.82
  58.9 0.6 fusion.10
  59.5 0.4 fusion.3
  59.9 1.6 %fusion.4 = s32[64,17,128]{2,1,0:T(8,128)S(1)} fusion(s32[128]{0:T(128)S(1)} %eq.94, s32[64,16,256]{2,1,0:T(8,128)S(1)} %fusion.3, bf16[64,8,256]{2,1,0:T(8,128)(2,1)S(1)} %get-tuple-element.17, bf16[64,8,256]{2,1,0:T(8,128)(2,1)S(1)} %get-tuple-element.16, bf16[17]{0:T(256)(128)(2,1)S(1)} %pad.11.clone), kind=kOutput, calls=%fused_computation.7 | convolution fusion | flops 75210752 | bytes 2130466 | tf_op jit(solution)/shard_map/dot_general | solution.py:52
  61.6 0.2 copy.46
  61.8 0.4 copy.51
  62.2 0.1 copy.47
  62.4 0.1 squeeze.30
  62.5 0.1 copy.50
  62.7 0.1 squeeze.33
  62.8 0.1 copy.49
  62.9 0.1 squeeze.32
  63.1 0.1 copy.48
  63.2 0.1 squeeze.31
  63.4 0.5 reshape.216
  63.9 1.3 reshape.220
  65.1 0.8 dynamic-slice_reduce_fusion
  65.9 0.2 reshape.221.codes_ref
  66.1 5.8 %gram_counts.1 = f32[64,8192]{1,0:T(8,128)} custom-call(s32[64]{0:T(128)S(1)} %get-tuple-element.19.book_ref, s32[64]{0:T(128)S(1)} %get-tuple-element.18.start_ref, s32[1,512]{1,0:T(1,128)S(1)} %compare_select_fusion.6.row_ref, s32[8,512]{1,0:T(8,128)S(1)} %reshape.221.codes_ref), custom_call_target="tpu_custom_call" | custom-call | tf_op jit(solution)/shard_map/gram_counts/pallas_call | solution.py:185
  72.0 0.7 compare_select_fusion.5.row_ref
  72.7 1.1 and_select_fusion.3.column_ref
  73.8 12.8 %weights.1.left_ref = bf16[1024,3072]{1,0:T(8,128)(2,1)} custom-call(s32[4,1,2048]{2,1,0:T(1,128)} %compare_select_fusion.5.row_ref, s32[4,2,2048]{2,1,0:T(2,128)} %and_select_fusion.3.column_ref, s32[4,1,3072]{2,1,0:T(1,128)} %reshape.219.vector_ref), custom_call_target="tpu_custom_call" | custom-call | tf_op jit(solution)/shard_map/weights/pallas_call | solution.py:81
  86.6 0.1 convert_reduce_fusion.1
  86.7 0.1 convert_subtract_fusion
  86.9 5.4 %all-gather.2.cloned.1.call-done.right_ref = bf16[3072,1024]{1,0:T(8,128)(2,1)} async-done(((bf16[96,1024]{1,0:T(8,128)(2,1)}), bf16[3072,1024]{1,0:T(8,128)(2,1)}) %all-gather.2.cloned.1.call-update) | async-done | bytes 6291472 | tf_op jit(solution)/shard_map/all_gather | solution.py:238
  92.3 9.7 %product.1 = bf16[1024,1024]{1,0:T(8,128)(2,1)S(1)} custom-call(bf16[1024,3072]{1,0:T(8,128)(2,1)} %weights.1.left_ref, bf16[3072,1024]{1,0:T(8,128)(2,1)} %all-gather.2.cloned.1.call-done.right_ref), custom_call_target="tpu_custom_call" | custom-call | tf_op jit(solution)/shard_map/product/pallas_call | solution.py:131
  102.0 33.7 %all_to_all.16 = bf16[16,64,1024]{2,1,0:T(8,128)(2,1)S(1)} all-to-all(bf16[16,64,1024]{2,1,0:T(8,128)(2,1)S(1)} %bitcast.64), channel_id=1, replica_groups=mesh['z'=16,'y'=4,'x'=4,'core'=2] {'x','y'}, dimensions={0} | all-to-all | bytes 4194304 | tf_op jit(solution)/shard_map/all_to_all | solution.py:260
  135.8 0.4 convert_reduce_fusion
  136.2 0.8 add_bitcast_fusion
  (31 shorter events, 0.7 us)
Async XLA Ops:
  7.2 42.9 %copy-start = (s32[256,64]{0,1:T(8,128)S(1)}, s32[256,64]{0,1:T(8,128)}, u32[]{:S(2)}) copy-start(s32[256,64]{0,1:T(8,128)} %param.7) | copy-start | bytes 196612
  7.2 85.1 %all-gather.2.cloned.1.call-start = ((), (), s32[]{:S(2)}) async-start(), calls=%async_computation.3 | async-start | bytes 6488064 | tf_op jit(solution)/shard_map/all_gather | solution.py:238
  44.9 10.2 %all-to-all-start.1 = ((s16[8,64,256]{2,1,0:T(8,128)(2,1)}), s16[8,64,256]{2,1,0:T(8,128)(2,1)S(1)}, u32[]{:S(2)}, u32[]{:S(2)}) async-start(s16[8,64,256]{2,1,0:T(8,128)(2,1)} %broadcast_in_dim.71), calls=%async_computation.1 | async-start | bytes 524288 | tf_op jit(solution)/shard_map/all_to_all | solution.py:28
  73.8 12.9 %copy-start.1 = (bf16[1,64,1024]{2,1,0:T(8,128)(2,1)S(1)}, bf16[1,64,1024]{2,1,0:T(8,128)(2,1)}, u32[]{:S(2)}) copy-start(bf16[1,64,1024]{2,1,0:T(8,128)(2,1)} %param.6) | copy-start | bytes 393220
Sparse Core Ops, SparseCore 0:
  10.1 82.1 all-gather.1

commit v10 on v9

--- a/solution.py
+++ b/solution.py
@@ -12,7 +12,7 @@
 Z, Y, X, C = 16, 4, 4, 2
 OWN = 64
 CAP = 8
-BANDS = 4
+BANDS = X
 HALF = 32
 PLANE = Y * OWN
 NT = (((1,), (1,)), ((), ()))
@@ -121,7 +121,12 @@
             total = lax.dot_general(
                 table_ref[band, :], rows_ref[n], NN, preferred_element_type=jnp.float32
             )
-            out_ref[band, n * width : (n + 1) * width] = total.astype(out_ref.dtype)
+            total = total.astype(out_ref.dtype)
+            for y in range(Y):
+                start = (y * X + m) * OWN
+                out_ref[start : start + OWN, n * width : (n + 1) * width] = total[
+                    y * OWN : (y + 1) * OWN, :
+                ]
 
 
 def product(left, right):
@@ -257,7 +262,7 @@
     table, gram, divisor, base = lax.optimization_barrier((table, gram, divisor, base))
     partial = product(table, rows)
     partial = partial.reshape(X * Y, OWN, features)
-    received = lax.all_to_all(partial, ("x", "y"), split_axis=0, concat_axis=0, tiled=True)
+    received = lax.all_to_all(partial, ("y", "x"), split_axis=0, concat_axis=0, tiled=True)
     right_side = jnp.sum(received.astype(jnp.float32), axis=0)
     return (base + right_side / divisor)[None], gram[None]
 

time: 145 us -> 146 us (level); the launches traced: 144 us -> 143 us
  no operation moved by 1% of the time
where the time goes in v10:
time: 146 us; the launch traced here: 143 us
  blocking collectives  66.4 us (45%)
  Pallas kernels  29.9 us (20%)
  between operations  14.3 us (10%)
  waiting for transfers between devices  10.3 us (7%)
  local copies, waits for them, and re-layouts  8.47 us (6%)
  other arithmetic  6.99 us (5%)
  starting transfers between devices  4.81 us (3%)
  matrix products  1.96 us (1%)
    all_to_all x1, blocking collectives, shards(): lax.all_to_all(partial, ('y', 'x'), split_axis=0, concat_axis=0, tiled=True)  33.2 us
    all_to_all x1, blocking collectives, gather_codes(): lax.all_to_all(copies, ('z', 'y'), split_axis=0, concat_axis=0, tiled=True)  33.2 us
    pallas_call x1, Pallas kernels, weights(): pl.pallas_call(weight_kernel, grid=(books,), in_specs=[pl.BlockSpec((1, 1...  12.8 us
    pallas_call x1, Pallas kernels, product(): pl.pallas_call(product_kernel, in_specs=[pl.BlockSpec(memory_space=pltpu....  9.72 us
    pallas_call x1, Pallas kernels, gram_counts(): pl.pallas_call(gram_kernel, grid_spec=pltpu.PrefetchScalarGridSpec(num_sc...  5.82 us
    all_gather x1, waiting for transfers between devices, shards(): rows = lax.all_gather(piece, ('core', 'z'), tiled=True)  5.4 us
    all_to_all x1, waiting for transfers between devices, gather_codes(): lax.all_to_all(copies, ('x', 'core'), split_axis=0, concat_axis=0, tiled=...  4.92 us
    all_to_all x1, starting transfers between devices, gather_codes(): lax.all_to_all(copies, ('x', 'core'), split_axis=0, concat_axis=0, tiled=...  4.77 us
  transfers between devices with their start and end apart: 2, of which 2 were waited for; matrix products, arithmetic and copies ran while one was open for 11% of the time, Pallas kernels for 13%

profile of v10, /device:TPU:6, one launch (start us, length us, event | category | flops | bytes accessed | tf_op | source)
XLA Modules:
  0.0 143.2 jit_solution(17257672003305184196)
XLA Ops:
  7.2 1.6 %make_piece.1 = bf16[96,1024]{1,0:T(8,128)(2,1)} custom-call(s32[1]{0:T(128)} %bitcast.16.index_ref, bf16[64,1024]{1,0:T(8,128)(2,1)} %bitcast.71, bf16[256,1024]{1,0:T(8,128)(2,1)} %vector_ref.1), custom_call_target="tpu_custom_call" | custom-call | tf_op jit(solution)/shard_map/make_piece/pallas_call | solution.py:158
  8.9 0.7 fusion.24
  9.6 0.5 broadcast.147
  10.1 0.8 reduce.8
  11.0 33.2 %all_to_all.15 = s16[64,2,128]{2,1,0:T(2,128)(2,1)S(1)} all-to-all(s16[64,2,128]{2,1,0:T(2,128)(2,1)S(1)} %reshape.234), channel_id=1, replica_groups=mesh['z'=16,'y'=4,'x'=4,'core'=2] {'z','y'}, dimensions={0} | all-to-all | bytes 65536 | tf_op jit(solution)/shard_map/all_to_all | solution.py:25
  44.2 0.7 broadcast_in_dim.71
  44.9 4.8 %all-to-all-start.1 = ((s16[8,64,256]{2,1,0:T(8,128)(2,1)}), s16[8,64,256]{2,1,0:T(8,128)(2,1)S(1)}, u32[]{:S(2)}, u32[]{:S(2)}) async-start(s16[8,64,256]{2,1,0:T(8,128)(2,1)} %broadcast_in_dim.71), calls=%async_computation.1 | async-start | bytes 524288 | tf_op jit(solution)/shard_map/all_to_all | solution.py:28
  49.7 0.1 eq.84
  49.8 0.1 eq.94
  49.9 0.1 copy.45
  50.1 0.2 dynamic-slice_reduce_fusion.1
  50.3 4.9 %all-to-all-done.1 = s16[8,64,256]{2,1,0:T(8,128)(2,1)S(1)} async-done(((s16[8,64,256]{2,1,0:T(8,128)(2,1)}), s16[8,64,256]{2,1,0:T(8,128)(2,1)S(1)}, u32[]{:S(2)}, u32[]{:S(2)}) %all-to-all-start.1) | async-done | bytes 262176 | tf_op jit(solution)/shard_map/all_to_all | solution.py:28
  55.2 0.2 copy_convert_fusion
  55.4 0.1 constant_dynamic-slice_fusion.2
  55.5 0.1 sub.81
  55.7 0.8 reshape.219.vector_ref
  56.5 0.3 reshape.214
  56.8 1.4 and_select_fusion
  58.2 0.3 eq.81
  58.5 0.4 eq.82
  58.9 0.6 fusion.10
  59.5 0.4 fusion.3
  59.9 1.6 %fusion.4 = s32[64,17,128]{2,1,0:T(8,128)S(1)} fusion(s32[128]{0:T(128)S(1)} %eq.94, s32[64,16,256]{2,1,0:T(8,128)S(1)} %fusion.3, bf16[64,8,256]{2,1,0:T(8,128)(2,1)S(1)} %get-tuple-element.17, bf16[64,8,256]{2,1,0:T(8,128)(2,1)S(1)} %get-tuple-element.16, bf16[17]{0:T(256)(128)(2,1)S(1)} %pad.11.clone), kind=kOutput, calls=%fused_computation.7 | convolution fusion | flops 75210752 | bytes 2130466 | tf_op jit(solution)/shard_map/dot_general | solution.py:52
  61.6 0.2 copy.46
  61.8 0.4 copy.51
  62.2 0.1 copy.47
  62.4 0.1 squeeze.30
  62.5 0.1 copy.50
  62.7 0.1 squeeze.33
  62.8 0.1 copy.49
  62.9 0.1 squeeze.32
  63.1 0.1 copy.48
  63.2 0.1 squeeze.31
  63.4 0.5 reshape.216
  63.9 1.3 reshape.220
  65.1 0.8 dynamic-slice_reduce_fusion
  65.9 0.2 reshape.221.codes_ref
  66.1 5.8 %gram_counts.1 = f32[64,8192]{1,0:T(8,128)} custom-call(s32[64]{0:T(128)S(1)} %get-tuple-element.19.book_ref, s32[64]{0:T(128)S(1)} %get-tuple-element.18.start_ref, s32[1,512]{1,0:T(1,128)S(1)} %compare_select_fusion.6.row_ref, s32[8,512]{1,0:T(8,128)S(1)} %reshape.221.codes_ref), custom_call_target="tpu_custom_call" | custom-call | tf_op jit(solution)/shard_map/gram_counts/pallas_call | solution.py:190
  72.0 0.7 compare_select_fusion.5.row_ref
  72.7 1.1 and_select_fusion.3.column_ref
  73.8 12.8 %weights.1.left_ref = bf16[1024,3072]{1,0:T(8,128)(2,1)} custom-call(s32[4,1,2048]{2,1,0:T(1,128)} %compare_select_fusion.5.row_ref, s32[4,2,2048]{2,1,0:T(2,128)} %and_select_fusion.3.column_ref, s32[4,1,3072]{2,1,0:T(1,128)} %reshape.219.vector_ref), custom_call_target="tpu_custom_call" | custom-call | tf_op jit(solution)/shard_map/weights/pallas_call | solution.py:81
  86.6 0.1 convert_reduce_fusion.1
  86.7 0.1 convert_subtract_fusion
  86.9 5.4 %all-gather.2.cloned.1.call-done.right_ref = bf16[3072,1024]{1,0:T(8,128)(2,1)} async-done(((bf16[96,1024]{1,0:T(8,128)(2,1)}), bf16[3072,1024]{1,0:T(8,128)(2,1)}) %all-gather.2.cloned.1.call-update) | async-done | bytes 6291472 | tf_op jit(solution)/shard_map/all_gather | solution.py:243
  92.3 9.7 %product.1 = bf16[1024,1024]{1,0:T(8,128)(2,1)S(1)} custom-call(bf16[1024,3072]{1,0:T(8,128)(2,1)} %weights.1.left_ref, bf16[3072,1024]{1,0:T(8,128)(2,1)} %all-gather.2.cloned.1.call-done.right_ref), custom_call_target="tpu_custom_call" | custom-call | tf_op jit(solution)/shard_map/product/pallas_call | solution.py:136
  102.0 33.2 %all_to_all.16 = bf16[16,64,1024]{2,1,0:T(8,128)(2,1)S(1)} all-to-all(bf16[16,64,1024]{2,1,0:T(8,128)(2,1)S(1)} %bitcast.64), channel_id=1, replica_groups=mesh['z'=16,'y'=4,'x'=4,'core'=2] {'y','x'}, dimensions={0} | all-to-all | bytes 4194304 | tf_op jit(solution)/shard_map/all_to_all | solution.py:265
  135.2 0.4 convert_reduce_fusion
  135.6 0.8 add_bitcast_fusion
  (31 shorter events, 0.7 us)
Async XLA Ops:
  7.2 42.9 %copy-start = (s32[256,64]{0,1:T(8,128)S(1)}, s32[256,64]{0,1:T(8,128)}, u32[]{:S(2)}) copy-start(s32[256,64]{0,1:T(8,128)} %param.7) | copy-start | bytes 196612
  7.2 85.1 %all-gather.2.cloned.1.call-start = ((), (), s32[]{:S(2)}) async-start(), calls=%async_computation.3 | async-start | bytes 6488064 | tf_op jit(solution)/shard_map/all_gather | solution.py:243
  44.9 10.2 %all-to-all-start.1 = ((s16[8,64,256]{2,1,0:T(8,128)(2,1)}), s16[8,64,256]{2,1,0:T(8,128)(2,1)S(1)}, u32[]{:S(2)}, u32[]{:S(2)}) async-start(s16[8,64,256]{2,1,0:T(8,128)(2,1)} %broadcast_in_dim.71), calls=%async_computation.1 | async-start | bytes 524288 | tf_op jit(solution)/shard_map/all_to_all | solution.py:28
  73.8 12.9 %copy-start.1 = (bf16[1,64,1024]{2,1,0:T(8,128)(2,1)S(1)}, bf16[1,64,1024]{2,1,0:T(8,128)(2,1)}, u32[]{:S(2)}) copy-start(bf16[1,64,1024]{2,1,0:T(8,128)(2,1)} %param.6) | copy-start | bytes 393220
Sparse Core Ops, SparseCore 0:
  10.1 82.1 all-gather.1
